TPU v7x, 512 devices: a whole 4x8x8 slice. The times are simulated.
512 devices in a mesh: pipe: 8 (over z), expert: 32 (over y, x), dp: 2 (over core).
Axes of the slice: x: 4, y: 8, z: 8, core: 2. Of those that a mesh axis runs over, the one named last changes fastest.
Arguments:
- saved: bfloat16 [1, 8, 8192, 2560], P(None, 'pipe', ('expert', 'dp')), may hold values from -6 to 6
- cotangent: bfloat16 [8192, 2560], P(('expert', 'dp'), 'pipe'), may hold values from -1.1953125 to 1.1953125
- routes: int32 [1, 8, 8192, 1], P(None, 'pipe', ('expert', 'dp')), may hold values from 0 to 7; in each aligned block of 16 rows (0 to 15, 16 to 31, ..., all dimensions but the last counted through in order) at most 2 rows name the same one
- w_gate: bfloat16 [1, 8, 8192, 2560], P(None, 'pipe', 'expert', 'dp'), may hold values from -0.125 to 0.125
- w_up: bfloat16 [1, 8, 8192, 2560], P(None, 'pipe', 'expert', 'dp'), may hold values from -0.125 to 0.125
- w_down: bfloat16 [1, 8, 8192, 2560], P(None, 'pipe', 'expert', 'dp'), may hold values from -0.0625 to 0.0625
Outputs:
- grad_gate: bfloat16 [1, 8, 8192, 2560], P(None, 'pipe', 'expert', 'dp')
- grad_up: bfloat16 [1, 8, 8192, 2560], P(None, 'pipe', 'expert', 'dp')
Inputs may be any that keep to these rules, and one draw needn't show every extreme that they name: In each aligned block of 16 rows of routes (one micro-batch of one device, rows taken in order over all leading dimensions) no expert is named more than 2 times.
All inputs are finite; a program needn't handle non-finite values.
Results may differ from a plain program's by a relative error of at most 0.017.
Values may be sent and summed in bfloat16 or wider, within the bound.
No kernel may reach another device: no remote copies, remote signals or barrier semaphores. Data moves between devices by JAX's collectives and lax.ppermute only.
A program may use at most 64 MiB of HBM per device.

v0:
```python
import jax
import jax.numpy as jnp
from jax import lax
from jax.sharding import PartitionSpec as P

GROUP = 4
MICRO = 8


epsilon = 1e-06


def shifted(block, axis, distance):
    devices = range(lax.axis_size(axis))
    route = [(i - distance, i) for i in devices if i - distance in devices]
    return lax.ppermute(block, axis, route)


def slot_tables(route_ids, experts, capacity):
    onehot = (route_ids[..., None] == jnp.arange(experts, dtype=jnp.int32)).astype(jnp.int32)
    ranking = jnp.sum((jnp.cumsum(onehot, axis=2) - onehot) * onehot, axis=3)
    slot_ids = route_ids * capacity + ranking
    positions = jnp.arange(experts * capacity, dtype=jnp.int32)[:, None]
    placing = (slot_ids[..., None, :] == positions).astype(jnp.bfloat16)
    return (placing, slot_ids)


def shards(saved, cotangent, routes, w_gate, w_up, w_down):
    sections = lax.axis_size("pipe")
    width_all = lax.axis_size("expert")
    section_index = lax.axis_index("pipe")
    stretches = saved.shape[0]
    tok_dev = saved.shape[2]
    tok_mb = tok_dev // MICRO
    experts = width_all // GROUP
    capacity = max(2, tok_mb // experts)
    period = sections + MICRO - 1
    slot_count = width_all * capacity
    head_grad = lax.all_gather(cotangent, "pipe", axis=1, tiled=True)
    feature_count = head_grad.shape[1]
    slabs = (
        lax.all_gather(w_gate, "dp", axis=3, tiled=True),
        lax.all_gather(w_up, "dp", axis=3, tiled=True),
        lax.all_gather(w_down, "dp", axis=3, tiled=True),
    )
    gate_w = slabs[0][:, 0]
    up_w = slabs[1][:, 0]
    down_w = slabs[2][:, 0]
    hidden = gate_w.shape[1]
    inputs_f = saved[:, 0].astype(jnp.float32).reshape(stretches, MICRO, tok_mb, feature_count)
    norm_scale = lax.rsqrt(jnp.mean(inputs_f * inputs_f, axis=3, keepdims=True) + epsilon)
    unit_f = inputs_f * norm_scale
    unit_b = unit_f.astype(jnp.bfloat16)
    route_ids = routes[:, 0, :, 0].reshape(stretches, MICRO, tok_mb)
    placing, slot_ids = slot_tables(route_ids, experts, capacity)
    unit_slots = jnp.einsum("vmst,vmtd->vmsd", placing, unit_b, preferred_element_type=jnp.float32)
    unit_slots = unit_slots.astype(jnp.bfloat16).reshape(
        stretches, MICRO, experts, capacity, feature_count
    )
    unit_send = jnp.repeat(unit_slots, GROUP, axis=2)
    unit_recv = lax.all_to_all(unit_send, "expert", split_axis=2, concat_axis=2, tiled=True)
    unit_rows = unit_recv.reshape(stretches, MICRO, slot_count, feature_count)
    top_section = section_index == sections - 1

    def tick_step(tick_index, loop_state):
        carried, gate_store, up_store = loop_state
        stretch_index = 0
        micro_raw = tick_index - (sections - 1 - section_index)
        active = (micro_raw >= 0) & (micro_raw < MICRO)
        micro_index = jnp.clip(micro_raw, 0, MICRO - 1)
        seed_rows = lax.dynamic_slice_in_dim(head_grad, micro_index * tok_mb, tok_mb, 0)
        grad_in = jnp.where(top_section, seed_rows, carried)
        grad_in = jnp.where(active, grad_in, jnp.zeros_like(grad_in))
        place_now = placing[stretch_index, micro_index].reshape(experts, capacity, tok_mb)
        slot_grads = jnp.einsum(
            "ect,td->ecd", place_now, grad_in, preferred_element_type=jnp.float32
        )
        sending = jnp.repeat(slot_grads.astype(jnp.bfloat16), GROUP, axis=0)
        grad_rows = lax.all_to_all(
            sending, "expert", split_axis=0, concat_axis=0, tiled=True
        ).reshape(slot_count, feature_count)
        gate_slab = gate_w[stretch_index]
        up_slab = up_w[stretch_index]
        down_slab = down_w[stretch_index]
        unit_now = unit_rows[stretch_index, micro_index]
        gate = jnp.einsum("rd,hd->rh", unit_now, gate_slab, preferred_element_type=jnp.float32)
        up = jnp.einsum("rd,hd->rh", unit_now, up_slab, preferred_element_type=jnp.float32)
        hidden_grad = jnp.einsum(
            "rd,hd->rh", grad_rows, down_slab, preferred_element_type=jnp.float32
        )
        sigmoid_gate = jax.nn.sigmoid(gate)
        gate_grad = (hidden_grad * up * sigmoid_gate * (1.0 + gate * (1.0 - sigmoid_gate))).astype(
            jnp.bfloat16
        )
        up_grad = (hidden_grad * gate * sigmoid_gate).astype(jnp.bfloat16)
        partial_value = jnp.dot(gate_grad, gate_slab, preferred_element_type=jnp.float32)
        partial_value = (
            partial_value + jnp.dot(up_grad, up_slab, preferred_element_type=jnp.float32)
        ).astype(jnp.bfloat16)
        returned = lax.all_to_all(
            partial_value.reshape(width_all, capacity, feature_count),
            "expert",
            split_axis=0,
            concat_axis=0,
            tiled=True,
        )
        summed = (
            returned.reshape(experts, GROUP, capacity, feature_count)
            .astype(jnp.float32)
            .sum(axis=1)
        )
        unit_grad = jnp.take(
            summed.reshape(experts * capacity, feature_count),
            slot_ids[stretch_index, micro_index],
            axis=0,
        )
        unit_here = unit_f[stretch_index, micro_index]
        scale_rows = norm_scale[stretch_index, micro_index]
        norm_grad = scale_rows * (
            unit_grad - unit_here * jnp.mean(unit_grad * unit_here, axis=1, keepdims=True)
        )
        grad_out = (grad_in.astype(jnp.float32) + norm_grad).astype(jnp.bfloat16)
        carried = shifted(grad_out, "pipe", -1)
        gate_store = jnp.where(
            active, gate_store.at[stretch_index, micro_index].set(gate_grad), gate_store
        )
        up_store = jnp.where(active, up_store.at[stretch_index, micro_index].set(up_grad), up_store)
        return (carried, gate_store, up_store)

    start_state = (
        jnp.zeros((tok_mb, feature_count), jnp.bfloat16),
        jnp.zeros((stretches, MICRO, slot_count, hidden), jnp.bfloat16),
        jnp.zeros((stretches, MICRO, slot_count, hidden), jnp.bfloat16),
    )
    final_state = lax.fori_loop(0, period, tick_step, start_state)
    flat_units = unit_rows.reshape(stretches, MICRO * slot_count, feature_count)
    part_gate = jnp.einsum(
        "vrh,vrd->vhd",
        final_state[1].reshape(stretches, MICRO * slot_count, hidden),
        flat_units,
        preferred_element_type=jnp.float32,
    )
    part_up = jnp.einsum(
        "vrh,vrd->vhd",
        final_state[2].reshape(stretches, MICRO * slot_count, hidden),
        flat_units,
        preferred_element_type=jnp.float32,
    )
    totals = (
        lax.psum_scatter(
            part_gate.astype(jnp.bfloat16), "dp", scatter_dimension=2, tiled=True
        ).astype(jnp.float32),
        lax.psum_scatter(
            part_up.astype(jnp.bfloat16), "dp", scatter_dimension=2, tiled=True
        ).astype(jnp.float32),
    )
    grad_gate = totals[0].astype(jnp.bfloat16)[:, None]
    grad_up = totals[1].astype(jnp.bfloat16)[:, None]
    return (grad_gate, grad_up)


def solution(mesh):
    in_specs = (
        P(None, "pipe", ("expert", "dp"), None),
        P(("expert", "dp"), "pipe"),
        P(None, "pipe", ("expert", "dp"), None),
        P(None, "pipe", "expert", "dp"),
        P(None, "pipe", "expert", "dp"),
        P(None, "pipe", "expert", "dp"),
    )
    out_specs = (P(None, "pipe", "expert", "dp"), P(None, "pipe", "expert", "dp"))
    return jax.shard_map(shards, mesh=mesh, in_specs=in_specs, out_specs=out_specs, check_vma=False)
```

profile of v0, /device:TPU:1, one launch (start us, length us, event | category | flops | bytes accessed | tf_op | source)
XLA Modules:
  0.0 954.3 jit_solution(4917801500919075737)
XLA Ops:
  12.8 4.0 broadcast_in_dim.60
  16.8 10.5 %all-to-all-start.2 = ((bf16[1,8,32,2,2560]{4,3,1,0,2:T(2,128)(2,1)}), bf16[1,8,32,2,2560]{4,3,1,0,2:T(2,128)(2,1)S(1)}, u32[]{:S(2)}, u32[]{:S(2)}) async-start(bf16[1,8,32,2,2560]{4,3,1,0,2:T(2,128)(2,1)} %bitcast.139), calls=%async_computation.2 | async-start | bytes 5242880 | tf_op jit(solution)/shard_map/all_to_all | solution.py:61
  29.6 28.2 %all_gather.12 = bf16[128,2560]{0,1:T(8,128)(2,1)S(1)} all-gather(bf16[128,320]{0,1:T(8,128)(2,1)S(1)} %copy-done.6), channel_id=1, replica_groups=mesh['pipe'=8,'expert'=32,'dp'=2] {'pipe'}, dimensions={1}, use_global_device_ids=true | all-gather | bytes 737280 | tf_op jit(solution)/shard_map/all_gather | solution.py:39
  61.6 25.4 %all-to-all-done.2 = bf16[1,8,32,2,2560]{4,3,1,0,2:T(2,128)(2,1)S(1)} async-done(((bf16[1,8,32,2,2560]{4,3,1,0,2:T(2,128)(2,1)}), bf16[1,8,32,2,2560]{4,3,1,0,2:T(2,128)(2,1)S(1)}, u32[]{:S(2)}, u32[]{:S(2)}) %all-to-all-start.2) | async-done | bytes 2621472 | tf_op jit(solution)/shard_map/all_to_all | solution.py:61
  93.1 6.7 reshape.422
  101.3 753.9 %while.21 = (s32[]{:T(128)}, bf16[16,2560]{1,0:T(8,128)(2,1)S(1)}, bf16[1,8,64,256]{3,2,1,0:T(8,128)(2,1)}, bf16[1,8,64,256]{3,2,1,0:T(8,128)(2,1)}, s32[]{:T(12...) while((s32[]{:T(128)}, bf16[16,2560]{1,0:T(8,128)(2,1)S(1)}, ...), condition=%wide.region_7.8_spmd, body=%wide.region_3.7_spmd.sunk | while | flops 422298752 | bytes 31975776 | solution.py:135
  103.4 6.9 all-to-all-start
  111.0 10.5 %all-to-all-done = bf16[32,2,2560]{2,1,0:T(2,128)(2,1)S(1)} async-done(((bf16[32,2,2560]{2,1,0:T(2,128)(2,1)}), bf16[32,2,2560]{2,1,0:T(2,128)(2,1)S(1)}, u32[]{:S(2)}, u32[]{:S(2)}) %all-to-all-start) | async-done | bytes 327712 | tf_op jit(solution)/shard_map/while/body/eval_jaxpr/all_to_all | solution.py:79
  129.3 5.9 all-to-all-start.1
  135.3 10.7 %all-to-all-done.1 = bf16[32,2,2560]{2,1,0:T(2,128)(2,1)S(1)} async-done(((bf16[32,2,2560]{2,1,0:T(2,128)(2,1)}), bf16[32,2,2560]{2,1,0:T(2,128)(2,1)S(1)}, u32[]{:S(2)}, u32[]{:S(2)}) %all-to-all-start.1) | async-done | bytes 327712 | tf_op jit(solution)/shard_map/while/body/eval_jaxpr/all_to_all | solution.py:100
  150.6 4.4 collective-permute-done
  157.1 6.2 all-to-all-start
  164.0 10.1 %all-to-all-done = bf16[32,2,2560]{2,1,0:T(2,128)(2,1)S(1)} async-done(((bf16[32,2,2560]{2,1,0:T(2,128)(2,1)}), bf16[32,2,2560]{2,1,0:T(2,128)(2,1)S(1)}, u32[]{:S(2)}, u32[]{:S(2)}) %all-to-all-start) | async-done | bytes 327712 | tf_op jit(solution)/shard_map/while/body/eval_jaxpr/all_to_all | solution.py:79
  181.9 4.3 all-to-all-start.1
  186.3 10.7 %all-to-all-done.1 = bf16[32,2,2560]{2,1,0:T(2,128)(2,1)S(1)} async-done(((bf16[32,2,2560]{2,1,0:T(2,128)(2,1)}), bf16[32,2,2560]{2,1,0:T(2,128)(2,1)S(1)}, u32[]{:S(2)}, u32[]{:S(2)}) %all-to-all-start.1) | async-done | bytes 327712 | tf_op jit(solution)/shard_map/while/body/eval_jaxpr/all_to_all | solution.py:100
  201.5 4.6 collective-permute-done
  208.2 4.2 all-to-all-start
  213.1 10.0 %all-to-all-done = bf16[32,2,2560]{2,1,0:T(2,128)(2,1)S(1)} async-done(((bf16[32,2,2560]{2,1,0:T(2,128)(2,1)}), bf16[32,2,2560]{2,1,0:T(2,128)(2,1)S(1)}, u32[]{:S(2)}, u32[]{:S(2)}) %all-to-all-start) | async-done | bytes 327712 | tf_op jit(solution)/shard_map/while/body/eval_jaxpr/all_to_all | solution.py:79
  230.8 4.0 all-to-all-start.1
  234.9 10.6 %all-to-all-done.1 = bf16[32,2,2560]{2,1,0:T(2,128)(2,1)S(1)} async-done(((bf16[32,2,2560]{2,1,0:T(2,128)(2,1)}), bf16[32,2,2560]{2,1,0:T(2,128)(2,1)S(1)}, u32[]{:S(2)}, u32[]{:S(2)}) %all-to-all-start.1) | async-done | bytes 327712 | tf_op jit(solution)/shard_map/while/body/eval_jaxpr/all_to_all | solution.py:100
  250.1 4.5 collective-permute-done
  261.4 10.0 %all-to-all-done = bf16[32,2,2560]{2,1,0:T(2,128)(2,1)S(1)} async-done(((bf16[32,2,2560]{2,1,0:T(2,128)(2,1)}), bf16[32,2,2560]{2,1,0:T(2,128)(2,1)S(1)}, u32[]{:S(2)}, u32[]{:S(2)}) %all-to-all-start) | async-done | bytes 327712 | tf_op jit(solution)/shard_map/while/body/eval_jaxpr/all_to_all | solution.py:79
  283.1 10.6 %all-to-all-done.1 = bf16[32,2,2560]{2,1,0:T(2,128)(2,1)S(1)} async-done(((bf16[32,2,2560]{2,1,0:T(2,128)(2,1)}), bf16[32,2,2560]{2,1,0:T(2,128)(2,1)S(1)}, u32[]{:S(2)}, u32[]{:S(2)}) %all-to-all-start.1) | async-done | bytes 327712 | tf_op jit(solution)/shard_map/while/body/eval_jaxpr/all_to_all | solution.py:100
  298.3 6.0 collective-permute-done
  306.5 3.9 all-to-all-start
  311.2 10.0 %all-to-all-done = bf16[32,2,2560]{2,1,0:T(2,128)(2,1)S(1)} async-done(((bf16[32,2,2560]{2,1,0:T(2,128)(2,1)}), bf16[32,2,2560]{2,1,0:T(2,128)(2,1)S(1)}, u32[]{:S(2)}, u32[]{:S(2)}) %all-to-all-start) | async-done | bytes 327712 | tf_op jit(solution)/shard_map/while/body/eval_jaxpr/all_to_all | solution.py:79
  332.9 10.6 %all-to-all-done.1 = bf16[32,2,2560]{2,1,0:T(2,128)(2,1)S(1)} async-done(((bf16[32,2,2560]{2,1,0:T(2,128)(2,1)}), bf16[32,2,2560]{2,1,0:T(2,128)(2,1)S(1)}, u32[]{:S(2)}, u32[]{:S(2)}) %all-to-all-start.1) | async-done | bytes 327712 | tf_op jit(solution)/shard_map/while/body/eval_jaxpr/all_to_all | solution.py:100
  348.1 5.4 collective-permute-done
  355.6 3.9 all-to-all-start
  360.3 10.0 %all-to-all-done = bf16[32,2,2560]{2,1,0:T(2,128)(2,1)S(1)} async-done(((bf16[32,2,2560]{2,1,0:T(2,128)(2,1)}), bf16[32,2,2560]{2,1,0:T(2,128)(2,1)S(1)}, u32[]{:S(2)}, u32[]{:S(2)}) %all-to-all-start) | async-done | bytes 327712 | tf_op jit(solution)/shard_map/while/body/eval_jaxpr/all_to_all | solution.py:79
  382.0 11.0 %all-to-all-done.1 = bf16[32,2,2560]{2,1,0:T(2,128)(2,1)S(1)} async-done(((bf16[32,2,2560]{2,1,0:T(2,128)(2,1)}), bf16[32,2,2560]{2,1,0:T(2,128)(2,1)S(1)}, u32[]{:S(2)}, u32[]{:S(2)}) %all-to-all-start.1) | async-done | bytes 327712 | tf_op jit(solution)/shard_map/while/body/eval_jaxpr/all_to_all | solution.py:100
  397.5 5.0 collective-permute-done
  409.2 10.5 %all-to-all-done = bf16[32,2,2560]{2,1,0:T(2,128)(2,1)S(1)} async-done(((bf16[32,2,2560]{2,1,0:T(2,128)(2,1)}), bf16[32,2,2560]{2,1,0:T(2,128)(2,1)S(1)}, u32[]{:S(2)}, u32[]{:S(2)}) %all-to-all-start) | async-done | bytes 327712 | tf_op jit(solution)/shard_map/while/body/eval_jaxpr/all_to_all | solution.py:79
  431.3 12.4 %all-to-all-done.1 = bf16[32,2,2560]{2,1,0:T(2,128)(2,1)S(1)} async-done(((bf16[32,2,2560]{2,1,0:T(2,128)(2,1)}), bf16[32,2,2560]{2,1,0:T(2,128)(2,1)S(1)}, u32[]{:S(2)}, u32[]{:S(2)}) %all-to-all-start.1) | async-done | bytes 327712 | tf_op jit(solution)/shard_map/while/body/eval_jaxpr/all_to_all | solution.py:100
  448.3 5.6 collective-permute-done
  460.5 10.3 %all-to-all-done = bf16[32,2,2560]{2,1,0:T(2,128)(2,1)S(1)} async-done(((bf16[32,2,2560]{2,1,0:T(2,128)(2,1)}), bf16[32,2,2560]{2,1,0:T(2,128)(2,1)S(1)}, u32[]{:S(2)}, u32[]{:S(2)}) %all-to-all-start) | async-done | bytes 327712 | tf_op jit(solution)/shard_map/while/body/eval_jaxpr/all_to_all | solution.py:79
  482.5 11.1 %all-to-all-done.1 = bf16[32,2,2560]{2,1,0:T(2,128)(2,1)S(1)} async-done(((bf16[32,2,2560]{2,1,0:T(2,128)(2,1)}), bf16[32,2,2560]{2,1,0:T(2,128)(2,1)S(1)}, u32[]{:S(2)}, u32[]{:S(2)}) %all-to-all-start.1) | async-done | bytes 327712 | tf_op jit(solution)/shard_map/while/body/eval_jaxpr/all_to_all | solution.py:100
  498.1 5.3 collective-permute-done
  505.6 5.8 all-to-all-start
  512.0 12.4 %all-to-all-done = bf16[32,2,2560]{2,1,0:T(2,128)(2,1)S(1)} async-done(((bf16[32,2,2560]{2,1,0:T(2,128)(2,1)}), bf16[32,2,2560]{2,1,0:T(2,128)(2,1)S(1)}, u32[]{:S(2)}, u32[]{:S(2)}) %all-to-all-start) | async-done | bytes 327712 | tf_op jit(solution)/shard_map/while/body/eval_jaxpr/all_to_all | solution.py:79
  536.1 11.1 %all-to-all-done.1 = bf16[32,2,2560]{2,1,0:T(2,128)(2,1)S(1)} async-done(((bf16[32,2,2560]{2,1,0:T(2,128)(2,1)}), bf16[32,2,2560]{2,1,0:T(2,128)(2,1)S(1)}, u32[]{:S(2)}, u32[]{:S(2)}) %all-to-all-start.1) | async-done | bytes 327712 | tf_op jit(solution)/shard_map/while/body/eval_jaxpr/all_to_all | solution.py:100
  551.8 5.4 collective-permute-done
  563.9 11.3 %all-to-all-done = bf16[32,2,2560]{2,1,0:T(2,128)(2,1)S(1)} async-done(((bf16[32,2,2560]{2,1,0:T(2,128)(2,1)}), bf16[32,2,2560]{2,1,0:T(2,128)(2,1)S(1)}, u32[]{:S(2)}, u32[]{:S(2)}) %all-to-all-start) | async-done | bytes 327712 | tf_op jit(solution)/shard_map/while/body/eval_jaxpr/all_to_all | solution.py:79
  582.9 5.1 all-to-all-start.1
  588.1 10.6 %all-to-all-done.1 = bf16[32,2,2560]{2,1,0:T(2,128)(2,1)S(1)} async-done(((bf16[32,2,2560]{2,1,0:T(2,128)(2,1)}), bf16[32,2,2560]{2,1,0:T(2,128)(2,1)S(1)}, u32[]{:S(2)}, u32[]{:S(2)}) %all-to-all-start.1) | async-done | bytes 327712 | tf_op jit(solution)/shard_map/while/body/eval_jaxpr/all_to_all | solution.py:100
  603.4 5.1 collective-permute-done
  615.2 10.0 %all-to-all-done = bf16[32,2,2560]{2,1,0:T(2,128)(2,1)S(1)} async-done(((bf16[32,2,2560]{2,1,0:T(2,128)(2,1)}), bf16[32,2,2560]{2,1,0:T(2,128)(2,1)S(1)}, u32[]{:S(2)}, u32[]{:S(2)}) %all-to-all-start) | async-done | bytes 327712 | tf_op jit(solution)/shard_map/while/body/eval_jaxpr/all_to_all | solution.py:79
  632.9 4.0 all-to-all-start.1
  637.0 10.6 %all-to-all-done.1 = bf16[32,2,2560]{2,1,0:T(2,128)(2,1)S(1)} async-done(((bf16[32,2,2560]{2,1,0:T(2,128)(2,1)}), bf16[32,2,2560]{2,1,0:T(2,128)(2,1)S(1)}, u32[]{:S(2)}, u32[]{:S(2)}) %all-to-all-start.1) | async-done | bytes 327712 | tf_op jit(solution)/shard_map/while/body/eval_jaxpr/all_to_all | solution.py:100
  652.2 5.5 collective-permute-done
  664.5 10.0 %all-to-all-done = bf16[32,2,2560]{2,1,0:T(2,128)(2,1)S(1)} async-done(((bf16[32,2,2560]{2,1,0:T(2,128)(2,1)}), bf16[32,2,2560]{2,1,0:T(2,128)(2,1)S(1)}, u32[]{:S(2)}, u32[]{:S(2)}) %all-to-all-start) | async-done | bytes 327712 | tf_op jit(solution)/shard_map/while/body/eval_jaxpr/all_to_all | solution.py:79
  686.3 10.6 %all-to-all-done.1 = bf16[32,2,2560]{2,1,0:T(2,128)(2,1)S(1)} async-done(((bf16[32,2,2560]{2,1,0:T(2,128)(2,1)}), bf16[32,2,2560]{2,1,0:T(2,128)(2,1)S(1)}, u32[]{:S(2)}, u32[]{:S(2)}) %all-to-all-start.1) | async-done | bytes 327712 | tf_op jit(solution)/shard_map/while/body/eval_jaxpr/all_to_all | solution.py:100
  701.5 5.2 collective-permute-done
  713.4 10.0 %all-to-all-done = bf16[32,2,2560]{2,1,0:T(2,128)(2,1)S(1)} async-done(((bf16[32,2,2560]{2,1,0:T(2,128)(2,1)}), bf16[32,2,2560]{2,1,0:T(2,128)(2,1)S(1)}, u32[]{:S(2)}, u32[]{:S(2)}) %all-to-all-start) | async-done | bytes 327712 | tf_op jit(solution)/shard_map/while/body/eval_jaxpr/all_to_all | solution.py:79
  735.1 10.6 %all-to-all-done.1 = bf16[32,2,2560]{2,1,0:T(2,128)(2,1)S(1)} async-done(((bf16[32,2,2560]{2,1,0:T(2,128)(2,1)}), bf16[32,2,2560]{2,1,0:T(2,128)(2,1)S(1)}, u32[]{:S(2)}, u32[]{:S(2)}) %all-to-all-start.1) | async-done | bytes 327712 | tf_op jit(solution)/shard_map/while/body/eval_jaxpr/all_to_all | solution.py:100
  750.3 5.2 collective-permute-done
  762.3 10.0 %all-to-all-done = bf16[32,2,2560]{2,1,0:T(2,128)(2,1)S(1)} async-done(((bf16[32,2,2560]{2,1,0:T(2,128)(2,1)}), bf16[32,2,2560]{2,1,0:T(2,128)(2,1)S(1)}, u32[]{:S(2)}, u32[]{:S(2)}) %all-to-all-start) | async-done | bytes 327712 | tf_op jit(solution)/shard_map/while/body/eval_jaxpr/all_to_all | solution.py:79
  784.1 10.6 %all-to-all-done.1 = bf16[32,2,2560]{2,1,0:T(2,128)(2,1)S(1)} async-done(((bf16[32,2,2560]{2,1,0:T(2,128)(2,1)}), bf16[32,2,2560]{2,1,0:T(2,128)(2,1)S(1)}, u32[]{:S(2)}, u32[]{:S(2)}) %all-to-all-start.1) | async-done | bytes 327712 | tf_op jit(solution)/shard_map/while/body/eval_jaxpr/all_to_all | solution.py:100
  799.3 5.0 collective-permute-done
  811.0 10.3 %all-to-all-done = bf16[32,2,2560]{2,1,0:T(2,128)(2,1)S(1)} async-done(((bf16[32,2,2560]{2,1,0:T(2,128)(2,1)}), bf16[32,2,2560]{2,1,0:T(2,128)(2,1)S(1)}, u32[]{:S(2)}, u32[]{:S(2)}) %all-to-all-start) | async-done | bytes 327712 | tf_op jit(solution)/shard_map/while/body/eval_jaxpr/all_to_all | solution.py:79
  833.0 11.8 %all-to-all-done.1 = bf16[32,2,2560]{2,1,0:T(2,128)(2,1)S(1)} async-done(((bf16[32,2,2560]{2,1,0:T(2,128)(2,1)}), bf16[32,2,2560]{2,1,0:T(2,128)(2,1)S(1)}, u32[]{:S(2)}, u32[]{:S(2)}) %all-to-all-start.1) | async-done | bytes 327712 | tf_op jit(solution)/shard_map/while/body/eval_jaxpr/all_to_all | solution.py:100
  849.4 5.8 collective-permute-done
  862.0 64.3 %reduce-scatter.5.cloned.1.call-done = bf16[1,256,1280]{2,1,0:T(8,128)(2,1)} async-done(((bf16[1,256,2560]{2,1,0:T(8,128)(2,1)}), bf16[1,256,1280]{2,1,0:T(8,128)(2,1)}) %reduce-scatter.5.cloned.1.call-update) | async-done | bytes 655376 | tf_op jit(solution)/shard_map/reduce_scatter | solution.py:153
  926.3 21.4 %reduce-scatter.3.cloned.1.call-done = bf16[1,256,1280]{2,1,0:T(8,128)(2,1)} async-done(((bf16[1,256,2560]{2,1,0:T(8,128)(2,1)}), bf16[1,256,1280]{2,1,0:T(8,128)(2,1)}) %reduce-scatter.3.cloned.1.call-update) | async-done | bytes 655376 | tf_op jit(solution)/shard_map/reduce_scatter | solution.py:150
  (507 shorter events, 326.2 us)
Async XLA Ops:
  16.8 70.2 %all-to-all-start.2 = ((bf16[1,8,32,2,2560]{4,3,1,0,2:T(2,128)(2,1)}), bf16[1,8,32,2,2560]{4,3,1,0,2:T(2,128)(2,1)S(1)}, u32[]{:S(2)}, u32[]{:S(2)}) async-start(bf16[1,8,32,2,2560]{4,3,1,0,2:T(2,128)(2,1)} %bitcast.139), calls=%async_computation.2 | async-start | bytes 5242880 | tf_op jit(solution)/shard_map/all_to_all | solution.py:61
  27.3 72.5 %all-gather.4.cloned.1.call-start = ((), (), s32[]{:S(2)}) async-start(), calls=%async_computation.5 | async-start | bytes 1966080 | tf_op jit(solution)/shard_map/all_gather | solution.py:44
  28.0 71.8 %all-gather.6.cloned.1.call-start = ((), (), s32[]{:S(2)}) async-start(), calls=%async_computation.6 | async-start | bytes 1966080 | tf_op jit(solution)/shard_map/all_gather | solution.py:43
  28.8 71.1 %all-gather.8.cloned.1.call-start = ((), (), s32[]{:S(2)}) async-start(), calls=%async_computation.7 | async-start | bytes 1966080 | tf_op jit(solution)/shard_map/all_gather | solution.py:42
  29.5 896.8 %reduce-scatter.5.cloned.1.call-start = ((), (), s32[]{:S(2)}) async-start(), calls=%async_computation.9 | async-start | bytes 1966080 | tf_op jit(solution)/shard_map/reduce_scatter | solution.py:153
  101.3 20.4 %copy-start.2 = (bf16[1,1,256,2560]{3,2,1,0:T(8,128)(2,1)S(1)}, bf16[1,1,256,2560]{3,2,1,0:T(8,128)(2,1)}, u32[]{:S(2)}) copy-start(bf16[1,1,256,2560]{3,2,1,0:T(8,128)(2,1)} %get-tuple-element.656) | copy-start | bytes 3932164 | tf_op jit(solution)/shard_map/while
  103.4 18.2 %all-to-all-start = ((bf16[32,2,2560]{2,1,0:T(2,128)(2,1)}), bf16[32,2,2560]{2,1,0:T(2,128)(2,1)S(1)}, u32[]{:S(2)}, u32[]{:S(2)}) async-start(bf16[32,2,2560]{2,1,0:T(2,128)(2,1)} %bitcast.136), calls=%async_computation | async-start | bytes 655360 | tf_op jit(solution)/shard_map/while/body/eval_jaxpr/all_to_all | solution.py:79
  129.3 16.7 %all-to-all-start.1 = ((bf16[32,2,2560]{2,1,0:T(2,128)(2,1)}), bf16[32,2,2560]{2,1,0:T(2,128)(2,1)S(1)}, u32[]{:S(2)}, u32[]{:S(2)}) async-start(bf16[32,2,2560]{2,1,0:T(2,128)(2,1)} %reshape.458), calls=%async_computation.1 | async-start | bytes 655360 | tf_op jit(solution)/shard_map/while/body/eval_jaxpr/all_to_all | solution.py:100
  149.2 5.7 collective-permute-start
  155.0 19.3 %copy-start.2 = (bf16[1,1,256,2560]{3,2,1,0:T(8,128)(2,1)S(1)}, bf16[1,1,256,2560]{3,2,1,0:T(8,128)(2,1)}, u32[]{:S(2)}) copy-start(bf16[1,1,256,2560]{3,2,1,0:T(8,128)(2,1)} %get-tuple-element.656) | copy-start | bytes 3932164 | tf_op jit(solution)/shard_map/while
  157.1 17.1 %all-to-all-start = ((bf16[32,2,2560]{2,1,0:T(2,128)(2,1)}), bf16[32,2,2560]{2,1,0:T(2,128)(2,1)S(1)}, u32[]{:S(2)}, u32[]{:S(2)}) async-start(bf16[32,2,2560]{2,1,0:T(2,128)(2,1)} %bitcast.136), calls=%async_computation | async-start | bytes 655360 | tf_op jit(solution)/shard_map/while/body/eval_jaxpr/all_to_all | solution.py:79
  181.9 15.0 %all-to-all-start.1 = ((bf16[32,2,2560]{2,1,0:T(2,128)(2,1)}), bf16[32,2,2560]{2,1,0:T(2,128)(2,1)S(1)}, u32[]{:S(2)}, u32[]{:S(2)}) async-start(bf16[32,2,2560]{2,1,0:T(2,128)(2,1)} %reshape.458), calls=%async_computation.1 | async-start | bytes 655360 | tf_op jit(solution)/shard_map/while/body/eval_jaxpr/all_to_all | solution.py:100
  200.2 5.9 collective-permute-start
  206.1 17.2 %copy-start.2 = (bf16[1,1,256,2560]{3,2,1,0:T(8,128)(2,1)S(1)}, bf16[1,1,256,2560]{3,2,1,0:T(8,128)(2,1)}, u32[]{:S(2)}) copy-start(bf16[1,1,256,2560]{3,2,1,0:T(8,128)(2,1)} %get-tuple-element.656) | copy-start | bytes 3932164 | tf_op jit(solution)/shard_map/while
  208.2 14.9 %all-to-all-start = ((bf16[32,2,2560]{2,1,0:T(2,128)(2,1)}), bf16[32,2,2560]{2,1,0:T(2,128)(2,1)S(1)}, u32[]{:S(2)}, u32[]{:S(2)}) async-start(bf16[32,2,2560]{2,1,0:T(2,128)(2,1)} %bitcast.136), calls=%async_computation | async-start | bytes 655360 | tf_op jit(solution)/shard_map/while/body/eval_jaxpr/all_to_all | solution.py:79
  230.8 14.7 %all-to-all-start.1 = ((bf16[32,2,2560]{2,1,0:T(2,128)(2,1)}), bf16[32,2,2560]{2,1,0:T(2,128)(2,1)S(1)}, u32[]{:S(2)}, u32[]{:S(2)}) async-start(bf16[32,2,2560]{2,1,0:T(2,128)(2,1)} %reshape.458), calls=%async_computation.1 | async-start | bytes 655360 | tf_op jit(solution)/shard_map/while/body/eval_jaxpr/all_to_all | solution.py:100
  248.8 5.8 collective-permute-start
  254.6 16.9 %copy-start.2 = (bf16[1,1,256,2560]{3,2,1,0:T(8,128)(2,1)S(1)}, bf16[1,1,256,2560]{3,2,1,0:T(8,128)(2,1)}, u32[]{:S(2)}) copy-start(bf16[1,1,256,2560]{3,2,1,0:T(8,128)(2,1)} %get-tuple-element.656) | copy-start | bytes 3932164 | tf_op jit(solution)/shard_map/while
  256.7 14.7 %all-to-all-start = ((bf16[32,2,2560]{2,1,0:T(2,128)(2,1)}), bf16[32,2,2560]{2,1,0:T(2,128)(2,1)S(1)}, u32[]{:S(2)}, u32[]{:S(2)}) async-start(bf16[32,2,2560]{2,1,0:T(2,128)(2,1)} %bitcast.136), calls=%async_computation | async-start | bytes 655360 | tf_op jit(solution)/shard_map/while/body/eval_jaxpr/all_to_all | solution.py:79
  279.1 14.7 %all-to-all-start.1 = ((bf16[32,2,2560]{2,1,0:T(2,128)(2,1)}), bf16[32,2,2560]{2,1,0:T(2,128)(2,1)S(1)}, u32[]{:S(2)}, u32[]{:S(2)}) async-start(bf16[32,2,2560]{2,1,0:T(2,128)(2,1)} %reshape.458), calls=%async_computation.1 | async-start | bytes 655360 | tf_op jit(solution)/shard_map/while/body/eval_jaxpr/all_to_all | solution.py:100
  297.0 7.3 collective-permute-start
  304.4 16.9 %copy-start.2 = (bf16[1,1,256,2560]{3,2,1,0:T(8,128)(2,1)S(1)}, bf16[1,1,256,2560]{3,2,1,0:T(8,128)(2,1)}, u32[]{:S(2)}) copy-start(bf16[1,1,256,2560]{3,2,1,0:T(8,128)(2,1)} %get-tuple-element.656) | copy-start | bytes 3932164 | tf_op jit(solution)/shard_map/while
  306.5 14.7 %all-to-all-start = ((bf16[32,2,2560]{2,1,0:T(2,128)(2,1)}), bf16[32,2,2560]{2,1,0:T(2,128)(2,1)S(1)}, u32[]{:S(2)}, u32[]{:S(2)}) async-start(bf16[32,2,2560]{2,1,0:T(2,128)(2,1)} %bitcast.136), calls=%async_computation | async-start | bytes 655360 | tf_op jit(solution)/shard_map/while/body/eval_jaxpr/all_to_all | solution.py:79
  328.9 14.7 %all-to-all-start.1 = ((bf16[32,2,2560]{2,1,0:T(2,128)(2,1)}), bf16[32,2,2560]{2,1,0:T(2,128)(2,1)S(1)}, u32[]{:S(2)}, u32[]{:S(2)}) async-start(bf16[32,2,2560]{2,1,0:T(2,128)(2,1)} %reshape.458), calls=%async_computation.1 | async-start | bytes 655360 | tf_op jit(solution)/shard_map/while/body/eval_jaxpr/all_to_all | solution.py:100
  346.8 6.7 collective-permute-start
  353.5 16.9 %copy-start.2 = (bf16[1,1,256,2560]{3,2,1,0:T(8,128)(2,1)S(1)}, bf16[1,1,256,2560]{3,2,1,0:T(8,128)(2,1)}, u32[]{:S(2)}) copy-start(bf16[1,1,256,2560]{3,2,1,0:T(8,128)(2,1)} %get-tuple-element.656) | copy-start | bytes 3932164 | tf_op jit(solution)/shard_map/while
  355.6 14.7 %all-to-all-start = ((bf16[32,2,2560]{2,1,0:T(2,128)(2,1)}), bf16[32,2,2560]{2,1,0:T(2,128)(2,1)S(1)}, u32[]{:S(2)}, u32[]{:S(2)}) async-start(bf16[32,2,2560]{2,1,0:T(2,128)(2,1)} %bitcast.136), calls=%async_computation | async-start | bytes 655360 | tf_op jit(solution)/shard_map/while/body/eval_jaxpr/all_to_all | solution.py:79
  378.0 15.0 %all-to-all-start.1 = ((bf16[32,2,2560]{2,1,0:T(2,128)(2,1)}), bf16[32,2,2560]{2,1,0:T(2,128)(2,1)S(1)}, u32[]{:S(2)}, u32[]{:S(2)}) async-start(bf16[32,2,2560]{2,1,0:T(2,128)(2,1)} %reshape.458), calls=%async_computation.1 | async-start | bytes 655360 | tf_op jit(solution)/shard_map/while/body/eval_jaxpr/all_to_all | solution.py:100
  396.2 6.3 collective-permute-start
  402.5 17.3 %copy-start.2 = (bf16[1,1,256,2560]{3,2,1,0:T(8,128)(2,1)S(1)}, bf16[1,1,256,2560]{3,2,1,0:T(8,128)(2,1)}, u32[]{:S(2)}) copy-start(bf16[1,1,256,2560]{3,2,1,0:T(8,128)(2,1)} %get-tuple-element.656) | copy-start | bytes 3932164 | tf_op jit(solution)/shard_map/while
  404.6 15.1 %all-to-all-start = ((bf16[32,2,2560]{2,1,0:T(2,128)(2,1)}), bf16[32,2,2560]{2,1,0:T(2,128)(2,1)S(1)}, u32[]{:S(2)}, u32[]{:S(2)}) async-start(bf16[32,2,2560]{2,1,0:T(2,128)(2,1)} %bitcast.136), calls=%async_computation | async-start | bytes 655360 | tf_op jit(solution)/shard_map/while/body/eval_jaxpr/all_to_all | solution.py:79
  427.4 16.3 %all-to-all-start.1 = ((bf16[32,2,2560]{2,1,0:T(2,128)(2,1)}), bf16[32,2,2560]{2,1,0:T(2,128)(2,1)S(1)}, u32[]{:S(2)}, u32[]{:S(2)}) async-start(bf16[32,2,2560]{2,1,0:T(2,128)(2,1)} %reshape.458), calls=%async_computation.1 | async-start | bytes 655360 | tf_op jit(solution)/shard_map/while/body/eval_jaxpr/all_to_all | solution.py:100
  447.0 6.9 collective-permute-start
  453.8 17.1 %copy-start.2 = (bf16[1,1,256,2560]{3,2,1,0:T(8,128)(2,1)S(1)}, bf16[1,1,256,2560]{3,2,1,0:T(8,128)(2,1)}, u32[]{:S(2)}) copy-start(bf16[1,1,256,2560]{3,2,1,0:T(8,128)(2,1)} %get-tuple-element.656) | copy-start | bytes 3932164 | tf_op jit(solution)/shard_map/while
  455.9 14.9 %all-to-all-start = ((bf16[32,2,2560]{2,1,0:T(2,128)(2,1)}), bf16[32,2,2560]{2,1,0:T(2,128)(2,1)S(1)}, u32[]{:S(2)}, u32[]{:S(2)}) async-start(bf16[32,2,2560]{2,1,0:T(2,128)(2,1)} %bitcast.136), calls=%async_computation | async-start | bytes 655360 | tf_op jit(solution)/shard_map/while/body/eval_jaxpr/all_to_all | solution.py:79
  478.5 15.1 %all-to-all-start.1 = ((bf16[32,2,2560]{2,1,0:T(2,128)(2,1)}), bf16[32,2,2560]{2,1,0:T(2,128)(2,1)S(1)}, u32[]{:S(2)}, u32[]{:S(2)}) async-start(bf16[32,2,2560]{2,1,0:T(2,128)(2,1)} %reshape.458), calls=%async_computation.1 | async-start | bytes 655360 | tf_op jit(solution)/shard_map/while/body/eval_jaxpr/all_to_all | solution.py:100
  496.8 6.6 collective-permute-start
  503.4 21.2 %copy-start.2 = (bf16[1,1,256,2560]{3,2,1,0:T(8,128)(2,1)S(1)}, bf16[1,1,256,2560]{3,2,1,0:T(8,128)(2,1)}, u32[]{:S(2)}) copy-start(bf16[1,1,256,2560]{3,2,1,0:T(8,128)(2,1)} %get-tuple-element.656) | copy-start | bytes 3932164 | tf_op jit(solution)/shard_map/while
  505.6 18.9 %all-to-all-start = ((bf16[32,2,2560]{2,1,0:T(2,128)(2,1)}), bf16[32,2,2560]{2,1,0:T(2,128)(2,1)S(1)}, u32[]{:S(2)}, u32[]{:S(2)}) async-start(bf16[32,2,2560]{2,1,0:T(2,128)(2,1)} %bitcast.136), calls=%async_computation | async-start | bytes 655360 | tf_op jit(solution)/shard_map/while/body/eval_jaxpr/all_to_all | solution.py:79
  532.2 15.1 %all-to-all-start.1 = ((bf16[32,2,2560]{2,1,0:T(2,128)(2,1)}), bf16[32,2,2560]{2,1,0:T(2,128)(2,1)S(1)}, u32[]{:S(2)}, u32[]{:S(2)}) async-start(bf16[32,2,2560]{2,1,0:T(2,128)(2,1)} %reshape.458), calls=%async_computation.1 | async-start | bytes 655360 | tf_op jit(solution)/shard_map/while/body/eval_jaxpr/all_to_all | solution.py:100
  550.5 6.7 collective-permute-start
  557.2 18.2 %copy-start.2 = (bf16[1,1,256,2560]{3,2,1,0:T(8,128)(2,1)S(1)}, bf16[1,1,256,2560]{3,2,1,0:T(8,128)(2,1)}, u32[]{:S(2)}) copy-start(bf16[1,1,256,2560]{3,2,1,0:T(8,128)(2,1)} %get-tuple-element.656) | copy-start | bytes 3932164 | tf_op jit(solution)/shard_map/while
  559.3 15.9 %all-to-all-start = ((bf16[32,2,2560]{2,1,0:T(2,128)(2,1)}), bf16[32,2,2560]{2,1,0:T(2,128)(2,1)S(1)}, u32[]{:S(2)}, u32[]{:S(2)}) async-start(bf16[32,2,2560]{2,1,0:T(2,128)(2,1)} %bitcast.136), calls=%async_computation | async-start | bytes 655360 | tf_op jit(solution)/shard_map/while/body/eval_jaxpr/all_to_all | solution.py:79
  582.9 15.9 %all-to-all-start.1 = ((bf16[32,2,2560]{2,1,0:T(2,128)(2,1)}), bf16[32,2,2560]{2,1,0:T(2,128)(2,1)S(1)}, u32[]{:S(2)}, u32[]{:S(2)}) async-start(bf16[32,2,2560]{2,1,0:T(2,128)(2,1)} %reshape.458), calls=%async_computation.1 | async-start | bytes 655360 | tf_op jit(solution)/shard_map/while/body/eval_jaxpr/all_to_all | solution.py:100
  602.1 6.4 collective-permute-start
  608.5 16.9 %copy-start.2 = (bf16[1,1,256,2560]{3,2,1,0:T(8,128)(2,1)S(1)}, bf16[1,1,256,2560]{3,2,1,0:T(8,128)(2,1)}, u32[]{:S(2)}) copy-start(bf16[1,1,256,2560]{3,2,1,0:T(8,128)(2,1)} %get-tuple-element.656) | copy-start | bytes 3932164 | tf_op jit(solution)/shard_map/while
  610.6 14.7 %all-to-all-start = ((bf16[32,2,2560]{2,1,0:T(2,128)(2,1)}), bf16[32,2,2560]{2,1,0:T(2,128)(2,1)S(1)}, u32[]{:S(2)}, u32[]{:S(2)}) async-start(bf16[32,2,2560]{2,1,0:T(2,128)(2,1)} %bitcast.136), calls=%async_computation | async-start | bytes 655360 | tf_op jit(solution)/shard_map/while/body/eval_jaxpr/all_to_all | solution.py:79
  632.9 14.7 %all-to-all-start.1 = ((bf16[32,2,2560]{2,1,0:T(2,128)(2,1)}), bf16[32,2,2560]{2,1,0:T(2,128)(2,1)S(1)}, u32[]{:S(2)}, u32[]{:S(2)}) async-start(bf16[32,2,2560]{2,1,0:T(2,128)(2,1)} %reshape.458), calls=%async_computation.1 | async-start | bytes 655360 | tf_op jit(solution)/shard_map/while/body/eval_jaxpr/all_to_all | solution.py:100
  650.9 6.8 collective-permute-start
  657.8 16.9 %copy-start.2 = (bf16[1,1,256,2560]{3,2,1,0:T(8,128)(2,1)S(1)}, bf16[1,1,256,2560]{3,2,1,0:T(8,128)(2,1)}, u32[]{:S(2)}) copy-start(bf16[1,1,256,2560]{3,2,1,0:T(8,128)(2,1)} %get-tuple-element.656) | copy-start | bytes 3932164 | tf_op jit(solution)/shard_map/while
  659.9 14.7 %all-to-all-start = ((bf16[32,2,2560]{2,1,0:T(2,128)(2,1)}), bf16[32,2,2560]{2,1,0:T(2,128)(2,1)S(1)}, u32[]{:S(2)}, u32[]{:S(2)}) async-start(bf16[32,2,2560]{2,1,0:T(2,128)(2,1)} %bitcast.136), calls=%async_computation | async-start | bytes 655360 | tf_op jit(solution)/shard_map/while/body/eval_jaxpr/all_to_all | solution.py:79
  682.2 14.7 %all-to-all-start.1 = ((bf16[32,2,2560]{2,1,0:T(2,128)(2,1)}), bf16[32,2,2560]{2,1,0:T(2,128)(2,1)S(1)}, u32[]{:S(2)}, u32[]{:S(2)}) async-start(bf16[32,2,2560]{2,1,0:T(2,128)(2,1)} %reshape.458), calls=%async_computation.1 | async-start | bytes 655360 | tf_op jit(solution)/shard_map/while/body/eval_jaxpr/all_to_all | solution.py:100
  700.2 6.5 collective-permute-start
  708.7 14.7 %all-to-all-start = ((bf16[32,2,2560]{2,1,0:T(2,128)(2,1)}), bf16[32,2,2560]{2,1,0:T(2,128)(2,1)S(1)}, u32[]{:S(2)}, u32[]{:S(2)}) async-start(bf16[32,2,2560]{2,1,0:T(2,128)(2,1)} %bitcast.136), calls=%async_computation | async-start | bytes 655360 | tf_op jit(solution)/shard_map/while/body/eval_jaxpr/all_to_all | solution.py:79
  731.1 14.7 %all-to-all-start.1 = ((bf16[32,2,2560]{2,1,0:T(2,128)(2,1)}), bf16[32,2,2560]{2,1,0:T(2,128)(2,1)S(1)}, u32[]{:S(2)}, u32[]{:S(2)}) async-start(bf16[32,2,2560]{2,1,0:T(2,128)(2,1)} %reshape.458), calls=%async_computation.1 | async-start | bytes 655360 | tf_op jit(solution)/shard_map/while/body/eval_jaxpr/all_to_all | solution.py:100
  749.0 6.5 collective-permute-start
  757.6 14.7 %all-to-all-start = ((bf16[32,2,2560]{2,1,0:T(2,128)(2,1)}), bf16[32,2,2560]{2,1,0:T(2,128)(2,1)S(1)}, u32[]{:S(2)}, u32[]{:S(2)}) async-start(bf16[32,2,2560]{2,1,0:T(2,128)(2,1)} %bitcast.136), calls=%async_computation | async-start | bytes 655360 | tf_op jit(solution)/shard_map/while/body/eval_jaxpr/all_to_all | solution.py:79
  780.0 14.7 %all-to-all-start.1 = ((bf16[32,2,2560]{2,1,0:T(2,128)(2,1)}), bf16[32,2,2560]{2,1,0:T(2,128)(2,1)S(1)}, u32[]{:S(2)}, u32[]{:S(2)}) async-start(bf16[32,2,2560]{2,1,0:T(2,128)(2,1)} %reshape.458), calls=%async_computation.1 | async-start | bytes 655360 | tf_op jit(solution)/shard_map/while/body/eval_jaxpr/all_to_all | solution.py:100
  798.0 6.3 collective-permute-start
  804.3 17.2 %copy-start.2 = (bf16[1,1,256,2560]{3,2,1,0:T(8,128)(2,1)S(1)}, bf16[1,1,256,2560]{3,2,1,0:T(8,128)(2,1)}, u32[]{:S(2)}) copy-start(bf16[1,1,256,2560]{3,2,1,0:T(8,128)(2,1)} %get-tuple-element.656) | copy-start | bytes 3932164 | tf_op jit(solution)/shard_map/while
  806.4 14.9 %all-to-all-start = ((bf16[32,2,2560]{2,1,0:T(2,128)(2,1)}), bf16[32,2,2560]{2,1,0:T(2,128)(2,1)S(1)}, u32[]{:S(2)}, u32[]{:S(2)}) async-start(bf16[32,2,2560]{2,1,0:T(2,128)(2,1)} %bitcast.136), calls=%async_computation | async-start | bytes 655360 | tf_op jit(solution)/shard_map/while/body/eval_jaxpr/all_to_all | solution.py:79
  829.0 15.8 %all-to-all-start.1 = ((bf16[32,2,2560]{2,1,0:T(2,128)(2,1)}), bf16[32,2,2560]{2,1,0:T(2,128)(2,1)S(1)}, u32[]{:S(2)}, u32[]{:S(2)}) async-start(bf16[32,2,2560]{2,1,0:T(2,128)(2,1)} %reshape.458), calls=%async_computation.1 | async-start | bytes 655360 | tf_op jit(solution)/shard_map/while/body/eval_jaxpr/all_to_all | solution.py:100
  848.1 7.1 collective-permute-start
  859.1 88.6 %reduce-scatter.3.cloned.1.call-start = ((), (), s32[]{:S(2)}) async-start(), calls=%async_computation.8 | async-start | bytes 1966080 | tf_op jit(solution)/shard_map/reduce_scatter | solution.py:150
  (38 other events, 273.3 us)
Sparse Core Ops, SparseCore 0:
  30.2 23.7 all-gather.3
  56.1 18.8 all-gather.5
  77.0 18.8 all-gather.7
  859.2 67.0 reduce-scatter.4
  929.5 18.1 reduce-scatter.2
where the time goes:
time: 959 us; the launch traced here: 954 us
  waiting for transfers between devices  511 us (53%)
  starting transfers between devices  159 us (17%)
  matrix products  123 us (13%)
  local copies, waits for them, and re-layouts  62.3 us (6%)
  other arithmetic  55 us (6%)
  blocking collectives  28.2 us (3%)
  between operations  13.9 us (1%)
    all_to_all x15, waiting for transfers between devices, tick_step(): lax.all_to_all(partial_value.reshape(width_all, capacity, feature_count),...  164 us
    all_to_all x15, waiting for transfers between devices, tick_step(): lax.all_to_all(sending, 'expert', split_axis=0, concat_axis=0, tiled=True)  156 us
    ppermute x15, waiting for transfers between devices, shifted(): return lax.ppermute(block, axis, route)  77.9 us
    all_to_all x15, starting transfers between devices, tick_step(): lax.all_to_all(sending, 'expert', split_axis=0, concat_axis=0, tiled=True)  66.2 us
    reduce_scatter x1, waiting for transfers between devices, shards(): lax.psum_scatter(part_up.astype(jnp.bfloat16), 'dp', scatter_dimension=2,...  64.3 us
    all_to_all x15, starting transfers between devices, tick_step(): lax.all_to_all(partial_value.reshape(width_all, capacity, feature_count),...  62.6 us
    dot_general x15, matrix products, tick_step(): jnp.einsum('rd,hd->rh', unit_now, gate_slab, preferred_element_type=jnp.f...  41.8 us
    dot_general x15, matrix products, tick_step(): jnp.einsum('rd,hd->rh', unit_now, up_slab, preferred_element_type=jnp.flo...  40 us
  transfers between devices with their start and end apart: 51, of which 48 were waited for; matrix products, arithmetic and copies ran while one was open for 3% of the time, Pallas kernels for 0%

commit v1 on v0

v1 whole, which is shorter than its diff:
```python
import jax
import jax.numpy as jnp
from jax import lax
from jax.sharding import PartitionSpec as P

GROUP = 4
MICRO = 8
EPS = 1e-06
F32 = jnp.float32
BF16 = jnp.bfloat16


def dot_t(a, b):
    return lax.dot_general(a, b, (((1,), (1,)), ((), ())), preferred_element_type=F32)


def dot_n(a, b):
    return lax.dot_general(a, b, (((1,), (0,)), ((), ())), preferred_element_type=F32)


def placing_of(route_ids, experts, capacity):
    onehot = (route_ids[..., None] == jnp.arange(experts, dtype=jnp.int32)).astype(jnp.int32)
    ranking = jnp.sum((jnp.cumsum(onehot, axis=1) - onehot) * onehot, axis=2)
    slot_ids = route_ids * capacity + ranking
    positions = jnp.arange(experts * capacity, dtype=jnp.int32)[:, None]
    return (slot_ids[:, None, :] == positions).astype(BF16)


def shards(saved, cotangent, routes, w_gate, w_up, w_down):
    layers = lax.axis_size("pipe")
    width = lax.axis_size("expert")
    dp_index = lax.axis_index("dp")
    experts = width // GROUP
    feat = saved.shape[3]
    half = w_gate.shape[3]
    hidden = w_gate.shape[2]
    tok = saved.shape[2] // MICRO
    cap = tok // experts
    rows_n = width * cap

    wd_all = lax.all_gather(w_down[0, 0], ("pipe", "dp"), axis=0).reshape(layers, 2, hidden, half)
    wg_all = lax.all_gather(w_gate[0, 0], ("pipe", "dp"), axis=0).reshape(layers, 2, hidden, half)
    wu_all = lax.all_gather(w_up[0, 0], ("pipe", "dp"), axis=0).reshape(layers, 2, hidden, half)

    place = placing_of(routes[0, 0, :, 0].reshape(MICRO, tok), experts, cap)
    x = saved[0, 0].reshape(MICRO, tok, feat)
    x_slot = jnp.einsum("mst,mtd->msd", place, x, preferred_element_type=F32)
    scale = lax.rsqrt(jnp.mean(x_slot * x_slot, axis=2, keepdims=True) + EPS)
    unit = (x_slot * scale).astype(BF16)
    send = jnp.broadcast_to(
        unit.reshape(MICRO, experts, 1, cap, feat), (MICRO, experts, GROUP, cap, feat)
    ).reshape(MICRO, width, cap, feat)
    unit_rows = lax.all_to_all(send, "expert", split_axis=1, concat_axis=1, tiled=True)
    unit_rows = unit_rows.reshape(MICRO * rows_n, feat)

    extra = jnp.zeros((MICRO, tok, 128 - tok), BF16)
    cot = cotangent.reshape(MICRO, tok, cotangent.shape[1])
    pack = jnp.concatenate([x_slot.astype(BF16), place, extra, cot], axis=2)
    pack = lax.all_to_all(pack, "pipe", split_axis=0, concat_axis=0, tiled=True)
    x_all = pack[:, :, :feat]
    place_all = pack[:, :, feat : feat + tok]
    grad = jnp.transpose(pack[:, :, feat + 128 :], (1, 0, 2)).reshape(tok, feat)

    swap = [(0, 1), (1, 0)]
    wg_other = lax.ppermute(w_gate[0, 0], "dp", swap)
    wu_other = lax.ppermute(w_up[0, 0], "dp", swap)
    own = lax.dynamic_slice_in_dim(unit_rows, dp_index * half, half, 1)
    other = lax.dynamic_slice_in_dim(unit_rows, (1 - dp_index) * half, half, 1)
    gate = dot_t(own, w_gate[0, 0]) + dot_t(other, wg_other)
    up = dot_t(own, w_up[0, 0]) + dot_t(other, wu_other)
    sig = jax.nn.sigmoid(gate)
    fac = jnp.concatenate([up * sig * (1.0 + gate * (1.0 - sig)), gate * sig], axis=1).astype(BF16)
    fac = lax.all_to_all(
        fac.reshape(MICRO, rows_n, 2 * hidden), "pipe", split_axis=0, concat_axis=0, tiled=True
    )

    kept = [None] * layers
    grad = dot_n(place_all[layers - 1], grad).astype(BF16)
    for layer in range(layers - 1, -1, -1):
        send = jnp.broadcast_to(
            grad.reshape(experts, 1, cap, feat), (experts, GROUP, cap, feat)
        ).reshape(width, cap, feat)
        rows = lax.all_to_all(send, "expert", split_axis=0, concat_axis=0, tiled=True)
        rows = rows.reshape(rows_n, feat)
        hidden_grad = dot_t(rows[:, :half], wd_all[layer, 0]) + dot_t(
            rows[:, half:], wd_all[layer, 1]
        )
        both = (jnp.concatenate([hidden_grad, hidden_grad], axis=1) * fac[layer].astype(F32)).astype(
            BF16
        )
        kept[layer] = both
        if layer == 0:
            break
        gate_grad = both[:, :hidden]
        up_grad = both[:, hidden:]
        partial = jnp.concatenate(
            [
                dot_n(gate_grad, wg_all[layer, c]) + dot_n(up_grad, wu_all[layer, c])
                for c in range(2)
            ],
            axis=1,
        ).astype(BF16)
        back = lax.all_to_all(
            partial.reshape(width, cap, feat), "expert", split_axis=0, concat_axis=0, tiled=True
        )
        unit_grad = back.reshape(experts, GROUP, cap, feat).astype(F32).sum(axis=1).reshape(tok, feat)
        xl = x_all[layer].astype(F32)
        sc = lax.rsqrt(jnp.mean(xl * xl, axis=1, keepdims=True) + EPS)
        x_hat = xl * sc
        norm_grad = sc * (unit_grad - x_hat * jnp.mean(unit_grad * x_hat, axis=1, keepdims=True))
        grad = (grad.astype(F32) + norm_grad).astype(BF16)
        move = dot_t(place_all[layer - 1], place_all[layer]).astype(BF16)
        grad = dot_n(move, grad).astype(BF16)

    grads = lax.all_to_all(jnp.stack(kept), "pipe", split_axis=0, concat_axis=0, tiled=True)
    grads = grads.reshape(MICRO * rows_n, 2 * hidden)
    own = lax.dynamic_slice_in_dim(unit_rows, dp_index * half, half, 1)
    other = lax.dynamic_slice_in_dim(unit_rows, (1 - dp_index) * half, half, 1)
    outer = lambda r: lax.dot_general(
        grads, r, (((0,), (0,)), ((), ())), preferred_element_type=F32
    ).astype(BF16)
    got = lax.ppermute(outer(other), "dp", swap)
    total = (outer(own).astype(F32) + got.astype(F32)).astype(BF16)
    return total[None, None, :hidden], total[None, None, hidden:]


def solution(mesh):
    in_specs = (
        P(None, "pipe", ("expert", "dp"), None),
        P(("expert", "dp"), "pipe"),
        P(None, "pipe", ("expert", "dp"), None),
        P(None, "pipe", "expert", "dp"),
        P(None, "pipe", "expert", "dp"),
        P(None, "pipe", "expert", "dp"),
    )
    out_specs = (P(None, "pipe", "expert", "dp"), P(None, "pipe", "expert", "dp"))
    return jax.shard_map(shards, mesh=mesh, in_specs=in_specs, out_specs=out_specs, check_vma=False)
```

time: 959 us -> 685 us (0.71)
  waiting for transfers between devices: 511 us -> 242 us
  blocking collectives: 28.2 us -> 123 us
  starting transfers between devices: 159 us -> 91.9 us
  matrix products: 123 us -> 94.3 us
  other arithmetic: 55 us -> 41.1 us
    all_to_all x31 -> x11, waiting for transfers between devices: 345 us -> 175 us  [the longest x7 77.5 us: shards(): lax.all_to_all(partial.reshape(width, cap, feat), 'expert', split_axis=0,...]
    all_to_all x0 -> x8, blocking collectives: none -> 123 us  [the longest x7 107 us: shards(): lax.all_to_all(send, 'expert', split_axis=0, concat_axis=0, tiled=True)]
    reduce_scatter x2 -> x0, waiting for transfers between devices: 85.7 us -> none  [the longest x1 64.3 us: shards(): lax.psum_scatter(part_up.astype(jnp.bfloat16), 'dp', scatter_dimension=2,...]
    ppermute x15 -> x3, waiting for transfers between devices: 77.9 us -> 2.64 us  [the longest x1 2.64 us: shards(): got = lax.ppermute(outer(other), 'dp', swap)]
    all_to_all x31 -> x11, starting transfers between devices: 139 us -> 70.6 us  [the longest x7 39.2 us: shards(): lax.all_to_all(partial.reshape(width, cap, feat), 'expert', split_axis=0,...]
    all_gather x3, waiting for transfers between devices: 0.01 us -> 61.7 us  [the longest x1 61.6 us: shards(): lax.all_gather(w_up[0, 0], ('pipe', 'dp'), axis=0)]
    dot_general x93 -> x59, matrix products: 123 us -> 94.3 us  [the longest x36 61.2 us: dot_n(): lax.dot_general(a, b, (((1,), (0,)), ((), ())), preferred_element_type=F32)]
    all_gather x1 -> x0, blocking collectives: 28.2 us -> none  [shards(): head_grad = lax.all_gather(cotangent, 'pipe', axis=1, tiled=True)]
  transfers between devices with their start and end apart: 51 -> 17, of which waited for: 48 -> 12; matrix products, arithmetic and copies ran while one was open for 3% -> 6% of each run, Pallas kernels for 0% -> 0%
where the time goes in v1:
time: 685 us; the launch traced here: 673 us
  waiting for transfers between devices  242 us (35%)
  blocking collectives  123 us (18%)
  matrix products  94.3 us (14%)
  starting transfers between devices  91.9 us (13%)
  local copies, waits for them, and re-layouts  65.7 us (10%)
  other arithmetic  41.1 us (6%)
  between operations  15 us (2%)
    all_to_all x7, blocking collectives, shards(): lax.all_to_all(send, 'expert', split_axis=0, concat_axis=0, tiled=True)  107 us
    all_to_all x7, waiting for transfers between devices, shards(): lax.all_to_all(partial.reshape(width, cap, feat), 'expert', split_axis=0,...  77.5 us
    all_gather x1, waiting for transfers between devices, shards(): lax.all_gather(w_up[0, 0], ('pipe', 'dp'), axis=0)  61.6 us
    dot_general x36, matrix products, dot_n(): lax.dot_general(a, b, (((1,), (0,)), ((), ())), preferred_element_type=F32)  61.2 us
    all_to_all x1, waiting for transfers between devices, shards(): lax.all_to_all(send, 'expert', split_axis=1, concat_axis=1, tiled=True)  53 us
    all_to_all x7, starting transfers between devices, shards(): lax.all_to_all(partial.reshape(width, cap, feat), 'expert', split_axis=0,...  39.2 us
    dot_general x20, matrix products, dot_t(): lax.dot_general(a, b, (((1,), (1,)), ((), ())), preferred_element_type=F32)  31 us
    all_to_all x1, waiting for transfers between devices, shards(): pack = lax.all_to_all(pack, 'pipe', split_axis=0, concat_axis=0, tiled=True)  30.5 us
  transfers between devices with their start and end apart: 17, of which 12 were waited for; matrix products, arithmetic and copies ran while one was open for 6% of the time, Pallas kernels for 0%

profile of v1, /device:TPU:1, one launch (start us, length us, event | category | flops | bytes accessed | tf_op | source)
XLA Modules:
  0.0 672.7 jit_solution(8104762951953383605)
XLA Ops:
  14.6 10.9 %all-to-all-start = ((bf16[8,16,3008]{2,1,0:T(8,128)(2,1)}), bf16[8,16,3008]{2,1,0:T(8,128)(2,1)S(1)}, u32[]{:S(2)}, u32[]{:S(2)}) async-start(bf16[8,16,3008]{2,1,0:T(8,128)(2,1)} %concatenate.137), calls=%async_computation | async-start | bytes 1572864 | tf_op jit(solution)/shard_map/all_to_all | solution.py:59
  26.2 30.5 %all-to-all-done = bf16[8,16,3008]{2,1,0:T(8,128)(2,1)S(1)} async-done(((bf16[8,16,3008]{2,1,0:T(8,128)(2,1)}), bf16[8,16,3008]{2,1,0:T(8,128)(2,1)S(1)}, u32[]{:S(2)}, u32[]{:S(2)}) %all-to-all-start) | async-done | bytes 770080 | tf_op jit(solution)/shard_map/all_to_all | solution.py:59
  56.7 3.9 broadcast_in_dim.46
  60.6 10.0 %all-to-all-start.2 = ((bf16[8,32,2,2560]{3,2,0,1:T(2,128)(2,1)}), bf16[8,32,2,2560]{3,2,0,1:T(2,128)(2,1)S(1)}, u32[]{:S(2)}, u32[]{:S(2)}) async-start(bf16[8,32,2,2560]{3,2,0,1:T(2,128)(2,1)} %bitcast.419), calls=%async_computation.2 | async-start | bytes 5242880 | tf_op jit(solution)/shard_map/all_to_all | solution.py:53
  70.6 2.9 collective-permute-start.1
  73.5 1.9 collective-permute-start
  77.4 53.0 %all-to-all-done.2 = bf16[8,32,2,2560]{3,2,0,1:T(2,128)(2,1)S(1)} async-done(((bf16[8,32,2,2560]{3,2,0,1:T(2,128)(2,1)}), bf16[8,32,2,2560]{3,2,0,1:T(2,128)(2,1)S(1)}, u32[]{:S(2)}, u32[]{:S(2)}) %all-to-all-start.2) | async-done | bytes 2621472 | tf_op jit(solution)/shard_map/all_to_all | solution.py:53
  131.3 6.9 %all-to-all-start.1 = ((bf16[32,2,2560]{2,1,0:T(2,128)(2,1)}), bf16[32,2,2560]{2,1,0:T(2,128)(2,1)}, u32[]{:S(2)}, u32[]{:S(2)}) async-start(bf16[32,2,2560]{2,1,0:T(2,128)(2,1)} %bitcast.12), calls=%async_computation.1 | async-start | bytes 655360 | tf_op jit(solution)/shard_map/all_to_all | solution.py:83
  138.2 3.5 copy.31
  141.7 5.5 reshape.432
  154.7 3.7 all-to-all-start.3
  158.4 1.8 reshape.429
  163.3 14.3 %all-to-all-done.3 = bf16[8,64,512]{2,1,0:T(8,128)(2,1)S(1)} async-done(((bf16[8,64,512]{2,1,0:T(8,128)(2,1)}), bf16[8,64,512]{2,1,0:T(8,128)(2,1)S(1)}, u32[]{:S(2)}, u32[]{:S(2)}) %all-to-all-start.3) | async-done | bytes 524320 | tf_op jit(solution)/shard_map/all_to_all | solution.py:73
  177.6 2.2 fusion.50
  179.8 2.1 fusion.49
  181.9 61.6 %all-gather.11.cloned.1.call-done = bf16[16,1,256,1280]{3,2,1,0:T(8,128)(2,1)} async-done(((bf16[1,1,256,1280]{3,2,1,0:T(8,128)(2,1)}), bf16[16,1,256,1280]{3,2,1,0:T(8,128)(2,1)}) %all-gather.11.cloned.1.call-update) | async-done | bytes 10485776 | tf_op jit(solution)/shard_map/all_gather | solution.py:43
  243.5 2.1 fusion.1
  246.6 2.1 fusion.2
  250.3 1.9 pad_maximum_fusion.1
  252.2 9.4 %all-to-all-start.4 = ((bf16[32,2,2560]{2,1,0:T(2,128)(2,1)}), bf16[32,2,2560]{2,1,0:T(2,128)(2,1)}, u32[]{:S(2)}, u32[]{:S(2)}) async-start(bf16[32,2,2560]{2,1,0:T(2,128)(2,1)} %pad_maximum_fusion.1), calls=%async_computation.4 | async-start | bytes 655360 | tf_op jit(solution)/shard_map/all_to_all | solution.py:103
  263.1 11.4 %all-to-all-done.4 = bf16[32,2,2560]{2,1,0:T(2,128)(2,1)} async-done(((bf16[32,2,2560]{2,1,0:T(2,128)(2,1)}), bf16[32,2,2560]{2,1,0:T(2,128)(2,1)}, u32[]{:S(2)}, u32[]{:S(2)}) %all-to-all-start.4) | async-done | bytes 327712 | tf_op jit(solution)/shard_map/all_to_all | solution.py:103
  280.0 16.2 %all_to_all.95 = bf16[32,2,2560]{2,1,0:T(2,128)(2,1)} all-to-all(bf16[32,2,2560]{2,1,0:T(2,128)(2,1)S(1)} %bitcast.450), channel_id=1, replica_groups=mesh['pipe'=8,'expert'=32,'dp'=2] {'expert'}, dimensions={0} | all-to-all | bytes 655360 | tf_op jit(solution)/shard_map/all_to_all | solution.py:83
  303.0 2.1 fusion.46
  305.1 2.0 fusion.3
  308.1 2.1 fusion.4
  311.8 1.9 pad_maximum_fusion.2
  313.7 5.7 all-to-all-start.6
  319.5 10.7 %all-to-all-done.6 = bf16[32,2,2560]{2,1,0:T(2,128)(2,1)} async-done(((bf16[32,2,2560]{2,1,0:T(2,128)(2,1)}), bf16[32,2,2560]{2,1,0:T(2,128)(2,1)}, u32[]{:S(2)}, u32[]{:S(2)}) %all-to-all-start.6) | async-done | bytes 327712 | tf_op jit(solution)/shard_map/all_to_all | solution.py:103
  335.7 16.9 %all_to_all.96 = bf16[32,2,2560]{2,1,0:T(2,128)(2,1)} all-to-all(bf16[32,2,2560]{2,1,0:T(2,128)(2,1)S(1)} %bitcast.451), channel_id=1, replica_groups=mesh['pipe'=8,'expert'=32,'dp'=2] {'expert'}, dimensions={0} | all-to-all | bytes 655360 | tf_op jit(solution)/shard_map/all_to_all | solution.py:83
  358.9 2.1 fusion.43
  360.9 2.0 fusion.5
  363.9 2.1 fusion.6
  367.6 1.9 pad_maximum_fusion.3
  369.5 6.2 all-to-all-start.8
  375.8 10.8 %all-to-all-done.8 = bf16[32,2,2560]{2,1,0:T(2,128)(2,1)} async-done(((bf16[32,2,2560]{2,1,0:T(2,128)(2,1)}), bf16[32,2,2560]{2,1,0:T(2,128)(2,1)}, u32[]{:S(2)}, u32[]{:S(2)}) %all-to-all-start.8) | async-done | bytes 327712 | tf_op jit(solution)/shard_map/all_to_all | solution.py:103
  392.1 15.0 %all_to_all.97 = bf16[32,2,2560]{2,1,0:T(2,128)(2,1)} all-to-all(bf16[32,2,2560]{2,1,0:T(2,128)(2,1)S(1)} %bitcast.452), channel_id=1, replica_groups=mesh['pipe'=8,'expert'=32,'dp'=2] {'expert'}, dimensions={0} | all-to-all | bytes 655360 | tf_op jit(solution)/shard_map/all_to_all | solution.py:83
  413.9 2.1 fusion.40
  416.0 2.0 fusion.7
  419.0 2.1 fusion.8
  422.7 1.9 pad_maximum_fusion.4
  424.6 4.6 all-to-all-start.10
  429.2 11.1 %all-to-all-done.10 = bf16[32,2,2560]{2,1,0:T(2,128)(2,1)} async-done(((bf16[32,2,2560]{2,1,0:T(2,128)(2,1)}), bf16[32,2,2560]{2,1,0:T(2,128)(2,1)}, u32[]{:S(2)}, u32[]{:S(2)}) %all-to-all-start.10) | async-done | bytes 327712 | tf_op jit(solution)/shard_map/all_to_all | solution.py:103
  445.9 14.8 %all_to_all.98 = bf16[32,2,2560]{2,1,0:T(2,128)(2,1)} all-to-all(bf16[32,2,2560]{2,1,0:T(2,128)(2,1)S(1)} %bitcast.453), channel_id=1, replica_groups=mesh['pipe'=8,'expert'=32,'dp'=2] {'expert'}, dimensions={0} | all-to-all | bytes 655360 | tf_op jit(solution)/shard_map/all_to_all | solution.py:83
  467.0 2.1 fusion.37
  469.0 2.0 fusion.9
  472.0 2.1 fusion.10
  475.7 1.9 pad_maximum_fusion.5
  477.7 4.6 all-to-all-start.12
  482.3 11.1 %all-to-all-done.12 = bf16[32,2,2560]{2,1,0:T(2,128)(2,1)} async-done(((bf16[32,2,2560]{2,1,0:T(2,128)(2,1)}), bf16[32,2,2560]{2,1,0:T(2,128)(2,1)}, u32[]{:S(2)}, u32[]{:S(2)}) %all-to-all-start.12) | async-done | bytes 327712 | tf_op jit(solution)/shard_map/all_to_all | solution.py:103
  499.0 14.8 %all_to_all.99 = bf16[32,2,2560]{2,1,0:T(2,128)(2,1)} all-to-all(bf16[32,2,2560]{2,1,0:T(2,128)(2,1)S(1)} %bitcast.454), channel_id=1, replica_groups=mesh['pipe'=8,'expert'=32,'dp'=2] {'expert'}, dimensions={0} | all-to-all | bytes 655360 | tf_op jit(solution)/shard_map/all_to_all | solution.py:83
  520.7 2.1 fusion.34
  522.7 2.0 fusion.11
  525.7 2.1 fusion.12
  529.4 1.9 pad_maximum_fusion.6
  531.4 4.6 all-to-all-start.14
  536.0 11.1 %all-to-all-done.14 = bf16[32,2,2560]{2,1,0:T(2,128)(2,1)} async-done(((bf16[32,2,2560]{2,1,0:T(2,128)(2,1)}), bf16[32,2,2560]{2,1,0:T(2,128)(2,1)}, u32[]{:S(2)}, u32[]{:S(2)}) %all-to-all-start.14) | async-done | bytes 327712 | tf_op jit(solution)/shard_map/all_to_all | solution.py:103
  552.7 14.8 %all_to_all.100 = bf16[32,2,2560]{2,1,0:T(2,128)(2,1)} all-to-all(bf16[32,2,2560]{2,1,0:T(2,128)(2,1)S(1)} %bitcast.455), channel_id=1, replica_groups=mesh['pipe'=8,'expert'=32,'dp'=2] {'expert'}, dimensions={0} | all-to-all | bytes 655360 | tf_op jit(solution)/shard_map/all_to_all | solution.py:83
  575.7 2.0 fusion.13
  581.1 4.1 all-to-all-start.16
  585.3 11.2 %all-to-all-done.16 = bf16[32,2,2560]{2,1,0:T(2,128)(2,1)S(1)} async-done(((bf16[32,2,2560]{2,1,0:T(2,128)(2,1)}), bf16[32,2,2560]{2,1,0:T(2,128)(2,1)S(1)}, u32[]{:S(2)}, u32[]{:S(2)}) %all-to-all-start.16) | async-done | bytes 327712 | tf_op jit(solution)/shard_map/all_to_all | solution.py:103
  601.0 14.8 %all_to_all.101 = bf16[32,2,2560]{2,1,0:T(2,128)(2,1)} all-to-all(bf16[32,2,2560]{2,1,0:T(2,128)(2,1)S(1)} %bitcast.456), channel_id=1, replica_groups=mesh['pipe'=8,'expert'=32,'dp'=2] {'expert'}, dimensions={0} | all-to-all | bytes 655360 | tf_op jit(solution)/shard_map/all_to_all | solution.py:83
  628.1 15.7 %all_to_all.102 = bf16[8,64,512]{2,1,0:T(8,128)(2,1)S(1)} all-to-all(bf16[8,64,512]{2,1,0:T(8,128)(2,1)S(1)} %fusion.188), channel_id=1, replica_groups=mesh['pipe'=8,'expert'=32,'dp'=2] {'pipe'}, dimensions={0} | all-to-all | bytes 1048576 | tf_op jit(solution)/shard_map/all_to_all | solution.py:115
  644.6 16.4 %collective-permute-start.2 = (bf16[512,1280]{1,0:T(8,128)(2,1)S(1)}, bf16[512,1280]{1,0:T(8,128)(2,1)S(1)}, u32[]{:S(2)}, u32[]{:S(2)}) collective-permute-start(bf16[512,1280]{1,0:T(8,128)(2,1)S(1)} %convolution_convert_fusion.8), channel_id=1, source_target_pairs={{0,1},{1,0},{2,3},{3,2},{4,5},{5,4},{6,7},{7,6},{8,9},{9,8},{10,11... | collective-permute-start | bytes 3932168 | tf_op jit(solution)/shard_map/ppermute | solution.py:122
  661.0 2.6 collective-permute-done.2
  (190 shorter events, 135.9 us)
Async XLA Ops:
  7.2 5.7 copy-start
  7.2 153.0 %all-gather.7.cloned.1.call-start = ((), (), s32[]{:S(2)}) async-start(), calls=%async_computation.19 | async-start | bytes 11141120 | tf_op jit(solution)/shard_map/all_gather | solution.py:41
  7.9 169.7 %all-gather.9.cloned.1.call-start = ((), (), s32[]{:S(2)}) async-start(), calls=%async_computation.20 | async-start | bytes 11141120 | tf_op jit(solution)/shard_map/all_gather | solution.py:42
  8.7 234.9 %all-gather.11.cloned.1.call-start = ((), (), s32[]{:S(2)}) async-start(), calls=%async_computation.21 | async-start | bytes 11141120 | tf_op jit(solution)/shard_map/all_gather | solution.py:43
  14.6 42.0 %all-to-all-start = ((bf16[8,16,3008]{2,1,0:T(8,128)(2,1)}), bf16[8,16,3008]{2,1,0:T(8,128)(2,1)S(1)}, u32[]{:S(2)}, u32[]{:S(2)}) async-start(bf16[8,16,3008]{2,1,0:T(8,128)(2,1)} %concatenate.137), calls=%async_computation | async-start | bytes 1572864 | tf_op jit(solution)/shard_map/all_to_all | solution.py:59
  56.7 3.9 copy-start.2
  60.6 69.8 %all-to-all-start.2 = ((bf16[8,32,2,2560]{3,2,0,1:T(2,128)(2,1)}), bf16[8,32,2,2560]{3,2,0,1:T(2,128)(2,1)S(1)}, u32[]{:S(2)}, u32[]{:S(2)}) async-start(bf16[8,32,2,2560]{3,2,0,1:T(2,128)(2,1)} %bitcast.419), calls=%async_computation.2 | async-start | bytes 5242880 | tf_op jit(solution)/shard_map/all_to_all | solution.py:53
  70.6 78.2 %collective-permute-start.1 = (bf16[256,1280]{1,0:T(8,128)(2,1)}, bf16[256,1280]{1,0:T(8,128)(2,1)}, u32[]{:S(2)}, u32[]{:S(2)}) collective-permute-start(bf16[256,1280]{1,0:T(8,128)(2,1)} %bitcast.448), channel_id=1, source_target_pairs={{0,1},{1,0},{2,3},{3,2},{4,5},{5,4},{6,7},{7,6},{8,9},{9,8},{10,11... | collective-permute-start | bytes 1966088 | tf_op jit(solution)/shard_map/ppermute | solution.py:65
  73.5 78.7 %collective-permute-start = (bf16[256,1280]{1,0:T(8,128)(2,1)}, bf16[256,1280]{1,0:T(8,128)(2,1)}, u32[]{:S(2)}, u32[]{:S(2)}) collective-permute-start(bf16[256,1280]{1,0:T(8,128)(2,1)} %bitcast.449), channel_id=1, source_target_pairs={{0,1},{1,0},{2,3},{3,2},{4,5},{5,4},{6,7},{7,6},{8,9},{9,8},{10,11... | collective-permute-start | bytes 1966088 | tf_op jit(solution)/shard_map/ppermute | solution.py:66
  131.3 23.4 %all-to-all-start.1 = ((bf16[32,2,2560]{2,1,0:T(2,128)(2,1)}), bf16[32,2,2560]{2,1,0:T(2,128)(2,1)}, u32[]{:S(2)}, u32[]{:S(2)}) async-start(bf16[32,2,2560]{2,1,0:T(2,128)(2,1)} %bitcast.12), calls=%async_computation.1 | async-start | bytes 655360 | tf_op jit(solution)/shard_map/all_to_all | solution.py:83
  154.7 22.9 %all-to-all-start.3 = ((bf16[8,64,512]{2,1,0:T(8,128)(2,1)}), bf16[8,64,512]{2,1,0:T(8,128)(2,1)S(1)}, u32[]{:S(2)}, u32[]{:S(2)}) async-start(bf16[8,64,512]{2,1,0:T(8,128)(2,1)} %pad_maximum_fusion), calls=%async_computation.3 | async-start | bytes 1048576 | tf_op jit(solution)/shard_map/all_to_all | solution.py:73
  163.3 115.3 %copy-start.5 = (f32[64,256]{1,0:T(8,128)}, f32[64,256]{1,0:T(8,128)S(1)}, u32[]{:S(2)}) copy-start(f32[64,256]{1,0:T(8,128)S(1)} %convolution_add_fusion.23) | copy-start | bytes 196612
  177.6 394.8 %copy-start.3 = (bf16[8,64,512]{2,1,0:T(8,128)(2,1)}, bf16[8,64,512]{2,1,0:T(8,128)(2,1)S(1)}, u32[]{:S(2)}) copy-start(bf16[8,64,512]{2,1,0:T(8,128)(2,1)S(1)} %all-to-all-done.3) | copy-start | bytes 1572868
  252.2 22.2 %all-to-all-start.4 = ((bf16[32,2,2560]{2,1,0:T(2,128)(2,1)}), bf16[32,2,2560]{2,1,0:T(2,128)(2,1)}, u32[]{:S(2)}, u32[]{:S(2)}) async-start(bf16[32,2,2560]{2,1,0:T(2,128)(2,1)} %pad_maximum_fusion.1), calls=%async_computation.4 | async-start | bytes 655360 | tf_op jit(solution)/shard_map/all_to_all | solution.py:103
  301.1 0.6 copy-start.6
  313.7 16.5 %all-to-all-start.6 = ((bf16[32,2,2560]{2,1,0:T(2,128)(2,1)}), bf16[32,2,2560]{2,1,0:T(2,128)(2,1)}, u32[]{:S(2)}, u32[]{:S(2)}) async-start(bf16[32,2,2560]{2,1,0:T(2,128)(2,1)} %pad_maximum_fusion.2), calls=%async_computation.6 | async-start | bytes 655360 | tf_op jit(solution)/shard_map/all_to_all | solution.py:103
  357.5 33.2 %copy-start.7 = (f32[64,256]{1,0:T(8,128)}, f32[64,256]{1,0:T(8,128)S(1)}, u32[]{:S(2)}) copy-start(f32[64,256]{1,0:T(8,128)S(1)} %convolution_add_fusion.21) | copy-start | bytes 196612
  369.5 17.0 %all-to-all-start.8 = ((bf16[32,2,2560]{2,1,0:T(2,128)(2,1)}), bf16[32,2,2560]{2,1,0:T(2,128)(2,1)}, u32[]{:S(2)}, u32[]{:S(2)}) async-start(bf16[32,2,2560]{2,1,0:T(2,128)(2,1)} %pad_maximum_fusion.3), calls=%async_computation.8 | async-start | bytes 655360 | tf_op jit(solution)/shard_map/all_to_all | solution.py:103
  412.0 0.6 copy-start.8
  424.6 15.7 %all-to-all-start.10 = ((bf16[32,2,2560]{2,1,0:T(2,128)(2,1)}), bf16[32,2,2560]{2,1,0:T(2,128)(2,1)}, u32[]{:S(2)}, u32[]{:S(2)}) async-start(bf16[32,2,2560]{2,1,0:T(2,128)(2,1)} %pad_maximum_fusion.4), calls=%async_computation.10 | async-start | bytes 655360 | tf_op jit(solution)/shard_map/all_to_all | solution.py:103
  465.6 31.9 %copy-start.9 = (f32[64,256]{1,0:T(8,128)}, f32[64,256]{1,0:T(8,128)S(1)}, u32[]{:S(2)}) copy-start(f32[64,256]{1,0:T(8,128)S(1)} %convolution_add_fusion.19) | copy-start | bytes 196612
  477.7 15.8 %all-to-all-start.12 = ((bf16[32,2,2560]{2,1,0:T(2,128)(2,1)}), bf16[32,2,2560]{2,1,0:T(2,128)(2,1)}, u32[]{:S(2)}, u32[]{:S(2)}) async-start(bf16[32,2,2560]{2,1,0:T(2,128)(2,1)} %pad_maximum_fusion.5), calls=%async_computation.12 | async-start | bytes 655360 | tf_op jit(solution)/shard_map/all_to_all | solution.py:103
  518.7 0.6 copy-start.10
  531.4 15.7 %all-to-all-start.14 = ((bf16[32,2,2560]{2,1,0:T(2,128)(2,1)}), bf16[32,2,2560]{2,1,0:T(2,128)(2,1)}, u32[]{:S(2)}, u32[]{:S(2)}) async-start(bf16[32,2,2560]{2,1,0:T(2,128)(2,1)} %pad_maximum_fusion.6), calls=%async_computation.14 | async-start | bytes 655360 | tf_op jit(solution)/shard_map/all_to_all | solution.py:103
  572.4 0.6 copy-start.11
  573.0 2.7 copy-start.4
  581.1 15.3 %all-to-all-start.16 = ((bf16[32,2,2560]{2,1,0:T(2,128)(2,1)}), bf16[32,2,2560]{2,1,0:T(2,128)(2,1)S(1)}, u32[]{:S(2)}, u32[]{:S(2)}) async-start(bf16[32,2,2560]{2,1,0:T(2,128)(2,1)} %pad_maximum_fusion.7), calls=%async_computation.16 | async-start | bytes 655360 | tf_op jit(solution)/shard_map/all_to_all | solution.py:103
  597.5 68.2 %copy-start.1 = (bf16[1,1,128,2560]{3,2,1,0:T(8,128)(2,1)S(1)}, bf16[1,1,128,2560]{3,2,1,0:T(8,128)(2,1)}, u32[]{:S(2)}) copy-start(bf16[1,1,128,2560]{3,2,1,0:T(8,128)(2,1)} %param.6) | copy-start | bytes 1966084
  644.6 19.0 %collective-permute-start.2 = (bf16[512,1280]{1,0:T(8,128)(2,1)S(1)}, bf16[512,1280]{1,0:T(8,128)(2,1)S(1)}, u32[]{:S(2)}, u32[]{:S(2)}) collective-permute-start(bf16[512,1280]{1,0:T(8,128)(2,1)S(1)} %convolution_convert_fusion.8), channel_id=1, source_target_pairs={{0,1},{1,0},{2,3},{3,2},{4,5},{5,4},{6,7},{7,6},{8,9},{9,8},{10,11... | collective-permute-start | bytes 3932168 | tf_op jit(solution)/shard_map/ppermute | solution.py:122
Sparse Core Ops, SparseCore 0:
  10.1 87.2 all-gather.6
  99.6 74.8 all-gather.8
  176.6 66.8 all-gather.10

commit v2 on v1

v2 whole, which is shorter than its diff:
```python
import jax
import jax.numpy as jnp
from jax import lax
from jax.experimental import pallas as pl
from jax.experimental.pallas import tpu as pltpu
from jax.sharding import PartitionSpec as P

GROUP = 4
MICRO = 8
PARTS = 4
EPS = 1e-06
F32 = jnp.float32
BF16 = jnp.bfloat16
SETS = ((7, 6), (5, 4, 3), (2, 1, 0))


def dot_t(a, b):
    return lax.dot_general(a, b, (((1,), (1,)), ((), ())), preferred_element_type=F32)


def dot_n(a, b):
    return lax.dot_general(a, b, (((1,), (0,)), ((), ())), preferred_element_type=F32)


def placing_of(route_ids, experts, capacity):
    onehot = (route_ids[..., None] == jnp.arange(experts, dtype=jnp.int32)).astype(jnp.int32)
    ranking = jnp.sum((jnp.cumsum(onehot, axis=1) - onehot) * onehot, axis=2)
    slot_ids = route_ids * capacity + ranking
    positions = jnp.arange(experts * capacity, dtype=jnp.int32)[:, None]
    return (slot_ids[:, None, :] == positions).astype(BF16)


def expert_call(layer, where, last, rows, weights, fac, kept):
    n_in, lanes = rows.shape
    rows_n = n_in // PARTS
    chunks, _, _, _, rows_c, half = weights.shape
    hidden = chunks * rows_c
    per_half = half // lanes
    mats = 1 if last else 3

    def body(rows_ref, w_ref, fac_ref, _, *refs):
        kept_ref = refs[0]
        outs = refs[1:]
        if last:
            w_vm, stage, sem = outs
        else:
            out_ref, w_vm, stage, sem = outs
        copies = [
            [
                pltpu.make_async_copy(w_ref.at[:, c, where, m], w_vm.at[m, c], sem.at[m, c])
                for c in range(2)
            ]
            for m in range(mats)
        ]
        for pair in copies:
            for copy in pair:
                copy.start()
        blocks = lanes // 128
        for b in range(blocks):
            stage[b] = rows_ref[:, b * 128 : (b + 1) * 128].astype(F32)
        hidden_grad = jnp.zeros((rows_n, hidden), F32)
        for c in range(2):
            copies[0][c].wait()
            for j in range(per_half):
                k = c * per_half + j
                part = jnp.concatenate(
                    [stage[b, pl.ds(k, rows_n, stride=PARTS), :] for b in range(blocks)], axis=1
                ).astype(BF16)
                w = w_vm[0, c, :, :, j * lanes : (j + 1) * lanes].reshape(hidden, lanes)
                hidden_grad = hidden_grad + dot_t(part, w)
        f = fac_ref[0].astype(F32)
        gate_grad = (hidden_grad * f[:, :hidden]).astype(BF16)
        up_grad = (hidden_grad * f[:, hidden:]).astype(BF16)
        kept_ref[0, :, :hidden] = gate_grad
        kept_ref[0, :, hidden:] = up_grad
        if last:
            return
        for c in range(2):
            copies[1][c].wait()
            copies[2][c].wait()
            for j in range(per_half):
                k = c * per_half + j
                g = w_vm[1, c, :, :, j * lanes : (j + 1) * lanes].reshape(hidden, lanes)
                u = w_vm[2, c, :, :, j * lanes : (j + 1) * lanes].reshape(hidden, lanes)
                part = dot_n(gate_grad, g) + dot_n(up_grad, u)
                for b in range(blocks):
                    stage[b, pl.ds(k, rows_n, stride=PARTS), :] = part[:, b * 128 : (b + 1) * 128]
        for b in range(blocks):
            out_ref[:, b * 128 : (b + 1) * 128] = stage[b].astype(BF16)

    block = pl.BlockSpec((1, rows_n, 2 * hidden), lambda i: (layer, 0, 0))
    whole = pl.BlockSpec((n_in, lanes), lambda i: (0, 0))
    out_shape = [jax.ShapeDtypeStruct(kept.shape, BF16)]
    out_specs = [block]
    if not last:
        out_shape.append(jax.ShapeDtypeStruct((n_in, lanes), BF16))
        out_specs.append(whole)
    return pl.pallas_call(
        body,
        grid=(1,),
        in_specs=[
            whole,
            pl.BlockSpec(memory_space=pl.ANY),
            block,
            pl.BlockSpec(memory_space=pl.ANY),
        ],
        out_specs=out_specs,
        out_shape=out_shape,
        scratch_shapes=[
            pltpu.VMEM((mats, 2, chunks, rows_c, half), BF16),
            pltpu.VMEM((lanes // 128, n_in, 128), F32),
            pltpu.SemaphoreType.DMA((3, 2)),
        ],
        input_output_aliases={3: 0},
        compiler_params=pltpu.CompilerParams(vmem_limit_bytes=24 * 1024 * 1024),
        cost_estimate=pl.CostEstimate(
            flops=6 * rows_n * hidden * 2 * half, bytes_accessed=mats * 4 * hidden * half, transcendentals=0
        ),
        name="expert",
    )(rows, weights, fac, kept)


def spread(send_ref, g, experts):
    size = g.shape[0] // experts
    for e in range(experts):
        piece = g[e * size : (e + 1) * size].astype(BF16)
        for q in range(GROUP):
            send_ref[e * GROUP + q] = piece


def home_call(layer, experts, back, grad, x, move):
    n_in, lanes = back.shape
    slots = n_in // GROUP
    size = slots // experts
    features = PARTS * lanes

    def body(back_ref, grad_ref, x_ref, move_ref, out_ref, send_ref):
        total = back_ref[...].astype(F32).reshape(experts, GROUP, size, lanes).sum(axis=1)
        total = total.reshape(slots, lanes)
        xf = x_ref[0].astype(F32)
        square = jnp.sum(xf * xf, axis=1, keepdims=True)
        cross = jnp.sum(total * xf, axis=1, keepdims=True)
        row = lax.broadcasted_iota(jnp.int32, (slots, slots), 0) // PARTS
        col = lax.broadcasted_iota(jnp.int32, (slots, slots), 1) // PARTS
        same = (row == col).astype(F32) * (1.0 / features)
        lane = lax.broadcasted_iota(jnp.int32, (slots, 128), 1)
        sums = jnp.where(lane < 64, square, cross)
        means = lax.dot_general(
            same, sums, (((1,), (0,)), ((), ())),
            precision=lax.Precision.HIGHEST, preferred_element_type=F32,
        )
        scale = lax.rsqrt(means[:, :1] + EPS)
        mean = scale * means[:, 64:65]
        grad_new = grad_ref[...].astype(F32) + scale * (total - (xf * scale) * mean)
        moved = dot_n(move_ref[0], grad_new.astype(BF16))
        out_ref[...] = moved.astype(BF16)
        spread(send_ref, moved, experts)

    return pl.pallas_call(
        body,
        grid=(1,),
        in_specs=[
            pl.BlockSpec((n_in, lanes), lambda i: (0, 0)),
            pl.BlockSpec((slots, lanes), lambda i: (0, 0)),
            pl.BlockSpec((1, slots, lanes), lambda i: (layer, 0, 0)),
            pl.BlockSpec((1, slots, slots), lambda i: (layer, 0, 0)),
        ],
        out_specs=[
            pl.BlockSpec((slots, lanes), lambda i: (0, 0)),
            pl.BlockSpec((experts * GROUP, size, lanes), lambda i: (0, 0, 0)),
        ],
        out_shape=[
            jax.ShapeDtypeStruct((slots, lanes), BF16),
            jax.ShapeDtypeStruct((experts * GROUP, size, lanes), BF16),
        ],
        cost_estimate=pl.CostEstimate(flops=10 * n_in * lanes, bytes_accessed=4 * n_in * lanes, transcendentals=0),
        name="home",
    )(back, grad, x, move)


def shards(saved, cotangent, routes, w_gate, w_up, w_down):
    layers = lax.axis_size("pipe")
    width = lax.axis_size("expert")
    dp_index = lax.axis_index("dp")
    experts = width // GROUP
    feat = saved.shape[3]
    half = w_gate.shape[3]
    hidden = w_gate.shape[2]
    tok = saved.shape[2] // MICRO
    cap = tok // experts
    rows_n = width * cap
    lanes = feat // PARTS
    slots = tok * PARTS
    size = cap * PARTS

    place = placing_of(routes[0, 0, :, 0].reshape(MICRO, tok), experts, cap)
    x = saved[0, 0].reshape(MICRO, tok, feat)
    x_slot = jnp.einsum("mst,mtd->msd", place, x, preferred_element_type=F32)

    thin = cotangent.shape[1] // PARTS
    extra = jnp.concatenate(
        [
            jnp.repeat(place, PARTS, axis=1),
            cotangent.reshape(MICRO, slots, thin),
            jnp.zeros((MICRO, slots, 128 - tok - thin), BF16),
        ],
        axis=2,
    )
    pack = jnp.concatenate([x_slot.astype(BF16).reshape(MICRO, slots, lanes), extra], axis=2)
    pack = lax.all_to_all(pack, "pipe", split_axis=0, concat_axis=0, tiled=True)
    x_all = pack[:, :, :lanes]
    place_all = pack[:, :, lanes : lanes + tok]
    grad = pack[:, :, lanes + tok : lanes + tok + thin].reshape(layers, tok, PARTS * thin)
    grad = jnp.transpose(grad, (1, 0, 2)).reshape(tok, feat)
    grad = dot_n(place_all[layers - 1, ::PARTS], grad).astype(BF16).reshape(slots, lanes)
    quarter = jnp.arange(slots, dtype=jnp.int32) % PARTS
    move = jnp.einsum("lat,lbt->lab", jnp.roll(place_all, 1, axis=0), place_all, preferred_element_type=F32)
    move = jnp.where(quarter[:, None] == quarter[None, :], move, 0.0).astype(BF16)

    cut = jnp.stack([w_down[0, 0], w_gate[0, 0], w_up[0, 0]]).reshape(3, layers, hidden // layers, half)
    cut = lax.all_to_all(cut, "pipe", split_axis=1, concat_axis=1, tiled=True)
    weights = {}
    for members in SETS:
        low = min(members)
        got = lax.all_gather(
            jnp.transpose(cut[:, low : low + len(members)], (1, 0, 2, 3)), ("pipe", "dp"), axis=0
        ).reshape(layers, 2, len(members), 3, hidden // layers, half)
        for layer in members:
            weights[layer] = (got, layer - low)

    scale = lax.rsqrt(jnp.mean(x_slot * x_slot, axis=2, keepdims=True) + EPS)
    unit = (x_slot * scale).astype(BF16)
    send = jnp.broadcast_to(
        unit.reshape(MICRO, experts, 1, cap, feat), (MICRO, experts, GROUP, cap, feat)
    ).reshape(MICRO, width, cap, feat)
    unit_rows = lax.all_to_all(send, "expert", split_axis=1, concat_axis=1, tiled=True)
    unit_rows = unit_rows.reshape(MICRO * rows_n, feat)
    swap = [(0, 1), (1, 0)]
    wg_other = lax.ppermute(w_gate[0, 0], "dp", swap)
    wu_other = lax.ppermute(w_up[0, 0], "dp", swap)
    own = lax.dynamic_slice_in_dim(unit_rows, dp_index * half, half, 1)
    other = lax.dynamic_slice_in_dim(unit_rows, (1 - dp_index) * half, half, 1)
    gate = dot_t(own, w_gate[0, 0]) + dot_t(other, wg_other)
    up = dot_t(own, w_up[0, 0]) + dot_t(other, wu_other)
    sig = jax.nn.sigmoid(gate)
    fac = jnp.concatenate([up * sig * (1.0 + gate * (1.0 - sig)), gate * sig], axis=1).astype(BF16)
    fac = lax.all_to_all(
        fac.reshape(MICRO, rows_n, 2 * hidden), "pipe", split_axis=0, concat_axis=0, tiled=True
    )

    def exchange(block):
        block = block.reshape(width, size, lanes)
        block = lax.all_to_all(block, "expert", split_axis=0, concat_axis=0, tiled=True)
        return block.reshape(width * size, lanes)

    kept = jnp.zeros((layers, rows_n, 2 * hidden), BF16)
    send = jnp.broadcast_to(
        grad.reshape(experts, 1, size, lanes), (experts, GROUP, size, lanes)
    ).reshape(width, size, lanes)
    for layer in range(layers - 1, -1, -1):
        rows = exchange(send)
        got, where = weights[layer]
        if layer == 0:
            (kept,) = expert_call(layer, where, True, rows, got, fac, kept)
            break
        kept, partial = expert_call(layer, where, False, rows, got, fac, kept)
        grad, send = home_call(layer, experts, exchange(partial), grad, x_all, move)

    grads = lax.all_to_all(kept, "pipe", split_axis=0, concat_axis=0, tiled=True)
    grads = grads.reshape(MICRO * rows_n, 2 * hidden)

    def outer(rows):
        return lax.dot_general(
            grads, rows, (((0,), (0,)), ((), ())), preferred_element_type=F32
        ).astype(BF16)

    got = lax.ppermute(outer(other), "dp", swap)
    total = (outer(own).astype(F32) + got.astype(F32)).astype(BF16)
    return total[None, None, :hidden], total[None, None, hidden:]


def solution(mesh):
    in_specs = (
        P(None, "pipe", ("expert", "dp"), None),
        P(("expert", "dp"), "pipe"),
        P(None, "pipe", ("expert", "dp"), None),
        P(None, "pipe", "expert", "dp"),
        P(None, "pipe", "expert", "dp"),
        P(None, "pipe", "expert", "dp"),
    )
    out_specs = (P(None, "pipe", "expert", "dp"), P(None, "pipe", "expert", "dp"))
    return jax.shard_map(shards, mesh=mesh, in_specs=in_specs, out_specs=out_specs, check_vma=False)
```

time: 685 us -> 568 us (0.83); the launches traced: 673 us -> 566 us
  blocking collectives: 123 us -> 272 us
  waiting for transfers between devices: 242 us -> 99.1 us
  matrix products: 94.3 us -> 9.52 us
  other arithmetic: 41.1 us -> 4.27 us
  Pallas kernels: 0 us -> 34.6 us
  starting transfers between devices: 91.9 us -> 70.2 us
    all_to_all x8 -> x15, blocking collectives: 123 us -> 272 us  [the longest x12 183 us: exchange(): lax.all_to_all(block, 'expert', split_axis=0, concat_axis=0, tiled=True)]
    all_to_all x9 -> x3, waiting for transfers between devices: 91.8 us -> 21.7 us  [exchange(): lax.all_to_all(block, 'expert', split_axis=0, concat_axis=0, tiled=True)]
    all_gather x3, waiting for transfers between devices: 61.7 us -> 0.02 us  [shards(): lax.all_gather(jnp.transpose(cut[:, low:low + len(members)], (1, 0, 2, 3)...]
    dot_general x36 -> x1, matrix products: 61.2 us -> 0.13 us  [dot_n(): lax.dot_general(a, b, (((1,), (0,)), ((), ())), preferred_element_type=F32)]
    pallas_call x0 -> x15, Pallas kernels: none -> 34.6 us  [the longest x8 17.7 us: expert_call(): pl.pallas_call(body, grid=(1,), in_specs=[whole, pl.BlockSpec(memory_spac...]
    unnamed x26 -> x42, local copies, waits for them, and re-layouts: 4 us -> 35.4 us
    all_to_all x9 -> x3, starting transfers between devices: 49.7 us -> 21.8 us  [exchange(): lax.all_to_all(block, 'expert', split_axis=0, concat_axis=0, tiled=True)]
    dot_general x20 -> x4, matrix products: 31 us -> 6.33 us  [dot_t(): lax.dot_general(a, b, (((1,), (1,)), ((), ())), preferred_element_type=F32)]
  transfers between devices with their start and end apart: 17 -> 11, of which waited for: 12 -> 5; matrix products, arithmetic and copies ran while one was open for 6% -> 6% of each run, Pallas kernels for 0% -> 4%
where the time goes in v2:
time: 568 us; the launch traced here: 566 us
  blocking collectives  272 us (48%)
  waiting for transfers between devices  99.1 us (17%)
  starting transfers between devices  70.2 us (12%)
  local copies, waits for them, and re-layouts  62.2 us (11%)
  Pallas kernels  34.6 us (6%)
  between operations  14.2 us (2%)
  matrix products  9.52 us (2%)
    all_to_all x12, blocking collectives, exchange(): lax.all_to_all(block, 'expert', split_axis=0, concat_axis=0, tiled=True)  183 us
    all_to_all x1, blocking collectives, shards(): cut = lax.all_to_all(cut, 'pipe', split_axis=1, concat_axis=1, tiled=True)  57.9 us
    all_to_all x1, waiting for transfers between devices, shards(): lax.all_to_all(send, 'expert', split_axis=1, concat_axis=1, tiled=True)  44.7 us
    unnamed x42, local copies, waits for them, and re-layouts  35.4 us
    all_to_all x1, waiting for transfers between devices, shards(): pack = lax.all_to_all(pack, 'pipe', split_axis=0, concat_axis=0, tiled=True)  29.3 us
    ppermute x1, starting transfers between devices, shards(): got = lax.ppermute(outer(other), 'dp', swap)  27.8 us
    all_to_all x3, starting transfers between devices, exchange(): lax.all_to_all(block, 'expert', split_axis=0, concat_axis=0, tiled=True)  21.8 us
    all_to_all x3, waiting for transfers between devices, exchange(): lax.all_to_all(block, 'expert', split_axis=0, concat_axis=0, tiled=True)  21.7 us
  transfers between devices with their start and end apart: 11, of which 5 were waited for; matrix products, arithmetic and copies ran while one was open for 6% of the time, Pallas kernels for 4%

profile of v2, /device:TPU:1, one launch (start us, length us, event | category | flops | bytes accessed | tf_op | source)
XLA Modules:
  0.0 566.2 jit_solution(8948939201582905496)
XLA Ops:
  7.2 1.8 pad_maximum_fusion
  9.0 57.9 %all_to_all.100 = bf16[3,8,32,1280]{3,2,0,1:T(8,128)(2,1)S(1)} all-to-all(bf16[3,8,32,1280]{3,2,0,1:T(8,128)(2,1)S(1)} %pad_maximum_fusion), channel_id=1, replica_groups=mesh['pipe'=8,'expert'=32,'dp'=2] {'pipe'}, dimensions={1} | all-to-all | bytes 3932160 | tf_op jit(solution)/shard_map/all_to_all | solution.py:221
  67.8 1.2 slice_bitcast_fusion
  73.4 1.1 maximum_maximum_fusion
  74.4 3.5 all-to-all-start
  78.7 29.3 %all-to-all-done = bf16[8,64,768]{2,1,0:T(8,128)(2,1)S(1)} async-done(((bf16[8,64,768]{2,1,0:T(8,128)(2,1)}), bf16[8,64,768]{2,1,0:T(8,128)(2,1)S(1)}, u32[]{:S(2)}, u32[]{:S(2)}) %all-to-all-start) | async-done | bytes 786464 | tf_op jit(solution)/shard_map/all_to_all | solution.py:210
  108.0 3.9 broadcast_in_dim.47
  111.9 9.8 %all-to-all-start.3 = ((bf16[8,32,2,2560]{3,2,0,1:T(2,128)(2,1)}), bf16[8,32,2,2560]{3,2,0,1:T(2,128)(2,1)S(1)}, u32[]{:S(2)}, u32[]{:S(2)}) async-start(bf16[8,32,2,2560]{3,2,0,1:T(2,128)(2,1)} %bitcast.87), calls=%async_computation.3 | async-start | bytes 5242880 | tf_op jit(solution)/shard_map/all_to_all | solution.py:236
  121.8 5.1 collective-permute-start.1
  126.9 1.9 collective-permute-start
  128.8 1.0 slice.49
  130.1 1.6 slice.48
  132.7 44.7 %all-to-all-done.3 = bf16[8,32,2,2560]{3,2,0,1:T(2,128)(2,1)S(1)} async-done(((bf16[8,32,2,2560]{3,2,0,1:T(2,128)(2,1)}), bf16[8,32,2,2560]{3,2,0,1:T(2,128)(2,1)S(1)}, u32[]{:S(2)}, u32[]{:S(2)}) %all-to-all-start.3) | async-done | bytes 2621472 | tf_op jit(solution)/shard_map/all_to_all | solution.py:236
  178.9 8.9 %all-to-all-start.1 = ((bf16[32,8,640]{2,1,0:T(8,128)(2,1)}), bf16[32,8,640]{2,1,0:T(8,128)(2,1)S(1)}, u32[]{:S(2)}, u32[]{:S(2)}) async-start(bf16[32,8,640]{2,1,0:T(8,128)(2,1)} %bitcast.99), calls=%async_computation.1 | async-start | bytes 655360 | tf_op jit(solution)/shard_map/all_to_all | solution.py:253
  187.9 5.2 copy.55
  193.1 6.7 %reshape.168 = bf16[512,2560]{1,0:T(8,128)(2,1)} reshape(bf16[8,32,2,2560]{3,2,1,0:T(2,128)(2,1)} %copy.55) | data formatting | bytes 5242880 | tf_op jit(solution)/shard_map/reshape | solution.py:237
  199.7 1.9 fusion.10
  201.6 2.3 multiply_convert_fusion.1
  204.7 1.7 fusion.3
  206.5 16.3 %all_to_all.101.fac_ref = bf16[8,64,512]{2,1,0:T(8,128)(2,1)S(1)} all-to-all(bf16[8,64,512]{2,1,0:T(8,128)(2,1)S(1)} %pad_maximum_fusion.1), channel_id=1, replica_groups=mesh['pipe'=8,'expert'=32,'dp'=2] {'pipe'}, dimensions={0} | all-to-all | bytes 1048576 | tf_op jit(solution)/shard_map/all_to_all | solution.py:247
  222.8 3.2 copy-done.8
  226.1 3.0 expert.8
  229.1 8.8 %all-to-all-start.5 = ((bf16[32,8,640]{2,1,0:T(8,128)(2,1)}), bf16[32,8,640]{2,1,0:T(8,128)(2,1)S(1)}, u32[]{:S(2)}, u32[]{:S(2)}) async-start(bf16[32,8,640]{2,1,0:T(8,128)(2,1)} %bitcast.16), calls=%async_computation.5 | async-start | bytes 655360 | tf_op jit(solution)/shard_map/all_to_all | solution.py:253
  238.9 0.9 slice.51.x_ref
  240.7 7.9 %all-to-all-done.5 = bf16[32,8,640]{2,1,0:T(8,128)(2,1)S(1)} async-done(((bf16[32,8,640]{2,1,0:T(8,128)(2,1)}), bf16[32,8,640]{2,1,0:T(8,128)(2,1)S(1)}, u32[]{:S(2)}, u32[]{:S(2)}) %all-to-all-start.5) | async-done | bytes 327712 | tf_op jit(solution)/shard_map/all_to_all | solution.py:253
  249.3 2.4 home.7
  251.8 14.8 %all_to_all.102 = bf16[32,8,640]{2,1,0:T(8,128)(2,1)S(1)} all-to-all(bf16[32,8,640]{2,1,0:T(8,128)(2,1)} %get-tuple-element.30), channel_id=1, replica_groups=mesh['pipe'=8,'expert'=32,'dp'=2] {'expert'}, dimensions={0} | all-to-all | bytes 655360 | tf_op jit(solution)/shard_map/all_to_all | solution.py:253
  266.6 3.4 copy-done.9
  270.0 2.3 expert.9
  272.2 14.8 %all_to_all.103 = bf16[32,8,640]{2,1,0:T(8,128)(2,1)} all-to-all(bf16[32,8,640]{2,1,0:T(8,128)(2,1)S(1)} %bitcast.81), channel_id=1, replica_groups=mesh['pipe'=8,'expert'=32,'dp'=2] {'expert'}, dimensions={0} | all-to-all | bytes 655360 | tf_op jit(solution)/shard_map/all_to_all | solution.py:253
  287.0 2.4 home.8
  289.4 14.7 %all_to_all.104 = bf16[32,8,640]{2,1,0:T(8,128)(2,1)S(1)} all-to-all(bf16[32,8,640]{2,1,0:T(8,128)(2,1)} %get-tuple-element.34), channel_id=1, replica_groups=mesh['pipe'=8,'expert'=32,'dp'=2] {'expert'}, dimensions={0} | all-to-all | bytes 655360 | tf_op jit(solution)/shard_map/all_to_all | solution.py:253
  304.1 4.4 copy-done.5
  308.5 2.3 expert.10
  310.8 14.6 %all_to_all.105 = bf16[32,8,640]{2,1,0:T(8,128)(2,1)} all-to-all(bf16[32,8,640]{2,1,0:T(8,128)(2,1)S(1)} %bitcast.83), channel_id=1, replica_groups=mesh['pipe'=8,'expert'=32,'dp'=2] {'expert'}, dimensions={0} | all-to-all | bytes 655360 | tf_op jit(solution)/shard_map/all_to_all | solution.py:253
  325.3 2.4 home.9
  327.7 14.9 %all_to_all.106 = bf16[32,8,640]{2,1,0:T(8,128)(2,1)S(1)} all-to-all(bf16[32,8,640]{2,1,0:T(8,128)(2,1)} %get-tuple-element.38), channel_id=1, replica_groups=mesh['pipe'=8,'expert'=32,'dp'=2] {'expert'}, dimensions={0} | all-to-all | bytes 655360 | tf_op jit(solution)/shard_map/all_to_all | solution.py:253
  342.6 4.3 copy-done.6
  347.0 2.3 expert.11
  349.3 14.8 %all_to_all.107 = bf16[32,8,640]{2,1,0:T(8,128)(2,1)} all-to-all(bf16[32,8,640]{2,1,0:T(8,128)(2,1)S(1)} %bitcast.84), channel_id=1, replica_groups=mesh['pipe'=8,'expert'=32,'dp'=2] {'expert'}, dimensions={0} | all-to-all | bytes 655360 | tf_op jit(solution)/shard_map/all_to_all | solution.py:253
  364.1 2.4 home.10
  366.5 15.8 %all_to_all.108 = bf16[32,8,640]{2,1,0:T(8,128)(2,1)S(1)} all-to-all(bf16[32,8,640]{2,1,0:T(8,128)(2,1)} %get-tuple-element.42), channel_id=1, replica_groups=mesh['pipe'=8,'expert'=32,'dp'=2] {'expert'}, dimensions={0} | all-to-all | bytes 655360 | tf_op jit(solution)/shard_map/all_to_all | solution.py:253
  382.3 4.3 copy-done.7
  386.6 2.3 expert.12
  388.9 14.9 %all_to_all.109 = bf16[32,8,640]{2,1,0:T(8,128)(2,1)} all-to-all(bf16[32,8,640]{2,1,0:T(8,128)(2,1)S(1)} %bitcast.82), channel_id=1, replica_groups=mesh['pipe'=8,'expert'=32,'dp'=2] {'expert'}, dimensions={0} | all-to-all | bytes 655360 | tf_op jit(solution)/shard_map/all_to_all | solution.py:253
  403.8 2.4 home.11
  406.2 4.1 all-to-all-start.14
  410.3 13.8 %all-to-all-done.14 = bf16[32,8,640]{2,1,0:T(8,128)(2,1)S(1)} async-done(((bf16[32,8,640]{2,1,0:T(8,128)(2,1)}), bf16[32,8,640]{2,1,0:T(8,128)(2,1)S(1)}, u32[]{:S(2)}, u32[]{:S(2)}) %all-to-all-start.14) | async-done | bytes 327712 | tf_op jit(solution)/shard_map/all_to_all | solution.py:253
  424.1 4.3 copy-done.2
  428.5 2.3 expert.13
  430.8 16.2 %all_to_all.110 = bf16[32,8,640]{2,1,0:T(8,128)(2,1)} all-to-all(bf16[32,8,640]{2,1,0:T(8,128)(2,1)S(1)} %bitcast.85), channel_id=1, replica_groups=mesh['pipe'=8,'expert'=32,'dp'=2] {'expert'}, dimensions={0} | all-to-all | bytes 655360 | tf_op jit(solution)/shard_map/all_to_all | solution.py:253
  447.0 2.4 home.12
  449.4 15.0 %all_to_all.111 = bf16[32,8,640]{2,1,0:T(8,128)(2,1)S(1)} all-to-all(bf16[32,8,640]{2,1,0:T(8,128)(2,1)} %get-tuple-element.50), channel_id=1, replica_groups=mesh['pipe'=8,'expert'=32,'dp'=2] {'expert'}, dimensions={0} | all-to-all | bytes 655360 | tf_op jit(solution)/shard_map/all_to_all | solution.py:253
  464.5 4.3 copy-done.3
  468.8 2.3 expert.14
  471.1 18.0 %all_to_all.112 = bf16[32,8,640]{2,1,0:T(8,128)(2,1)} all-to-all(bf16[32,8,640]{2,1,0:T(8,128)(2,1)S(1)} %bitcast.86), channel_id=1, replica_groups=mesh['pipe'=8,'expert'=32,'dp'=2] {'expert'}, dimensions={0} | all-to-all | bytes 655360 | tf_op jit(solution)/shard_map/all_to_all | solution.py:253
  489.1 2.4 home.13
  491.5 14.6 %all_to_all.113 = bf16[32,8,640]{2,1,0:T(8,128)(2,1)S(1)} all-to-all(bf16[32,8,640]{2,1,0:T(8,128)(2,1)} %get-tuple-element.54), channel_id=1, replica_groups=mesh['pipe'=8,'expert'=32,'dp'=2] {'expert'}, dimensions={0} | all-to-all | bytes 655360 | tf_op jit(solution)/shard_map/all_to_all | solution.py:253
  506.1 4.3 copy-done.4
  510.4 1.0 expert.15
  511.4 14.8 %all_to_all.114 = bf16[8,64,512]{2,1,0:T(8,128)(2,1)S(1)} all-to-all(bf16[8,64,512]{2,1,0:T(8,128)(2,1)S(1)} %expert.15), channel_id=1, replica_groups=mesh['pipe'=8,'expert'=32,'dp'=2] {'pipe'}, dimensions={0} | all-to-all | bytes 1048576 | tf_op jit(solution)/shard_map/all_to_all | solution.py:269
  527.2 27.8 %collective-permute-start.2 = (bf16[512,1280]{1,0:T(8,128)(2,1)S(1)}, bf16[512,1280]{1,0:T(8,128)(2,1)S(1)}, u32[]{:S(2)}, u32[]{:S(2)}) collective-permute-start(bf16[512,1280]{1,0:T(8,128)(2,1)S(1)} %convolution_convert_fusion.1), channel_id=1, source_target_pairs={{0,1},{1,0},{2,3},{3,2},{4,5},{5,4},{6,7},{7,6},{8,9},{9,8},{10,11... | collective-permute-start | bytes 3932168 | tf_op jit(solution)/shard_map/ppermute | solution.py:277
  555.0 2.6 collective-permute-done.2
  558.5 1.1 slice_bitcast_fusion.2
  (84 shorter events, 13.9 us)
Async XLA Ops:
  7.2 64.5 %copy-start = (bf16[1,1,128,2560]{3,2,1,0:T(8,128)(2,1)S(1)}, bf16[1,1,128,2560]{3,2,1,0:T(8,128)(2,1)}, u32[]{:S(2)}) copy-start(bf16[1,1,128,2560]{3,2,1,0:T(8,128)(2,1)} %param.6) | copy-start | bytes 1966084
  7.2 215.6 %all-gather.7.cloned.1.call-start = ((), (), s32[]{:S(2)}) async-start(), calls=%async_computation.20 | async-start | bytes 8355840 | tf_op jit(solution)/shard_map/all_gather | solution.py:225
  67.8 2.6 copy-start.19
  67.8 236.3 %all-gather.9.cloned.1.call-start = ((), (), s32[]{:S(2)}) async-start(), calls=%async_computation.21 | async-start | bytes 12533760 | tf_op jit(solution)/shard_map/all_gather | solution.py:225
  69.1 341.3 %all-gather.11.cloned.1.call-start = ((), (), s32[]{:S(2)}) async-start(), calls=%async_computation.22 | async-start | bytes 12533760 | tf_op jit(solution)/shard_map/all_gather | solution.py:225
  72.0 0.9 copy-start.18
  74.4 33.6 %all-to-all-start = ((bf16[8,64,768]{2,1,0:T(8,128)(2,1)}), bf16[8,64,768]{2,1,0:T(8,128)(2,1)S(1)}, u32[]{:S(2)}, u32[]{:S(2)}) async-start(bf16[8,64,768]{2,1,0:T(8,128)(2,1)} %maximum_maximum_fusion), calls=%async_computation | async-start | bytes 1572864 | tf_op jit(solution)/shard_map/all_to_all | solution.py:210
  108.0 3.9 copy-start.13
  111.9 9.9 %copy-start.15 = (bf16[1,1,256,1280]{3,2,1,0:T(8,128)(2,1)S(1)}, bf16[1,1,256,1280]{3,2,1,0:T(8,128)(2,1)}, u32[]{:S(2)}) copy-start(bf16[1,1,256,1280]{3,2,1,0:T(8,128)(2,1)} %param.9) | copy-start | bytes 1966084
  111.9 65.4 %all-to-all-start.3 = ((bf16[8,32,2,2560]{3,2,0,1:T(2,128)(2,1)}), bf16[8,32,2,2560]{3,2,0,1:T(2,128)(2,1)S(1)}, u32[]{:S(2)}, u32[]{:S(2)}) async-start(bf16[8,32,2,2560]{3,2,0,1:T(2,128)(2,1)} %bitcast.87), calls=%async_computation.3 | async-start | bytes 5242880 | tf_op jit(solution)/shard_map/all_to_all | solution.py:236
  121.8 79.8 %collective-permute-start.1 = (bf16[256,1280]{1,0:T(8,128)(2,1)S(1)}, bf16[256,1280]{1,0:T(8,128)(2,1)}, u32[]{:S(2)}, u32[]{:S(2)}) collective-permute-start(bf16[256,1280]{1,0:T(8,128)(2,1)S(1)} %bitcast.89), channel_id=1, source_target_pairs={{0,1},{1,0},{2,3},{3,2},{4,5},{5,4},{6,7},{7,6},{8,9},{9,8},{10,11... | collective-permute-start | bytes 1966088 | tf_op jit(solution)/shard_map/ppermute | solution.py:239
  126.9 77.9 %collective-permute-start = (bf16[256,1280]{1,0:T(8,128)(2,1)}, bf16[256,1280]{1,0:T(8,128)(2,1)}, u32[]{:S(2)}, u32[]{:S(2)}) collective-permute-start(bf16[256,1280]{1,0:T(8,128)(2,1)} %bitcast.91), channel_id=1, source_target_pairs={{0,1},{1,0},{2,3},{3,2},{4,5},{5,4},{6,7},{7,6},{8,9},{9,8},{10,11... | collective-permute-start | bytes 1966088 | tf_op jit(solution)/shard_map/ppermute | solution.py:240
  177.4 1.6 copy-start.10
  178.9 27.5 %all-to-all-start.1 = ((bf16[32,8,640]{2,1,0:T(8,128)(2,1)}), bf16[32,8,640]{2,1,0:T(8,128)(2,1)S(1)}, u32[]{:S(2)}, u32[]{:S(2)}) async-start(bf16[32,8,640]{2,1,0:T(8,128)(2,1)} %bitcast.99), calls=%async_computation.1 | async-start | bytes 655360 | tf_op jit(solution)/shard_map/all_to_all | solution.py:253
  201.6 2.5 copy-start.11
  201.6 2.6 copy-start.16
  222.8 3.2 copy-start.8
  226.1 12.6 %copy-start.14 = (bf16[8,64,768]{2,1,0:T(8,128)(2,1)S(1)}, bf16[8,64,768]{2,1,0:T(8,128)(2,1)}, u32[]{:S(2)}) copy-start(bf16[8,64,768]{2,1,0:T(8,128)(2,1)} %copy-done.13) | copy-start | bytes 2359300
  229.1 19.5 %all-to-all-start.5 = ((bf16[32,8,640]{2,1,0:T(8,128)(2,1)}), bf16[32,8,640]{2,1,0:T(8,128)(2,1)S(1)}, u32[]{:S(2)}, u32[]{:S(2)}) async-start(bf16[32,8,640]{2,1,0:T(8,128)(2,1)} %bitcast.16), calls=%async_computation.5 | async-start | bytes 655360 | tf_op jit(solution)/shard_map/all_to_all | solution.py:253
  248.6 0.7 copy-start.17
  266.6 3.4 copy-start.9
  304.1 4.4 copy-start.5
  342.6 4.4 copy-start.6
  382.3 4.4 copy-start.7
  406.2 17.9 %all-to-all-start.14 = ((bf16[32,8,640]{2,1,0:T(8,128)(2,1)}), bf16[32,8,640]{2,1,0:T(8,128)(2,1)S(1)}, u32[]{:S(2)}, u32[]{:S(2)}) async-start(bf16[32,8,640]{2,1,0:T(8,128)(2,1)} %get-tuple-element.46), calls=%async_computation.14 | async-start | bytes 655360 | tf_op jit(solution)/shard_map/all_to_all | solution.py:253
  424.1 4.4 copy-start.2
  464.5 4.4 copy-start.3
  506.0 4.4 copy-start.4
  510.4 15.9 %copy-start.12 = (bf16[512,2560]{1,0:T(8,128)(2,1)S(1)}, bf16[512,2560]{1,0:T(8,128)(2,1)}, u32[]{:S(2)}) copy-start(bf16[512,2560]{1,0:T(8,128)(2,1)} %reshape.168) | copy-start | bytes 7864324
  527.2 30.5 %collective-permute-start.2 = (bf16[512,1280]{1,0:T(8,128)(2,1)S(1)}, bf16[512,1280]{1,0:T(8,128)(2,1)S(1)}, u32[]{:S(2)}, u32[]{:S(2)}) collective-permute-start(bf16[512,1280]{1,0:T(8,128)(2,1)S(1)} %convolution_convert_fusion.1), channel_id=1, source_target_pairs={{0,1},{1,0},{2,3},{3,2},{4,5},{5,4},{6,7},{7,6},{8,9},{9,8},{10,11... | collective-permute-start | bytes 3932168 | tf_op jit(solution)/shard_map/ppermute | solution.py:277
  557.6 2.0 copy-start.1
Sparse Core Ops, SparseCore 0:
  67.9 69.6 all-gather.6
  139.7 74.1 all-gather.8
  216.0 73.3 all-gather.10

commit v3 on v2

--- a/solution.py
+++ b/solution.py
@@ -4,6 +4,7 @@
 from jax.experimental import pallas as pl
 from jax.experimental.pallas import tpu as pltpu
 from jax.sharding import PartitionSpec as P
+
 
 GROUP = 4
 MICRO = 8
@@ -100,7 +101,7 @@
         grid=(1,),
         in_specs=[
             whole,
-            pl.BlockSpec(memory_space=pl.ANY),
+            pl.BlockSpec(memory_space=pltpu.HBM),
             block,
             pl.BlockSpec(memory_space=pl.ANY),
         ],
@@ -112,12 +113,68 @@
             pltpu.SemaphoreType.DMA((3, 2)),
         ],
         input_output_aliases={3: 0},
-        compiler_params=pltpu.CompilerParams(vmem_limit_bytes=24 * 1024 * 1024),
         cost_estimate=pl.CostEstimate(
             flops=6 * rows_n * hidden * 2 * half, bytes_accessed=mats * 4 * hidden * half, transcendentals=0
         ),
         name="expert",
     )(rows, weights, fac, kept)
+
+
+def factor_call(units, pair):
+    width, micro, size, lanes = units.shape
+    cap = size // PARTS
+    rows_n = width * cap
+    _, _, hidden, half = pair.shape
+    per_half = half // lanes
+    blocks = lanes // 128
+    step = 4
+    n_in = step * width * size
+
+    def body(u_ref, w_ref, rows_ref, fac_ref, stage):
+        for m in range(step):
+            for b in range(blocks):
+                block = u_ref[:, m, :, b * 128 : (b + 1) * 128].astype(F32)
+                stage[b, m * width * size : (m + 1) * width * size] = block.reshape(width * size, 128)
+        gate = jnp.zeros((step * rows_n, hidden), F32)
+        up = jnp.zeros((step * rows_n, hidden), F32)
+        for k in range(PARTS):
+            part = jnp.concatenate(
+                [stage[b, pl.ds(k, step * rows_n, stride=PARTS), :] for b in range(blocks)], axis=1
+            ).astype(BF16)
+            rows_ref[:, k * lanes : (k + 1) * lanes] = part
+            c, j = k // per_half, k % per_half
+            gate = gate + dot_t(part, w_ref[0, c, :, j * lanes : (j + 1) * lanes])
+            up = up + dot_t(part, w_ref[1, c, :, j * lanes : (j + 1) * lanes])
+        sig = jax.nn.sigmoid(gate)
+        a = (up * sig * (1.0 + gate * (1.0 - sig))).astype(BF16)
+        b = (gate * sig).astype(BF16)
+        for m in range(step):
+            fac_ref[m, :, :hidden] = a[m * rows_n : (m + 1) * rows_n]
+            fac_ref[m, :, hidden:] = b[m * rows_n : (m + 1) * rows_n]
+
+    return pl.pallas_call(
+        body,
+        grid=(micro // step,),
+        in_specs=[
+            pl.BlockSpec((width, step, size, lanes), lambda i: (0, i, 0, 0)),
+            pl.BlockSpec((2, 2, hidden, half), lambda i: (0, 0, 0, 0)),
+        ],
+        out_specs=[
+            pl.BlockSpec((step * rows_n, PARTS * lanes), lambda i: (i, 0)),
+            pl.BlockSpec((step, rows_n, 2 * hidden), lambda i: (i, 0, 0)),
+        ],
+        out_shape=[
+            jax.ShapeDtypeStruct((micro * rows_n, PARTS * lanes), BF16),
+            jax.ShapeDtypeStruct((micro, rows_n, 2 * hidden), BF16),
+        ],
+        scratch_shapes=[pltpu.VMEM((blocks, n_in, 128), F32)],
+        cost_estimate=pl.CostEstimate(
+            flops=4 * micro * rows_n * hidden * 2 * half,
+            bytes_accessed=4 * micro * rows_n * 2 * half,
+            transcendentals=micro * rows_n * hidden,
+        ),
+        name="factors",
+    )(units, pair)
 
 
 def spread(send_ref, g, experts):
@@ -193,9 +250,36 @@
     slots = tok * PARTS
     size = cap * PARTS
 
+    z = lax.axis_index("pipe")
+
+    def to_planes(blocks):
+        got = blocks
+        for d in range(1, layers):
+            piece = lax.dynamic_index_in_dim(blocks, (z - d + layers) % layers, 0, keepdims=False)
+            piece = lax.ppermute(piece, "pipe", [((p + d) % layers, p) for p in range(layers)])
+            got = lax.dynamic_update_index_in_dim(got, piece, (z + d) % layers, 0)
+        return got
+
     place = placing_of(routes[0, 0, :, 0].reshape(MICRO, tok), experts, cap)
     x = saved[0, 0].reshape(MICRO, tok, feat)
     x_slot = jnp.einsum("mst,mtd->msd", place, x, preferred_element_type=F32)
+    scale = lax.rsqrt(jnp.mean(x_slot * x_slot, axis=2, keepdims=True) + EPS)
+    unit = (x_slot * scale).astype(BF16).reshape(MICRO, experts, size, lanes)
+    unit = jnp.transpose(unit, (1, 0, 2, 3))[:, None]
+    send = jnp.broadcast_to(unit, (experts, GROUP, MICRO, size, lanes)).reshape(width, MICRO, size, lanes)
+    units = lax.all_to_all(send, "expert", split_axis=0, concat_axis=0, tiled=True)
+
+    cut = jnp.stack([w_down[0, 0], w_gate[0, 0], w_up[0, 0]]).reshape(3, layers, hidden // layers, half)
+    cut = to_planes(jnp.transpose(cut, (1, 0, 2, 3)))
+    weights = {}
+    for members in SETS:
+        low = min(members)
+        mine = cut[low : low + len(members)]
+        got = lax.all_gather(mine, ("pipe", "dp"), axis=0).reshape(
+            layers, 2, len(members), 3, hidden // layers, half
+        )
+        for layer in members:
+            weights[layer] = (got, layer - low)
 
     thin = cotangent.shape[1] // PARTS
     extra = jnp.concatenate(
@@ -207,7 +291,7 @@
         axis=2,
     )
     pack = jnp.concatenate([x_slot.astype(BF16).reshape(MICRO, slots, lanes), extra], axis=2)
-    pack = lax.all_to_all(pack, "pipe", split_axis=0, concat_axis=0, tiled=True)
+    pack = to_planes(pack)
     x_all = pack[:, :, :lanes]
     place_all = pack[:, :, lanes : lanes + tok]
     grad = pack[:, :, lanes + tok : lanes + tok + thin].reshape(layers, tok, PARTS * thin)
@@ -217,36 +301,13 @@
     move = jnp.einsum("lat,lbt->lab", jnp.roll(place_all, 1, axis=0), place_all, preferred_element_type=F32)
     move = jnp.where(quarter[:, None] == quarter[None, :], move, 0.0).astype(BF16)
 
-    cut = jnp.stack([w_down[0, 0], w_gate[0, 0], w_up[0, 0]]).reshape(3, layers, hidden // layers, half)
-    cut = lax.all_to_all(cut, "pipe", split_axis=1, concat_axis=1, tiled=True)
-    weights = {}
-    for members in SETS:
-        low = min(members)
-        got = lax.all_gather(
-            jnp.transpose(cut[:, low : low + len(members)], (1, 0, 2, 3)), ("pipe", "dp"), axis=0
-        ).reshape(layers, 2, len(members), 3, hidden // layers, half)
-        for layer in members:
-            weights[layer] = (got, layer - low)
-
-    scale = lax.rsqrt(jnp.mean(x_slot * x_slot, axis=2, keepdims=True) + EPS)
-    unit = (x_slot * scale).astype(BF16)
-    send = jnp.broadcast_to(
-        unit.reshape(MICRO, experts, 1, cap, feat), (MICRO, experts, GROUP, cap, feat)
-    ).reshape(MICRO, width, cap, feat)
-    unit_rows = lax.all_to_all(send, "expert", split_axis=1, concat_axis=1, tiled=True)
-    unit_rows = unit_rows.reshape(MICRO * rows_n, feat)
     swap = [(0, 1), (1, 0)]
-    wg_other = lax.ppermute(w_gate[0, 0], "dp", swap)
-    wu_other = lax.ppermute(w_up[0, 0], "dp", swap)
-    own = lax.dynamic_slice_in_dim(unit_rows, dp_index * half, half, 1)
-    other = lax.dynamic_slice_in_dim(unit_rows, (1 - dp_index) * half, half, 1)
-    gate = dot_t(own, w_gate[0, 0]) + dot_t(other, wg_other)
-    up = dot_t(own, w_up[0, 0]) + dot_t(other, wu_other)
-    sig = jax.nn.sigmoid(gate)
-    fac = jnp.concatenate([up * sig * (1.0 + gate * (1.0 - sig)), gate * sig], axis=1).astype(BF16)
-    fac = lax.all_to_all(
-        fac.reshape(MICRO, rows_n, 2 * hidden), "pipe", split_axis=0, concat_axis=0, tiled=True
-    )
+    pair = jnp.stack([w_gate[0, 0], w_up[0, 0]])
+    pair_other = lax.ppermute(pair, "dp", swap)
+    first = dp_index == 0
+    pair = jnp.stack([jnp.where(first, pair, pair_other), jnp.where(first, pair_other, pair)], axis=1)
+    unit_rows, fac = factor_call(units, pair)
+    fac = lax.all_to_all(fac, "pipe", split_axis=0, concat_axis=0, tiled=True)
 
     def exchange(block):
         block = block.reshape(width, size, lanes)
@@ -274,6 +335,8 @@
             grads, rows, (((0,), (0,)), ((), ())), preferred_element_type=F32
         ).astype(BF16)
 
+    own = lax.dynamic_slice_in_dim(unit_rows, dp_index * half, half, 1)
+    other = lax.dynamic_slice_in_dim(unit_rows, (1 - dp_index) * half, half, 1)
     got = lax.ppermute(outer(other), "dp", swap)
     total = (outer(own).astype(F32) + got.astype(F32)).astype(BF16)
     return total[None, None, :hidden], total[None, None, hidden:]

time: 568 us -> 541 us (0.952)
  blocking collectives: 272 us -> 219 us
  starting transfers between devices: 70.2 us -> 112 us
  local copies, waits for them, and re-layouts: 62.2 us -> 27.1 us
  Pallas kernels: 34.6 us -> 58.8 us
  waiting for transfers between devices: 99.1 us -> 88.5 us
  other arithmetic: 4.27 us -> 9.98 us
    all_to_all x2, waiting for transfers between devices: 74 us -> 12.1 us  [the longest x1 12.1 us: shards(): lax.all_to_all(kept, 'pipe', split_axis=0, concat_axis=0, tiled=True)]
    all_to_all x3 -> x1, blocking collectives: 89.1 us -> 27.8 us  [shards(): fac = lax.all_to_all(fac, 'pipe', split_axis=0, concat_axis=0, tiled=True)]
    ppermute x2 -> x15, waiting for transfers between devices: 0.01 us -> 53.5 us  [the longest x14 53.5 us: to_planes(): lax.ppermute(piece, 'pipe', [((p + d) % layers, p) for p in range(layers)])]
    ppermute x2 -> x15, starting transfers between devices: 7 us -> 58.4 us  [the longest x14 54.6 us: to_planes(): lax.ppermute(piece, 'pipe', [((p + d) % layers, p) for p in range(layers)])]
    unnamed x42 -> x20, local copies, waits for them, and re-layouts: 35.4 us -> 2.14 us
    pallas_call x8, Pallas kernels: 17.7 us -> 36.5 us  [expert_call(): pl.pallas_call(body, grid=(1,), in_specs=[whole, pl.BlockSpec(memory_spac...]
    all_to_all x12, blocking collectives: 183 us -> 192 us  [exchange(): lax.all_to_all(block, 'expert', split_axis=0, concat_axis=0, tiled=True)]
    ppermute x1, starting transfers between devices: 27.8 us -> 21 us  [shards(): got = lax.ppermute(outer(other), 'dp', swap)]
  transfers between devices with their start and end apart: 11 -> 24, of which waited for: 5 -> 12; matrix products, arithmetic and copies ran while one was open for 6% -> 6% of each run, Pallas kernels for 4% -> 8%
where the time goes in v3:
time: 541 us; the launch traced here: 538 us
  blocking collectives  219 us (40%)
  starting transfers between devices  112 us (21%)
  waiting for transfers between devices  88.5 us (16%)
  Pallas kernels  58.8 us (11%)
  local copies, waits for them, and re-layouts  27.1 us (5%)
  between operations  14.4 us (3%)
  other arithmetic  9.98 us (2%)
  matrix products  7.9 us (1%)
    all_to_all x12, blocking collectives, exchange(): lax.all_to_all(block, 'expert', split_axis=0, concat_axis=0, tiled=True)  192 us
    ppermute x14, starting transfers between devices, to_planes(): lax.ppermute(piece, 'pipe', [((p + d) % layers, p) for p in range(layers)])  54.6 us
    ppermute x14, waiting for transfers between devices, to_planes(): lax.ppermute(piece, 'pipe', [((p + d) % layers, p) for p in range(layers)])  53.5 us
    pallas_call x8, Pallas kernels, expert_call(): pl.pallas_call(body, grid=(1,), in_specs=[whole, pl.BlockSpec(memory_spac...  36.5 us
    all_to_all x1, blocking collectives, shards(): fac = lax.all_to_all(fac, 'pipe', split_axis=0, concat_axis=0, tiled=True)  27.8 us
    ppermute x1, starting transfers between devices, shards(): got = lax.ppermute(outer(other), 'dp', swap)  21 us
    all_to_all x3, waiting for transfers between devices, exchange(): lax.all_to_all(block, 'expert', split_axis=0, concat_axis=0, tiled=True)  19.4 us
    all_to_all x3, starting transfers between devices, exchange(): lax.all_to_all(block, 'expert', split_axis=0, concat_axis=0, tiled=True)  19.1 us
  transfers between devices with their start and end apart: 24, of which 12 were waited for; matrix products, arithmetic and copies ran while one was open for 6% of the time, Pallas kernels for 8%

profile of v3, /device:TPU:1, one launch (start us, length us, event | category | flops | bytes accessed | tf_op | source)
XLA Modules:
  0.0 537.9 jit_solution(11760861532295006962)
XLA Ops:
  9.3 11.5 %collective-permute-start.7 = (bf16[3,32,1280]{2,1,0:T(8,128)(2,1)S(1)}, bf16[3,32,1280]{2,1,0:T(8,128)(2,1)S(1)}, u32[]{:S(2)}, u32[]{:S(2)}) collective-permute-start(bf16[3,32,1280]{2,1,0:T(8,128)(2,1)S(1)} %get-tuple-element.70), channel_id=1, source_target_pairs={{64,0},{128,64},{192,128},{256,192},{320,256},{384,320},{448,384},... | collective-permute-start | bytes 737288 | tf_op jit(solution)/shard_map/ppermute | solution.py:259
  20.7 2.2 collective-permute-start.8
  24.9 7.3 %collective-permute-start.10 = (bf16[3,32,1280]{2,1,0:T(8,128)(2,1)S(1)}, bf16[3,32,1280]{2,1,0:T(8,128)(2,1)S(1)}, u32[]{:S(2)}, u32[]{:S(2)}) collective-permute-start(bf16[3,32,1280]{2,1,0:T(8,128)(2,1)S(1)} %get-tuple-element.67), channel_id=1, source_target_pairs={{256,0},{320,64},{384,128},{448,192},{0,256},{64,320},{128,384},{1... | collective-permute-start | bytes 737288 | tf_op jit(solution)/shard_map/ppermute | solution.py:259
  34.1 3.1 collective-permute-start.12
  37.2 3.3 collective-permute-start.13
  40.6 21.5 %collective-permute-done.9 = bf16[3,32,1280]{2,1,0:T(8,128)(2,1)S(1)} collective-permute-done((bf16[3,32,1280]{2,1,0:T(8,128)(2,1)S(1)}, bf16[3,32,1280]{2,1,0:T(8,128)(2,1)S(1)}, u32[]{:S(2)}, u32[]{:S(2)}) %collective-permute-start.9) | collective-permute-done | bytes 245792 | tf_op jit(solution)/shard_map/ppermute | solution.py:259
  62.2 6.4 %collective-permute-done.12 = bf16[3,32,1280]{2,1,0:T(8,128)(2,1)S(1)} collective-permute-done((bf16[3,32,1280]{2,1,0:T(8,128)(2,1)S(1)}, bf16[3,32,1280]{2,1,0:T(8,128)(2,1)S(1)}, u32[]{:S(2)}, u32[]{:S(2)}) %collective-permute-start.12) | collective-permute-done | bytes 245792 | tf_op jit(solution)/shard_map/ppermute | solution.py:259
  68.6 7.1 %collective-permute-done.13 = bf16[3,32,1280]{2,1,0:T(8,128)(2,1)S(1)} collective-permute-done((bf16[3,32,1280]{2,1,0:T(8,128)(2,1)S(1)}, bf16[3,32,1280]{2,1,0:T(8,128)(2,1)S(1)}, u32[]{:S(2)}, u32[]{:S(2)}) %collective-permute-start.13) | collective-permute-done | bytes 245792 | tf_op jit(solution)/shard_map/ppermute | solution.py:259
  83.5 9.7 %all-to-all-start.1 = ((bf16[32,8,8,640]{3,2,1,0:T(8,128)(2,1)}), bf16[32,8,8,640]{3,2,1,0:T(8,128)(2,1)S(1)}, u32[]{:S(2)}, u32[]{:S(2)}) async-start(bf16[32,8,8,640]{3,2,1,0:T(8,128)(2,1)} %bitcast.124), calls=%async_computation.1 | async-start | bytes 5242880 | tf_op jit(solution)/shard_map/all_to_all | solution.py:270
  94.8 2.2 maximum_maximum_fusion
  98.0 2.1 collective-permute-start
  100.1 6.3 %collective-permute-done = bf16[64,768]{1,0:T(8,128)(2,1)S(1)} collective-permute-done((bf16[64,768]{1,0:T(8,128)(2,1)S(1)}, bf16[64,768]{1,0:T(8,128)(2,1)S(1)}, u32[]{:S(2)}, u32[]{:S(2)}) %collective-permute-start) | collective-permute-done | bytes 98336 | tf_op jit(solution)/shard_map/ppermute | solution.py:259
  106.4 1.9 dynamic-slice_bitcast_fusion.7
  108.3 2.1 collective-permute-start.1
  111.6 3.8 collective-permute-start.14
  115.4 5.0 collective-permute-start.2
  120.4 5.4 %collective-permute-start.3 = (bf16[64,768]{1,0:T(8,128)(2,1)}, bf16[64,768]{1,0:T(8,128)(2,1)S(1)}, u32[]{:S(2)}, u32[]{:S(2)}) collective-permute-start(bf16[64,768]{1,0:T(8,128)(2,1)} %get-tuple-element.80), channel_id=1, source_target_pairs={{256,0},{320,64},{384,128},{448,192},{0,256},{64,320},{128,384},{1... | collective-permute-start | bytes 294920 | tf_op jit(solution)/shard_map/ppermute | solution.py:259
  125.8 3.6 collective-permute-start.4
  132.9 3.2 collective-permute-start.6
  137.5 4.8 collective-permute-done.4
  143.0 2.5 collective-permute-done.5
  146.1 4.9 collective-permute-done.6
  156.3 9.4 %all-to-all-start = ((bf16[32,8,640]{2,1,0:T(8,128)(2,1)}), bf16[32,8,640]{2,1,0:T(8,128)(2,1)}, u32[]{:S(2)}, u32[]{:S(2)}) async-start(bf16[32,8,640]{2,1,0:T(8,128)(2,1)} %bitcast.145), calls=%async_computation | async-start | bytes 655360 | tf_op jit(solution)/shard_map/all_to_all | solution.py:314
  169.1 5.4 factors.1
  174.5 3.9 all-to-all-done
  178.4 27.8 %all_to_all.90.fac_ref = bf16[8,64,512]{2,1,0:T(8,128)(2,1)} all-to-all(bf16[8,64,512]{2,1,0:T(8,128)(2,1)} %get-tuple-element.31), channel_id=1, replica_groups=mesh['pipe'=8,'expert'=32,'dp'=2] {'pipe'}, dimensions={0} | all-to-all | bytes 1048576 | tf_op jit(solution)/shard_map/all_to_all | solution.py:310
  207.0 4.7 expert.8
  211.7 5.8 %all-to-all-start.3 = ((bf16[32,8,640]{2,1,0:T(8,128)(2,1)}), bf16[32,8,640]{2,1,0:T(8,128)(2,1)S(1)}, u32[]{:S(2)}, u32[]{:S(2)}) async-start(bf16[32,8,640]{2,1,0:T(8,128)(2,1)} %bitcast.152), calls=%async_computation.3 | async-start | bytes 655360 | tf_op jit(solution)/shard_map/all_to_all | solution.py:314
  220.0 2.0 slice.51.x_ref
  223.9 4.4 all-to-all-done.3
  229.1 2.4 home.7
  231.5 16.2 %all_to_all.91 = bf16[32,8,640]{2,1,0:T(8,128)(2,1)} all-to-all(bf16[32,8,640]{2,1,0:T(8,128)(2,1)} %get-tuple-element.33), channel_id=1, replica_groups=mesh['pipe'=8,'expert'=32,'dp'=2] {'expert'}, dimensions={0} | all-to-all | bytes 655360 | tf_op jit(solution)/shard_map/all_to_all | solution.py:314
  247.6 4.7 expert.9
  252.3 15.9 %all_to_all.92 = bf16[32,8,640]{2,1,0:T(8,128)(2,1)} all-to-all(bf16[32,8,640]{2,1,0:T(8,128)(2,1)} %bitcast.153), channel_id=1, replica_groups=mesh['pipe'=8,'expert'=32,'dp'=2] {'expert'}, dimensions={0} | all-to-all | bytes 655360 | tf_op jit(solution)/shard_map/all_to_all | solution.py:314
  268.2 2.4 home.8
  270.7 15.7 %all_to_all.93 = bf16[32,8,640]{2,1,0:T(8,128)(2,1)} all-to-all(bf16[32,8,640]{2,1,0:T(8,128)(2,1)} %get-tuple-element.37), channel_id=1, replica_groups=mesh['pipe'=8,'expert'=32,'dp'=2] {'expert'}, dimensions={0} | all-to-all | bytes 655360 | tf_op jit(solution)/shard_map/all_to_all | solution.py:314
  286.4 4.7 expert.10
  291.1 15.8 %all_to_all.94 = bf16[32,8,640]{2,1,0:T(8,128)(2,1)} all-to-all(bf16[32,8,640]{2,1,0:T(8,128)(2,1)} %bitcast.155), channel_id=1, replica_groups=mesh['pipe'=8,'expert'=32,'dp'=2] {'expert'}, dimensions={0} | all-to-all | bytes 655360 | tf_op jit(solution)/shard_map/all_to_all | solution.py:314
  306.9 2.5 home.9
  309.3 15.7 %all_to_all.95 = bf16[32,8,640]{2,1,0:T(8,128)(2,1)} all-to-all(bf16[32,8,640]{2,1,0:T(8,128)(2,1)} %get-tuple-element.41), channel_id=1, replica_groups=mesh['pipe'=8,'expert'=32,'dp'=2] {'expert'}, dimensions={0} | all-to-all | bytes 655360 | tf_op jit(solution)/shard_map/all_to_all | solution.py:314
  325.1 4.7 expert.11
  329.8 15.7 %all_to_all.96 = bf16[32,8,640]{2,1,0:T(8,128)(2,1)} all-to-all(bf16[32,8,640]{2,1,0:T(8,128)(2,1)} %bitcast.156), channel_id=1, replica_groups=mesh['pipe'=8,'expert'=32,'dp'=2] {'expert'}, dimensions={0} | all-to-all | bytes 655360 | tf_op jit(solution)/shard_map/all_to_all | solution.py:314
  345.5 2.4 home.10
  347.9 15.7 %all_to_all.97 = bf16[32,8,640]{2,1,0:T(8,128)(2,1)} all-to-all(bf16[32,8,640]{2,1,0:T(8,128)(2,1)} %get-tuple-element.45), channel_id=1, replica_groups=mesh['pipe'=8,'expert'=32,'dp'=2] {'expert'}, dimensions={0} | all-to-all | bytes 655360 | tf_op jit(solution)/shard_map/all_to_all | solution.py:314
  363.7 4.7 expert.12
  368.4 15.7 %all_to_all.98 = bf16[32,8,640]{2,1,0:T(8,128)(2,1)} all-to-all(bf16[32,8,640]{2,1,0:T(8,128)(2,1)} %bitcast.154), channel_id=1, replica_groups=mesh['pipe'=8,'expert'=32,'dp'=2] {'expert'}, dimensions={0} | all-to-all | bytes 655360 | tf_op jit(solution)/shard_map/all_to_all | solution.py:314
  384.1 2.4 home.11
  386.5 3.9 all-to-all-start.12
  390.4 11.0 %all-to-all-done.12 = bf16[32,8,640]{2,1,0:T(8,128)(2,1)S(1)} async-done(((bf16[32,8,640]{2,1,0:T(8,128)(2,1)}), bf16[32,8,640]{2,1,0:T(8,128)(2,1)S(1)}, u32[]{:S(2)}, u32[]{:S(2)}) %all-to-all-start.12) | async-done | bytes 327712 | tf_op jit(solution)/shard_map/all_to_all | solution.py:314
  402.2 4.7 expert.13
  406.9 15.7 %all_to_all.99 = bf16[32,8,640]{2,1,0:T(8,128)(2,1)} all-to-all(bf16[32,8,640]{2,1,0:T(8,128)(2,1)} %bitcast.157), channel_id=1, replica_groups=mesh['pipe'=8,'expert'=32,'dp'=2] {'expert'}, dimensions={0} | all-to-all | bytes 655360 | tf_op jit(solution)/shard_map/all_to_all | solution.py:314
  422.7 2.4 home.12
  425.1 16.0 %all_to_all.100 = bf16[32,8,640]{2,1,0:T(8,128)(2,1)} all-to-all(bf16[32,8,640]{2,1,0:T(8,128)(2,1)} %get-tuple-element.53), channel_id=1, replica_groups=mesh['pipe'=8,'expert'=32,'dp'=2] {'expert'}, dimensions={0} | all-to-all | bytes 655360 | tf_op jit(solution)/shard_map/all_to_all | solution.py:314
  441.1 4.7 expert.14
  445.9 15.6 %all_to_all.101 = bf16[32,8,640]{2,1,0:T(8,128)(2,1)} all-to-all(bf16[32,8,640]{2,1,0:T(8,128)(2,1)} %bitcast.158), channel_id=1, replica_groups=mesh['pipe'=8,'expert'=32,'dp'=2] {'expert'}, dimensions={0} | all-to-all | bytes 655360 | tf_op jit(solution)/shard_map/all_to_all | solution.py:314
  461.5 2.4 home.13
  463.9 17.7 %all_to_all.102 = bf16[32,8,640]{2,1,0:T(8,128)(2,1)} all-to-all(bf16[32,8,640]{2,1,0:T(8,128)(2,1)} %get-tuple-element.57), channel_id=1, replica_groups=mesh['pipe'=8,'expert'=32,'dp'=2] {'expert'}, dimensions={0} | all-to-all | bytes 655360 | tf_op jit(solution)/shard_map/all_to_all | solution.py:314
  481.7 3.6 expert.15
  485.2 3.5 all-to-all-start.17
  488.8 12.1 %all-to-all-done.17 = bf16[8,64,512]{2,1,0:T(8,128)(2,1)S(1)} async-done(((bf16[8,64,512]{2,1,0:T(8,128)(2,1)}), bf16[8,64,512]{2,1,0:T(8,128)(2,1)S(1)}, u32[]{:S(2)}, u32[]{:S(2)}) %all-to-all-start.17) | async-done | bytes 524320 | tf_op jit(solution)/shard_map/all_to_all | solution.py:330
  500.8 3.3 convolution_convert_fusion.1
  504.1 21.0 %collective-permute-start.15 = (bf16[512,1280]{1,0:T(8,128)(2,1)}, bf16[512,1280]{1,0:T(8,128)(2,1)S(1)}, u32[]{:S(2)}, u32[]{:S(2)}) collective-permute-start(bf16[512,1280]{1,0:T(8,128)(2,1)} %convolution_convert_fusion.1), channel_id=1, source_target_pairs={{0,1},{1,0},{2,3},{3,2},{4,5},{5,4},{6,7},{7,6},{8,9},{9,8},{10,11... | collective-permute-start | bytes 3932168 | tf_op jit(solution)/shard_map/ppermute | solution.py:340
  525.1 2.8 collective-permute-done.15
  528.0 2.3 add_convert_fusion
  (99 shorter events, 39.9 us)
Async XLA Ops:
  7.2 73.4 %copy-start = (bf16[1,1,128,2560]{3,2,1,0:T(8,128)(2,1)S(1)}, bf16[1,1,128,2560]{3,2,1,0:T(8,128)(2,1)}, u32[]{:S(2)}) copy-start(bf16[1,1,128,2560]{3,2,1,0:T(8,128)(2,1)} %param.6) | copy-start | bytes 1966084
  7.2 199.0 %all-gather.7.cloned.1.call-start = ((), (), s32[]{:S(2)}) async-start(), calls=%async_computation.18 | async-start | bytes 8355840 | tf_op jit(solution)/shard_map/all_gather | solution.py:278
  9.3 24.8 %collective-permute-start.7 = (bf16[3,32,1280]{2,1,0:T(8,128)(2,1)S(1)}, bf16[3,32,1280]{2,1,0:T(8,128)(2,1)S(1)}, u32[]{:S(2)}, u32[]{:S(2)}) collective-permute-start(bf16[3,32,1280]{2,1,0:T(8,128)(2,1)S(1)} %get-tuple-element.70), channel_id=1, source_target_pairs={{64,0},{128,64},{192,128},{256,192},{320,256},{384,320},{448,384},... | collective-permute-start | bytes 737288 | tf_op jit(solution)/shard_map/ppermute | solution.py:259
  20.7 16.5 %collective-permute-start.8 = (bf16[3,32,1280]{2,1,0:T(8,128)(2,1)S(1)}, bf16[3,32,1280]{2,1,0:T(8,128)(2,1)S(1)}, u32[]{:S(2)}, u32[]{:S(2)}) collective-permute-start(bf16[3,32,1280]{2,1,0:T(8,128)(2,1)S(1)} %get-tuple-element.69), channel_id=1, source_target_pairs={{128,0},{192,64},{256,128},{320,192},{384,256},{448,320},{0,384},{... | collective-permute-start | bytes 737288 | tf_op jit(solution)/shard_map/ppermute | solution.py:259
  22.9 39.2 %collective-permute-start.9 = (bf16[3,32,1280]{2,1,0:T(8,128)(2,1)S(1)}, bf16[3,32,1280]{2,1,0:T(8,128)(2,1)S(1)}, u32[]{:S(2)}, u32[]{:S(2)}) collective-permute-start(bf16[3,32,1280]{2,1,0:T(8,128)(2,1)S(1)} %get-tuple-element.68), channel_id=1, source_target_pairs={{192,0},{256,64},{320,128},{384,192},{448,256},{0,320},{64,384},{1... | collective-permute-start | bytes 737288 | tf_op jit(solution)/shard_map/ppermute | solution.py:259
  24.9 37.3 %collective-permute-start.10 = (bf16[3,32,1280]{2,1,0:T(8,128)(2,1)S(1)}, bf16[3,32,1280]{2,1,0:T(8,128)(2,1)S(1)}, u32[]{:S(2)}, u32[]{:S(2)}) collective-permute-start(bf16[3,32,1280]{2,1,0:T(8,128)(2,1)S(1)} %get-tuple-element.67), channel_id=1, source_target_pairs={{256,0},{320,64},{384,128},{448,192},{0,256},{64,320},{128,384},{1... | collective-permute-start | bytes 737288 | tf_op jit(solution)/shard_map/ppermute | solution.py:259
  32.1 30.1 %collective-permute-start.11 = (bf16[3,32,1280]{2,1,0:T(8,128)(2,1)S(1)}, bf16[3,32,1280]{2,1,0:T(8,128)(2,1)S(1)}, u32[]{:S(2)}, u32[]{:S(2)}) collective-permute-start(bf16[3,32,1280]{2,1,0:T(8,128)(2,1)S(1)} %get-tuple-element.66), channel_id=1, source_target_pairs={{320,0},{384,64},{448,128},{0,192},{64,256},{128,320},{192,384},{2... | collective-permute-start | bytes 737288 | tf_op jit(solution)/shard_map/ppermute | solution.py:259
  34.1 34.5 %collective-permute-start.12 = (bf16[3,32,1280]{2,1,0:T(8,128)(2,1)S(1)}, bf16[3,32,1280]{2,1,0:T(8,128)(2,1)S(1)}, u32[]{:S(2)}, u32[]{:S(2)}) collective-permute-start(bf16[3,32,1280]{2,1,0:T(8,128)(2,1)S(1)} %get-tuple-element.65), channel_id=1, source_target_pairs={{384,0},{448,64},{0,128},{64,192},{128,256},{192,320},{256,384},{3... | collective-permute-start | bytes 737288 | tf_op jit(solution)/shard_map/ppermute | solution.py:259
  37.2 38.5 %collective-permute-start.13 = (bf16[3,32,1280]{2,1,0:T(8,128)(2,1)S(1)}, bf16[3,32,1280]{2,1,0:T(8,128)(2,1)S(1)}, u32[]{:S(2)}, u32[]{:S(2)}) collective-permute-start(bf16[3,32,1280]{2,1,0:T(8,128)(2,1)S(1)} %get-tuple-element.64), channel_id=1, source_target_pairs={{448,0},{0,64},{64,128},{128,192},{192,256},{256,320},{320,384},{3... | collective-permute-start | bytes 737288 | tf_op jit(solution)/shard_map/ppermute | solution.py:259
  76.6 2.6 copy-start.8
  76.6 209.8 %all-gather.9.cloned.1.call-start = ((), (), s32[]{:S(2)}) async-start(), calls=%async_computation.19 | async-start | bytes 12533760 | tf_op jit(solution)/shard_map/all_gather | solution.py:278
  78.0 312.5 %all-gather.11.cloned.1.call-start = ((), (), s32[]{:S(2)}) async-start(), calls=%async_computation.20 | async-start | bytes 12533760 | tf_op jit(solution)/shard_map/all_gather | solution.py:278
  83.5 11.0 %copy-start.7 = (bf16[128,320]{0,1:T(8,128)(2,1)S(1)}, bf16[128,320]{0,1:T(8,128)(2,1)}, u32[]{:S(2)}) copy-start(bf16[128,320]{0,1:T(8,128)(2,1)} %param.7) | copy-start | bytes 245764
  83.5 72.0 %all-to-all-start.1 = ((bf16[32,8,8,640]{3,2,1,0:T(8,128)(2,1)}), bf16[32,8,8,640]{3,2,1,0:T(8,128)(2,1)S(1)}, u32[]{:S(2)}, u32[]{:S(2)}) async-start(bf16[32,8,8,640]{3,2,1,0:T(8,128)(2,1)} %bitcast.124), calls=%async_computation.1 | async-start | bytes 5242880 | tf_op jit(solution)/shard_map/all_to_all | solution.py:270
  94.4 16.0 %copy-start.3 = (bf16[1,1,256,1280]{3,2,1,0:T(8,128)(2,1)S(1)}, bf16[1,1,256,1280]{3,2,1,0:T(8,128)(2,1)}, u32[]{:S(2)}) copy-start(bf16[1,1,256,1280]{3,2,1,0:T(8,128)(2,1)} %param.10) | copy-start | bytes 1966084
  94.7 15.7 %copy-start.4 = (bf16[1,1,256,1280]{3,2,1,0:T(8,128)(2,1)S(1)}, bf16[1,1,256,1280]{3,2,1,0:T(8,128)(2,1)}, u32[]{:S(2)}) copy-start(bf16[1,1,256,1280]{3,2,1,0:T(8,128)(2,1)} %param.9) | copy-start | bytes 1966084
  98.0 8.4 %collective-permute-start = (bf16[64,768]{1,0:T(8,128)(2,1)S(1)}, bf16[64,768]{1,0:T(8,128)(2,1)S(1)}, u32[]{:S(2)}, u32[]{:S(2)}) collective-permute-start(bf16[64,768]{1,0:T(8,128)(2,1)S(1)} %dynamic-slice_bitcast_fusion.13), channel_id=1, source_target_pairs={{64,0},{128,64},{192,128},{256,192},{320,256},{384,320},{448,384},... | collective-permute-start | bytes 294920 | tf_op jit(solution)/shard_map/ppermute | solution.py:259
  108.3 21.1 %collective-permute-start.1 = (bf16[64,768]{1,0:T(8,128)(2,1)}, bf16[64,768]{1,0:T(8,128)(2,1)}, u32[]{:S(2)}, u32[]{:S(2)}) collective-permute-start(bf16[64,768]{1,0:T(8,128)(2,1)} %get-tuple-element.82), channel_id=1, source_target_pairs={{128,0},{192,64},{256,128},{320,192},{384,256},{448,320},{0,384},{... | collective-permute-start | bytes 294920 | tf_op jit(solution)/shard_map/ppermute | solution.py:259
  111.6 54.1 %collective-permute-start.14 = (bf16[2,256,1280]{2,1,0:T(8,128)(2,1)}, bf16[2,256,1280]{2,1,0:T(8,128)(2,1)}, u32[]{:S(2)}, u32[]{:S(2)}) collective-permute-start(bf16[2,256,1280]{2,1,0:T(8,128)(2,1)} %pad_maximum_fusion.2), channel_id=1, source_target_pairs={{0,1},{1,0},{2,3},{3,2},{4,5},{5,4},{6,7},{7,6},{8,9},{9,8},{10,11... | collective-permute-start | bytes 3932168 | tf_op jit(solution)/shard_map/ppermute | solution.py:306
  115.4 17.6 %collective-permute-start.2 = (bf16[64,768]{1,0:T(8,128)(2,1)}, bf16[64,768]{1,0:T(8,128)(2,1)S(1)}, u32[]{:S(2)}, u32[]{:S(2)}) collective-permute-start(bf16[64,768]{1,0:T(8,128)(2,1)} %get-tuple-element.81), channel_id=1, source_target_pairs={{192,0},{256,64},{320,128},{384,192},{448,256},{0,320},{64,384},{1... | collective-permute-start | bytes 294920 | tf_op jit(solution)/shard_map/ppermute | solution.py:259
  120.4 16.4 %collective-permute-start.3 = (bf16[64,768]{1,0:T(8,128)(2,1)}, bf16[64,768]{1,0:T(8,128)(2,1)S(1)}, u32[]{:S(2)}, u32[]{:S(2)}) collective-permute-start(bf16[64,768]{1,0:T(8,128)(2,1)} %get-tuple-element.80), channel_id=1, source_target_pairs={{256,0},{320,64},{384,128},{448,192},{0,256},{64,320},{128,384},{1... | collective-permute-start | bytes 294920 | tf_op jit(solution)/shard_map/ppermute | solution.py:259
  125.8 16.5 %collective-permute-start.4 = (bf16[64,768]{1,0:T(8,128)(2,1)}, bf16[64,768]{1,0:T(8,128)(2,1)S(1)}, u32[]{:S(2)}, u32[]{:S(2)}) collective-permute-start(bf16[64,768]{1,0:T(8,128)(2,1)} %get-tuple-element.79), channel_id=1, source_target_pairs={{320,0},{384,64},{448,128},{0,192},{64,256},{128,320},{192,384},{2... | collective-permute-start | bytes 294920 | tf_op jit(solution)/shard_map/ppermute | solution.py:259
  129.5 16.0 %collective-permute-start.5 = (bf16[64,768]{1,0:T(8,128)(2,1)S(1)}, bf16[64,768]{1,0:T(8,128)(2,1)S(1)}, u32[]{:S(2)}, u32[]{:S(2)}) collective-permute-start(bf16[64,768]{1,0:T(8,128)(2,1)S(1)} %get-tuple-element.78), channel_id=1, source_target_pairs={{384,0},{448,64},{0,128},{64,192},{128,256},{192,320},{256,384},{3... | collective-permute-start | bytes 294920 | tf_op jit(solution)/shard_map/ppermute | solution.py:259
  132.9 18.0 %collective-permute-start.6 = (bf16[64,768]{1,0:T(8,128)(2,1)S(1)}, bf16[64,768]{1,0:T(8,128)(2,1)S(1)}, u32[]{:S(2)}, u32[]{:S(2)}) collective-permute-start(bf16[64,768]{1,0:T(8,128)(2,1)S(1)} %get-tuple-element.77), channel_id=1, source_target_pairs={{448,0},{0,64},{64,128},{128,192},{192,256},{256,320},{320,384},{3... | collective-permute-start | bytes 294920 | tf_op jit(solution)/shard_map/ppermute | solution.py:259
  155.4 11.9 %copy-start.2 = (bf16[32,8,8,640]{3,2,1,0:T(8,128)(2,1)}, bf16[32,8,8,640]{3,2,1,0:T(8,128)(2,1)S(1)}, u32[]{:S(2)}) copy-start(bf16[32,8,8,640]{3,2,1,0:T(8,128)(2,1)S(1)} %all-to-all-done.1.u_ref) | copy-start | bytes 7864324
  156.3 22.1 %all-to-all-start = ((bf16[32,8,640]{2,1,0:T(8,128)(2,1)}), bf16[32,8,640]{2,1,0:T(8,128)(2,1)}, u32[]{:S(2)}, u32[]{:S(2)}) async-start(bf16[32,8,640]{2,1,0:T(8,128)(2,1)} %bitcast.145), calls=%async_computation | async-start | bytes 655360 | tf_op jit(solution)/shard_map/all_to_all | solution.py:314
  211.7 16.6 %all-to-all-start.3 = ((bf16[32,8,640]{2,1,0:T(8,128)(2,1)}), bf16[32,8,640]{2,1,0:T(8,128)(2,1)S(1)}, u32[]{:S(2)}, u32[]{:S(2)}) async-start(bf16[32,8,640]{2,1,0:T(8,128)(2,1)} %bitcast.152), calls=%async_computation.3 | async-start | bytes 655360 | tf_op jit(solution)/shard_map/all_to_all | solution.py:314
  228.3 0.7 copy-start.6
  386.5 15.0 %all-to-all-start.12 = ((bf16[32,8,640]{2,1,0:T(8,128)(2,1)}), bf16[32,8,640]{2,1,0:T(8,128)(2,1)S(1)}, u32[]{:S(2)}, u32[]{:S(2)}) async-start(bf16[32,8,640]{2,1,0:T(8,128)(2,1)} %get-tuple-element.49), calls=%async_computation.12 | async-start | bytes 655360 | tf_op jit(solution)/shard_map/all_to_all | solution.py:314
  401.5 0.7 copy-start.5
  485.2 15.6 %all-to-all-start.17 = ((bf16[8,64,512]{2,1,0:T(8,128)(2,1)}), bf16[8,64,512]{2,1,0:T(8,128)(2,1)S(1)}, u32[]{:S(2)}, u32[]{:S(2)}) async-start(bf16[8,64,512]{2,1,0:T(8,128)(2,1)} %expert.15), calls=%async_computation.17 | async-start | bytes 1048576 | tf_op jit(solution)/shard_map/all_to_all | solution.py:330
  504.1 23.8 %collective-permute-start.15 = (bf16[512,1280]{1,0:T(8,128)(2,1)}, bf16[512,1280]{1,0:T(8,128)(2,1)S(1)}, u32[]{:S(2)}, u32[]{:S(2)}) collective-permute-start(bf16[512,1280]{1,0:T(8,128)(2,1)} %convolution_convert_fusion.1), channel_id=1, source_target_pairs={{0,1},{1,0},{2,3},{3,2},{4,5},{5,4},{6,7},{7,6},{8,9},{9,8},{10,11... | collective-permute-start | bytes 3932168 | tf_op jit(solution)/shard_map/ppermute | solution.py:340
  528.0 3.4 copy-start.1
Sparse Core Ops, SparseCore 0:
  76.7 76.1 all-gather.6
  155.0 86.0 all-gather.8
  243.3 73.3 all-gather.10

commit v4 on v3

--- a/solution.py
+++ b/solution.py
@@ -12,6 +12,7 @@
 EPS = 1e-06
 F32 = jnp.float32
 BF16 = jnp.bfloat16
+LIMIT = 48 * 1024 * 1024
 SETS = ((7, 6), (5, 4, 3), (2, 1, 0))
 
 
@@ -31,37 +32,45 @@
     return (slot_ids[:, None, :] == positions).astype(BF16)
 
 
+def load(src, where, dst, sem):
+    return [
+        [pltpu.make_async_copy(src.at[:, c, where, m], dst.at[m, c], sem.at[m, c]) for c in range(2)]
+        for m in range(dst.shape[0])
+    ]
+
+
 def expert_call(layer, where, last, rows, weights, fac, kept):
     n_in, lanes = rows.shape
     rows_n = n_in // PARTS
-    chunks, _, _, _, rows_c, half = weights.shape
+    loaded = where is None
+    if loaded:
+        _, _, chunks, rows_c, half = weights.shape
+    else:
+        chunks, _, _, _, rows_c, half = weights.shape
     hidden = chunks * rows_c
     per_half = half // lanes
     mats = 1 if last else 3
 
     def body(rows_ref, w_ref, fac_ref, _, *refs):
-        kept_ref = refs[0]
-        outs = refs[1:]
-        if last:
-            w_vm, stage, sem = outs
+        refs = list(refs)
+        kept_ref = refs.pop(0)
+        out_ref = None if last else refs.pop(0)
+        stage = refs.pop(0)
+        if loaded:
+            w_vm = w_ref
         else:
-            out_ref, w_vm, stage, sem = outs
-        copies = [
-            [
-                pltpu.make_async_copy(w_ref.at[:, c, where, m], w_vm.at[m, c], sem.at[m, c])
-                for c in range(2)
-            ]
-            for m in range(mats)
-        ]
-        for pair in copies:
-            for copy in pair:
-                copy.start()
+            w_vm, sem = refs
+            copies = load(w_ref, where, w_vm, sem)
+            for pair in copies:
+                for copy in pair:
+                    copy.start()
         blocks = lanes // 128
         for b in range(blocks):
             stage[b] = rows_ref[:, b * 128 : (b + 1) * 128].astype(F32)
         hidden_grad = jnp.zeros((rows_n, hidden), F32)
         for c in range(2):
-            copies[0][c].wait()
+            if not loaded:
+                copies[0][c].wait()
             for j in range(per_half):
                 k = c * per_half + j
                 part = jnp.concatenate(
@@ -77,8 +86,9 @@
         if last:
             return
         for c in range(2):
-            copies[1][c].wait()
-            copies[2][c].wait()
+            if not loaded:
+                copies[1][c].wait()
+                copies[2][c].wait()
             for j in range(per_half):
                 k = c * per_half + j
                 g = w_vm[1, c, :, :, j * lanes : (j + 1) * lanes].reshape(hidden, lanes)
@@ -101,18 +111,20 @@
         grid=(1,),
         in_specs=[
             whole,
-            pl.BlockSpec(memory_space=pltpu.HBM),
+            pl.BlockSpec(memory_space=pltpu.VMEM if loaded else pltpu.HBM),
             block,
             pl.BlockSpec(memory_space=pl.ANY),
         ],
         out_specs=out_specs,
         out_shape=out_shape,
-        scratch_shapes=[
-            pltpu.VMEM((mats, 2, chunks, rows_c, half), BF16),
-            pltpu.VMEM((lanes // 128, n_in, 128), F32),
-            pltpu.SemaphoreType.DMA((3, 2)),
-        ],
+        scratch_shapes=[pltpu.VMEM((lanes // 128, n_in, 128), F32)]
+        + (
+            []
+            if loaded
+            else [pltpu.VMEM((mats, 2, chunks, rows_c, half), BF16), pltpu.SemaphoreType.DMA((mats, 2))]
+        ),
         input_output_aliases={3: 0},
+        compiler_params=pltpu.CompilerParams(vmem_limit_bytes=LIMIT),
         cost_estimate=pl.CostEstimate(
             flops=6 * rows_n * hidden * 2 * half, bytes_accessed=mats * 4 * hidden * half, transcendentals=0
         ),
@@ -185,13 +197,18 @@
             send_ref[e * GROUP + q] = piece
 
 
-def home_call(layer, experts, back, grad, x, move):
+def home_call(layer, experts, back, grad, x, move, weights, where, mats):
+    chunks, _, _, _, rows_c, half = weights.shape
     n_in, lanes = back.shape
     slots = n_in // GROUP
     size = slots // experts
     features = PARTS * lanes
 
-    def body(back_ref, grad_ref, x_ref, move_ref, out_ref, send_ref):
+    def body(back_ref, grad_ref, x_ref, move_ref, w_ref, out_ref, send_ref, next_ref, sem):
+        copies = load(w_ref, where, next_ref, sem)
+        for pair in copies:
+            for copy in pair:
+                copy.start()
         total = back_ref[...].astype(F32).reshape(experts, GROUP, size, lanes).sum(axis=1)
         total = total.reshape(slots, lanes)
         xf = x_ref[0].astype(F32)
@@ -212,6 +229,9 @@
         moved = dot_n(move_ref[0], grad_new.astype(BF16))
         out_ref[...] = moved.astype(BF16)
         spread(send_ref, moved, experts)
+        for pair in copies:
+            for copy in pair:
+                copy.wait()
 
     return pl.pallas_call(
         body,
@@ -221,18 +241,23 @@
             pl.BlockSpec((slots, lanes), lambda i: (0, 0)),
             pl.BlockSpec((1, slots, lanes), lambda i: (layer, 0, 0)),
             pl.BlockSpec((1, slots, slots), lambda i: (layer, 0, 0)),
+            pl.BlockSpec(memory_space=pltpu.HBM),
         ],
         out_specs=[
             pl.BlockSpec((slots, lanes), lambda i: (0, 0)),
             pl.BlockSpec((experts * GROUP, size, lanes), lambda i: (0, 0, 0)),
+            pl.BlockSpec(memory_space=pltpu.VMEM),
         ],
         out_shape=[
             jax.ShapeDtypeStruct((slots, lanes), BF16),
             jax.ShapeDtypeStruct((experts * GROUP, size, lanes), BF16),
-        ],
+            jax.ShapeDtypeStruct((mats, 2, chunks, rows_c, half), BF16),
+        ],
+        scratch_shapes=[pltpu.SemaphoreType.DMA((mats, 2))],
+        compiler_params=pltpu.CompilerParams(vmem_limit_bytes=LIMIT),
         cost_estimate=pl.CostEstimate(flops=10 * n_in * lanes, bytes_accessed=4 * n_in * lanes, transcendentals=0),
         name="home",
-    )(back, grad, x, move)
+    )(back, grad, x, move, weights)
 
 
 def shards(saved, cotangent, routes, w_gate, w_up, w_down):
@@ -275,9 +300,8 @@
     for members in SETS:
         low = min(members)
         mine = cut[low : low + len(members)]
-        got = lax.all_gather(mine, ("pipe", "dp"), axis=0).reshape(
-            layers, 2, len(members), 3, hidden // layers, half
-        )
+        got = lax.all_gather(mine, ("pipe", "dp"), axis=0)
+        got = got.reshape(layers, 2, len(members), 3, hidden // layers, half)
         for layer in members:
             weights[layer] = (got, layer - low)
 
@@ -320,12 +344,16 @@
     ).reshape(width, size, lanes)
     for layer in range(layers - 1, -1, -1):
         rows = exchange(send)
-        got, where = weights[layer]
         if layer == 0:
-            (kept,) = expert_call(layer, where, True, rows, got, fac, kept)
+            (kept,) = expert_call(layer, None, True, rows, loaded, fac, kept)
             break
-        kept, partial = expert_call(layer, where, False, rows, got, fac, kept)
-        grad, send = home_call(layer, experts, exchange(partial), grad, x_all, move)
+        if layer == layers - 1:
+            kept, partial = expert_call(layer, weights[layer][1], False, rows, weights[layer][0], fac, kept)
+        else:
+            kept, partial = expert_call(layer, None, False, rows, loaded, fac, kept)
+        grad, send, loaded = home_call(
+            layer, experts, exchange(partial), grad, x_all, move, *weights[layer - 1], 1 if layer == 1 else 3
+        )
 
     grads = lax.all_to_all(kept, "pipe", split_axis=0, concat_axis=0, tiled=True)
     grads = grads.reshape(MICRO * rows_n, 2 * hidden)

time: 541 us -> 516 us (0.954)
  Pallas kernels: 58.8 us -> 38.5 us
  waiting for transfers between devices: 88.5 us -> 96.7 us
  local copies, waits for them, and re-layouts: 27.1 us -> 21.4 us
    pallas_call x8, Pallas kernels: 36.5 us -> 17.8 us  [expert_call(): pl.pallas_call(body, grid=(1,), in_specs=[whole, pl.BlockSpec(memory_spac...]
  transfers between devices with their start and end apart: 24 -> 24, of which waited for: 12 -> 12; matrix products, arithmetic and copies ran while one was open for 6% -> 6% of each run, Pallas kernels for 8% -> 5%
where the time goes in v4:
time: 516 us; the launch traced here: 514 us
  blocking collectives  214 us (41%)
  starting transfers between devices  112 us (22%)
  waiting for transfers between devices  96.7 us (19%)
  Pallas kernels  38.5 us (7%)
  local copies, waits for them, and re-layouts  21.4 us (4%)
  between operations  14.4 us (3%)
  other arithmetic  10.6 us (2%)
  matrix products  7.23 us (1%)
    all_to_all x12, blocking collectives, exchange(): lax.all_to_all(block, 'expert', split_axis=0, concat_axis=0, tiled=True)  187 us
    ppermute x14, waiting for transfers between devices, to_planes(): lax.ppermute(piece, 'pipe', [((p + d) % layers, p) for p in range(layers)])  56.7 us
    ppermute x14, starting transfers between devices, to_planes(): lax.ppermute(piece, 'pipe', [((p + d) % layers, p) for p in range(layers)])  55.3 us
    all_to_all x1, blocking collectives, shards(): fac = lax.all_to_all(fac, 'pipe', split_axis=0, concat_axis=0, tiled=True)  26.9 us
    all_to_all x3, waiting for transfers between devices, exchange(): lax.all_to_all(block, 'expert', split_axis=0, concat_axis=0, tiled=True)  24.4 us
    all_to_all x3, starting transfers between devices, exchange(): lax.all_to_all(block, 'expert', split_axis=0, concat_axis=0, tiled=True)  19.6 us
    ppermute x1, starting transfers between devices, shards(): got = lax.ppermute(outer(other), 'dp', swap)  19.5 us
    pallas_call x8, Pallas kernels, expert_call(): pl.pallas_call(body, grid=(1,), in_specs=[whole, pl.BlockSpec(memory_spac...  17.8 us
  transfers between devices with their start and end apart: 24, of which 12 were waited for; matrix products, arithmetic and copies ran while one was open for 6% of the time, Pallas kernels for 5%

profile of v4, /device:TPU:1, one launch (start us, length us, event | category | flops | bytes accessed | tf_op | source)
XLA Modules:
  0.0 514.3 jit_solution(13549237004061269740)
XLA Ops:
  9.3 11.5 %collective-permute-start.7 = (bf16[3,32,1280]{2,1,0:T(8,128)(2,1)S(1)}, bf16[3,32,1280]{2,1,0:T(8,128)(2,1)S(1)}, u32[]{:S(2)}, u32[]{:S(2)}) collective-permute-start(bf16[3,32,1280]{2,1,0:T(8,128)(2,1)S(1)} %get-tuple-element.84), channel_id=1, source_target_pairs={{64,0},{128,64},{192,128},{256,192},{320,256},{384,320},{448,384},... | collective-permute-start | bytes 737288 | tf_op jit(solution)/shard_map/ppermute | solution.py:284
  20.7 2.2 collective-permute-start.8
  22.9 1.9 collective-permute-start.9
  24.9 7.3 %collective-permute-start.10 = (bf16[3,32,1280]{2,1,0:T(8,128)(2,1)S(1)}, bf16[3,32,1280]{2,1,0:T(8,128)(2,1)S(1)}, u32[]{:S(2)}, u32[]{:S(2)}) collective-permute-start(bf16[3,32,1280]{2,1,0:T(8,128)(2,1)S(1)} %get-tuple-element.81), channel_id=1, source_target_pairs={{256,0},{320,64},{384,128},{448,192},{0,256},{64,320},{128,384},{1... | collective-permute-start | bytes 737288 | tf_op jit(solution)/shard_map/ppermute | solution.py:284
  32.1 1.9 collective-permute-start.11
  34.1 3.1 collective-permute-start.12
  37.2 3.3 collective-permute-start.13
  40.6 21.5 %collective-permute-done.9 = bf16[3,32,1280]{2,1,0:T(8,128)(2,1)S(1)} collective-permute-done((bf16[3,32,1280]{2,1,0:T(8,128)(2,1)S(1)}, bf16[3,32,1280]{2,1,0:T(8,128)(2,1)S(1)}, u32[]{:S(2)}, u32[]{:S(2)}) %collective-permute-start.9) | collective-permute-done | bytes 245792 | tf_op jit(solution)/shard_map/ppermute | solution.py:284
  62.2 6.4 %collective-permute-done.12 = bf16[3,32,1280]{2,1,0:T(8,128)(2,1)S(1)} collective-permute-done((bf16[3,32,1280]{2,1,0:T(8,128)(2,1)S(1)}, bf16[3,32,1280]{2,1,0:T(8,128)(2,1)S(1)}, u32[]{:S(2)}, u32[]{:S(2)}) %collective-permute-start.12) | collective-permute-done | bytes 245792 | tf_op jit(solution)/shard_map/ppermute | solution.py:284
  68.6 7.1 %collective-permute-done.13 = bf16[3,32,1280]{2,1,0:T(8,128)(2,1)S(1)} collective-permute-done((bf16[3,32,1280]{2,1,0:T(8,128)(2,1)S(1)}, bf16[3,32,1280]{2,1,0:T(8,128)(2,1)S(1)}, u32[]{:S(2)}, u32[]{:S(2)}) %collective-permute-start.13) | collective-permute-done | bytes 245792 | tf_op jit(solution)/shard_map/ppermute | solution.py:284
  83.4 9.7 %all-to-all-start.1 = ((bf16[32,8,8,640]{3,2,1,0:T(8,128)(2,1)}), bf16[32,8,8,640]{3,2,1,0:T(8,128)(2,1)S(1)}, u32[]{:S(2)}, u32[]{:S(2)}) async-start(bf16[32,8,8,640]{3,2,1,0:T(8,128)(2,1)} %bitcast.144), calls=%async_computation.1 | async-start | bytes 5242880 | tf_op jit(solution)/shard_map/all_to_all | solution.py:295
  96.8 2.2 collective-permute-start
  99.1 6.4 %collective-permute-done = bf16[64,768]{1,0:T(8,128)(2,1)S(1)} collective-permute-done((bf16[64,768]{1,0:T(8,128)(2,1)S(1)}, bf16[64,768]{1,0:T(8,128)(2,1)S(1)}, u32[]{:S(2)}, u32[]{:S(2)}) %collective-permute-start) | collective-permute-done | bytes 98336 | tf_op jit(solution)/shard_map/ppermute | solution.py:284
  106.3 1.9 collective-permute-start.1
  108.2 2.5 pad_maximum_fusion.2
  110.7 3.8 collective-permute-start.14
  114.5 5.0 collective-permute-start.2
  119.5 5.5 %collective-permute-start.3 = (bf16[64,768]{1,0:T(8,128)(2,1)}, bf16[64,768]{1,0:T(8,128)(2,1)S(1)}, u32[]{:S(2)}, u32[]{:S(2)}) collective-permute-start(bf16[64,768]{1,0:T(8,128)(2,1)} %get-tuple-element.94), channel_id=1, source_target_pairs={{256,0},{320,64},{384,128},{448,192},{0,256},{64,320},{128,384},{1... | collective-permute-start | bytes 294920 | tf_op jit(solution)/shard_map/ppermute | solution.py:284
  125.0 3.5 collective-permute-start.4
  128.5 1.9 collective-permute-start.5
  131.4 4.0 collective-permute-start.6
  135.5 4.2 collective-permute-done.4
  139.8 4.0 collective-permute-done.5
  143.7 7.1 %collective-permute-done.6 = bf16[64,768]{1,0:T(8,128)(2,1)S(1)} collective-permute-done((bf16[64,768]{1,0:T(8,128)(2,1)}, bf16[64,768]{1,0:T(8,128)(2,1)S(1)}, u32[]{:S(2)}, u32[]{:S(2)}) %collective-permute-start.6) | collective-permute-done | bytes 98336 | tf_op jit(solution)/shard_map/ppermute | solution.py:284
  161.5 9.0 %all-to-all-start = ((bf16[32,8,640]{2,1,0:T(8,128)(2,1)}), bf16[32,8,640]{2,1,0:T(8,128)(2,1)S(1)}, u32[]{:S(2)}, u32[]{:S(2)}) async-start(bf16[32,8,640]{2,1,0:T(8,128)(2,1)} %bitcast.152), calls=%async_computation | async-start | bytes 655360 | tf_op jit(solution)/shard_map/all_to_all | solution.py:338
  174.1 5.5 %factors.1 = (bf16[512,2560]{1,0:T(8,128)(2,1)}, bf16[8,64,512]{2,1,0:T(8,128)(2,1)}) custom-call(bf16[32,8,8,640]{3,2,1,0:T(8,128)(2,1)} %copy-done.2, bf16[2,2,256,1280]{3,2,1,0:T(8,128)(2,1)} %pad_maximum_fusion.w_ref), custom_call_target="tpu_custom_call" | custom-call | flops 1342177280 | bytes 5242880 | tf_op jit(solution)/shard_map/factors/pallas_call | solution.py:167
  179.5 3.6 all-to-all-done
  183.2 26.9 %all_to_all.90.fac_ref = bf16[8,64,512]{2,1,0:T(8,128)(2,1)S(1)} all-to-all(bf16[8,64,512]{2,1,0:T(8,128)(2,1)} %get-tuple-element.38), channel_id=1, replica_groups=mesh['pipe'=8,'expert'=32,'dp'=2] {'pipe'}, dimensions={0} | all-to-all | bytes 1048576 | tf_op jit(solution)/shard_map/all_to_all | solution.py:334
  210.9 3.8 expert.8
  214.8 6.4 %all-to-all-start.3 = ((bf16[32,8,640]{2,1,0:T(8,128)(2,1)}), bf16[32,8,640]{2,1,0:T(8,128)(2,1)S(1)}, u32[]{:S(2)}, u32[]{:S(2)}) async-start(bf16[32,8,640]{2,1,0:T(8,128)(2,1)} %bitcast.46), calls=%async_computation.3 | async-start | bytes 655360 | tf_op jit(solution)/shard_map/all_to_all | solution.py:338
  221.9 10.0 %all-to-all-done.3 = bf16[32,8,640]{2,1,0:T(8,128)(2,1)S(1)} async-done(((bf16[32,8,640]{2,1,0:T(8,128)(2,1)}), bf16[32,8,640]{2,1,0:T(8,128)(2,1)S(1)}, u32[]{:S(2)}, u32[]{:S(2)}) %all-to-all-start.3) | async-done | bytes 327712 | tf_op jit(solution)/shard_map/all_to_all | solution.py:338
  231.9 2.3 home.7
  234.3 16.8 %all_to_all.91 = bf16[32,8,640]{2,1,0:T(8,128)(2,1)S(1)} all-to-all(bf16[32,8,640]{2,1,0:T(8,128)(2,1)S(1)} %get-tuple-element.40), channel_id=1, replica_groups=mesh['pipe'=8,'expert'=32,'dp'=2] {'expert'}, dimensions={0} | all-to-all | bytes 655360 | tf_op jit(solution)/shard_map/all_to_all | solution.py:338
  251.1 2.1 expert.9
  253.2 16.8 %all_to_all.92 = bf16[32,8,640]{2,1,0:T(8,128)(2,1)S(1)} all-to-all(bf16[32,8,640]{2,1,0:T(8,128)(2,1)S(1)} %bitcast.131), channel_id=1, replica_groups=mesh['pipe'=8,'expert'=32,'dp'=2] {'expert'}, dimensions={0} | all-to-all | bytes 655360 | tf_op jit(solution)/shard_map/all_to_all | solution.py:338
  269.9 2.2 home.8
  272.2 16.7 %all_to_all.93 = bf16[32,8,640]{2,1,0:T(8,128)(2,1)S(1)} all-to-all(bf16[32,8,640]{2,1,0:T(8,128)(2,1)S(1)} %get-tuple-element.45), channel_id=1, replica_groups=mesh['pipe'=8,'expert'=32,'dp'=2] {'expert'}, dimensions={0} | all-to-all | bytes 655360 | tf_op jit(solution)/shard_map/all_to_all | solution.py:338
  288.9 2.1 expert.10
  291.0 16.6 %all_to_all.94 = bf16[32,8,640]{2,1,0:T(8,128)(2,1)S(1)} all-to-all(bf16[32,8,640]{2,1,0:T(8,128)(2,1)S(1)} %bitcast.132), channel_id=1, replica_groups=mesh['pipe'=8,'expert'=32,'dp'=2] {'expert'}, dimensions={0} | all-to-all | bytes 655360 | tf_op jit(solution)/shard_map/all_to_all | solution.py:338
  307.6 2.2 home.9
  309.8 16.5 %all_to_all.95 = bf16[32,8,640]{2,1,0:T(8,128)(2,1)S(1)} all-to-all(bf16[32,8,640]{2,1,0:T(8,128)(2,1)S(1)} %get-tuple-element.50), channel_id=1, replica_groups=mesh['pipe'=8,'expert'=32,'dp'=2] {'expert'}, dimensions={0} | all-to-all | bytes 655360 | tf_op jit(solution)/shard_map/all_to_all | solution.py:338
  326.3 2.1 expert.11
  328.4 16.2 %all_to_all.96 = bf16[32,8,640]{2,1,0:T(8,128)(2,1)S(1)} all-to-all(bf16[32,8,640]{2,1,0:T(8,128)(2,1)S(1)} %bitcast.133), channel_id=1, replica_groups=mesh['pipe'=8,'expert'=32,'dp'=2] {'expert'}, dimensions={0} | all-to-all | bytes 655360 | tf_op jit(solution)/shard_map/all_to_all | solution.py:338
  344.6 2.2 home.10
  346.8 14.9 %all_to_all.97 = bf16[32,8,640]{2,1,0:T(8,128)(2,1)S(1)} all-to-all(bf16[32,8,640]{2,1,0:T(8,128)(2,1)S(1)} %get-tuple-element.55), channel_id=1, replica_groups=mesh['pipe'=8,'expert'=32,'dp'=2] {'expert'}, dimensions={0} | all-to-all | bytes 655360 | tf_op jit(solution)/shard_map/all_to_all | solution.py:338
  361.7 2.4 expert.12
  364.1 4.2 all-to-all-start.11
  368.3 10.7 %all-to-all-done.11 = bf16[32,8,640]{2,1,0:T(8,128)(2,1)S(1)} async-done(((bf16[32,8,640]{2,1,0:T(8,128)(2,1)}), bf16[32,8,640]{2,1,0:T(8,128)(2,1)S(1)}, u32[]{:S(2)}, u32[]{:S(2)}) %all-to-all-start.11) | async-done | bytes 327712 | tf_op jit(solution)/shard_map/all_to_all | solution.py:338
  379.0 2.1 home.11
  381.2 14.5 %all_to_all.98 = bf16[32,8,640]{2,1,0:T(8,128)(2,1)S(1)} all-to-all(bf16[32,8,640]{2,1,0:T(8,128)(2,1)S(1)} %get-tuple-element.60), channel_id=1, replica_groups=mesh['pipe'=8,'expert'=32,'dp'=2] {'expert'}, dimensions={0} | all-to-all | bytes 655360 | tf_op jit(solution)/shard_map/all_to_all | solution.py:338
  395.7 2.1 expert.13
  397.8 14.4 %all_to_all.99 = bf16[32,8,640]{2,1,0:T(8,128)(2,1)S(1)} all-to-all(bf16[32,8,640]{2,1,0:T(8,128)(2,1)S(1)} %bitcast.134), channel_id=1, replica_groups=mesh['pipe'=8,'expert'=32,'dp'=2] {'expert'}, dimensions={0} | all-to-all | bytes 655360 | tf_op jit(solution)/shard_map/all_to_all | solution.py:338
  412.2 2.1 home.12
  414.4 14.5 %all_to_all.100 = bf16[32,8,640]{2,1,0:T(8,128)(2,1)S(1)} all-to-all(bf16[32,8,640]{2,1,0:T(8,128)(2,1)S(1)} %get-tuple-element.65), channel_id=1, replica_groups=mesh['pipe'=8,'expert'=32,'dp'=2] {'expert'}, dimensions={0} | all-to-all | bytes 655360 | tf_op jit(solution)/shard_map/all_to_all | solution.py:338
  428.8 2.1 expert.14
  430.9 14.4 %all_to_all.101 = bf16[32,8,640]{2,1,0:T(8,128)(2,1)S(1)} all-to-all(bf16[32,8,640]{2,1,0:T(8,128)(2,1)S(1)} %bitcast.135), channel_id=1, replica_groups=mesh['pipe'=8,'expert'=32,'dp'=2] {'expert'}, dimensions={0} | all-to-all | bytes 655360 | tf_op jit(solution)/shard_map/all_to_all | solution.py:338
  445.4 2.0 home.13
  447.3 14.7 %all_to_all.102 = bf16[32,8,640]{2,1,0:T(8,128)(2,1)S(1)} all-to-all(bf16[32,8,640]{2,1,0:T(8,128)(2,1)S(1)} %get-tuple-element.70), channel_id=1, replica_groups=mesh['pipe'=8,'expert'=32,'dp'=2] {'expert'}, dimensions={0} | all-to-all | bytes 655360 | tf_op jit(solution)/shard_map/all_to_all | solution.py:338
  463.2 3.5 all-to-all-start.17
  466.7 12.1 %all-to-all-done.17 = bf16[8,64,512]{2,1,0:T(8,128)(2,1)S(1)} async-done(((bf16[8,64,512]{2,1,0:T(8,128)(2,1)}), bf16[8,64,512]{2,1,0:T(8,128)(2,1)S(1)}, u32[]{:S(2)}, u32[]{:S(2)}) %all-to-all-start.17) | async-done | bytes 524320 | tf_op jit(solution)/shard_map/all_to_all | solution.py:358
  478.7 3.3 convolution_convert_fusion.1
  482.0 19.5 %collective-permute-start.15 = (bf16[512,1280]{1,0:T(8,128)(2,1)}, bf16[512,1280]{1,0:T(8,128)(2,1)S(1)}, u32[]{:S(2)}, u32[]{:S(2)}) collective-permute-start(bf16[512,1280]{1,0:T(8,128)(2,1)} %convolution_convert_fusion.1), channel_id=1, source_target_pairs={{0,1},{1,0},{2,3},{3,2},{4,5},{5,4},{6,7},{7,6},{8,9},{9,8},{10,11... | collective-permute-start | bytes 3932168 | tf_op jit(solution)/shard_map/ppermute | solution.py:368
  501.5 2.8 collective-permute-done.15
  504.3 2.3 add_convert_fusion
  (95 shorter events, 33.2 us)
Async XLA Ops:
  7.2 73.4 %copy-start = (bf16[1,1,128,2560]{3,2,1,0:T(8,128)(2,1)S(1)}, bf16[1,1,128,2560]{3,2,1,0:T(8,128)(2,1)}, u32[]{:S(2)}) copy-start(bf16[1,1,128,2560]{3,2,1,0:T(8,128)(2,1)} %param.6) | copy-start | bytes 1966084
  7.2 202.9 %all-gather.7.cloned.1.call-start = ((), (), s32[]{:S(2)}) async-start(), calls=%async_computation.18 | async-start | bytes 8355840 | tf_op jit(solution)/shard_map/all_gather | solution.py:303
  9.3 24.8 %collective-permute-start.7 = (bf16[3,32,1280]{2,1,0:T(8,128)(2,1)S(1)}, bf16[3,32,1280]{2,1,0:T(8,128)(2,1)S(1)}, u32[]{:S(2)}, u32[]{:S(2)}) collective-permute-start(bf16[3,32,1280]{2,1,0:T(8,128)(2,1)S(1)} %get-tuple-element.84), channel_id=1, source_target_pairs={{64,0},{128,64},{192,128},{256,192},{320,256},{384,320},{448,384},... | collective-permute-start | bytes 737288 | tf_op jit(solution)/shard_map/ppermute | solution.py:284
  20.7 16.5 %collective-permute-start.8 = (bf16[3,32,1280]{2,1,0:T(8,128)(2,1)S(1)}, bf16[3,32,1280]{2,1,0:T(8,128)(2,1)S(1)}, u32[]{:S(2)}, u32[]{:S(2)}) collective-permute-start(bf16[3,32,1280]{2,1,0:T(8,128)(2,1)S(1)} %get-tuple-element.83), channel_id=1, source_target_pairs={{128,0},{192,64},{256,128},{320,192},{384,256},{448,320},{0,384},{... | collective-permute-start | bytes 737288 | tf_op jit(solution)/shard_map/ppermute | solution.py:284
  22.9 39.2 %collective-permute-start.9 = (bf16[3,32,1280]{2,1,0:T(8,128)(2,1)S(1)}, bf16[3,32,1280]{2,1,0:T(8,128)(2,1)S(1)}, u32[]{:S(2)}, u32[]{:S(2)}) collective-permute-start(bf16[3,32,1280]{2,1,0:T(8,128)(2,1)S(1)} %get-tuple-element.82), channel_id=1, source_target_pairs={{192,0},{256,64},{320,128},{384,192},{448,256},{0,320},{64,384},{1... | collective-permute-start | bytes 737288 | tf_op jit(solution)/shard_map/ppermute | solution.py:284
  24.9 37.3 %collective-permute-start.10 = (bf16[3,32,1280]{2,1,0:T(8,128)(2,1)S(1)}, bf16[3,32,1280]{2,1,0:T(8,128)(2,1)S(1)}, u32[]{:S(2)}, u32[]{:S(2)}) collective-permute-start(bf16[3,32,1280]{2,1,0:T(8,128)(2,1)S(1)} %get-tuple-element.81), channel_id=1, source_target_pairs={{256,0},{320,64},{384,128},{448,192},{0,256},{64,320},{128,384},{1... | collective-permute-start | bytes 737288 | tf_op jit(solution)/shard_map/ppermute | solution.py:284
  32.1 30.1 %collective-permute-start.11 = (bf16[3,32,1280]{2,1,0:T(8,128)(2,1)S(1)}, bf16[3,32,1280]{2,1,0:T(8,128)(2,1)S(1)}, u32[]{:S(2)}, u32[]{:S(2)}) collective-permute-start(bf16[3,32,1280]{2,1,0:T(8,128)(2,1)S(1)} %get-tuple-element.80), channel_id=1, source_target_pairs={{320,0},{384,64},{448,128},{0,192},{64,256},{128,320},{192,384},{2... | collective-permute-start | bytes 737288 | tf_op jit(solution)/shard_map/ppermute | solution.py:284
  34.1 34.5 %collective-permute-start.12 = (bf16[3,32,1280]{2,1,0:T(8,128)(2,1)S(1)}, bf16[3,32,1280]{2,1,0:T(8,128)(2,1)S(1)}, u32[]{:S(2)}, u32[]{:S(2)}) collective-permute-start(bf16[3,32,1280]{2,1,0:T(8,128)(2,1)S(1)} %get-tuple-element.79), channel_id=1, source_target_pairs={{384,0},{448,64},{0,128},{64,192},{128,256},{192,320},{256,384},{3... | collective-permute-start | bytes 737288 | tf_op jit(solution)/shard_map/ppermute | solution.py:284
  37.2 38.5 %collective-permute-start.13 = (bf16[3,32,1280]{2,1,0:T(8,128)(2,1)S(1)}, bf16[3,32,1280]{2,1,0:T(8,128)(2,1)S(1)}, u32[]{:S(2)}, u32[]{:S(2)}) collective-permute-start(bf16[3,32,1280]{2,1,0:T(8,128)(2,1)S(1)} %get-tuple-element.78), channel_id=1, source_target_pairs={{448,0},{0,64},{64,128},{128,192},{192,256},{256,320},{320,384},{3... | collective-permute-start | bytes 737288 | tf_op jit(solution)/shard_map/ppermute | solution.py:284
  76.6 2.6 copy-start.6
  76.6 193.3 %all-gather.9.cloned.1.call-start = ((), (), s32[]{:S(2)}) async-start(), calls=%async_computation.19 | async-start | bytes 12533760 | tf_op jit(solution)/shard_map/all_gather | solution.py:303
  77.9 290.4 %all-gather.11.cloned.1.call-start = ((), (), s32[]{:S(2)}) async-start(), calls=%async_computation.20 | async-start | bytes 12533760 | tf_op jit(solution)/shard_map/all_gather | solution.py:303
  83.4 11.0 %copy-start.5 = (bf16[128,320]{0,1:T(8,128)(2,1)S(1)}, bf16[128,320]{0,1:T(8,128)(2,1)}, u32[]{:S(2)}) copy-start(bf16[128,320]{0,1:T(8,128)(2,1)} %param.7) | copy-start | bytes 245764
  83.4 76.3 %all-to-all-start.1 = ((bf16[32,8,8,640]{3,2,1,0:T(8,128)(2,1)}), bf16[32,8,8,640]{3,2,1,0:T(8,128)(2,1)S(1)}, u32[]{:S(2)}, u32[]{:S(2)}) async-start(bf16[32,8,8,640]{3,2,1,0:T(8,128)(2,1)} %bitcast.144), calls=%async_computation.1 | async-start | bytes 5242880 | tf_op jit(solution)/shard_map/all_to_all | solution.py:295
  96.8 8.6 %collective-permute-start = (bf16[64,768]{1,0:T(8,128)(2,1)S(1)}, bf16[64,768]{1,0:T(8,128)(2,1)S(1)}, u32[]{:S(2)}, u32[]{:S(2)}) collective-permute-start(bf16[64,768]{1,0:T(8,128)(2,1)S(1)} %dynamic-slice_bitcast_fusion.13), channel_id=1, source_target_pairs={{64,0},{128,64},{192,128},{256,192},{320,256},{384,320},{448,384},... | collective-permute-start | bytes 294920 | tf_op jit(solution)/shard_map/ppermute | solution.py:284
  106.3 22.2 %collective-permute-start.1 = (bf16[64,768]{1,0:T(8,128)(2,1)}, bf16[64,768]{1,0:T(8,128)(2,1)}, u32[]{:S(2)}, u32[]{:S(2)}) collective-permute-start(bf16[64,768]{1,0:T(8,128)(2,1)} %get-tuple-element.96), channel_id=1, source_target_pairs={{128,0},{192,64},{256,128},{320,192},{384,256},{448,320},{0,384},{... | collective-permute-start | bytes 294920 | tf_op jit(solution)/shard_map/ppermute | solution.py:284
  110.7 59.8 %collective-permute-start.14 = (bf16[2,256,1280]{2,1,0:T(8,128)(2,1)}, bf16[2,256,1280]{2,1,0:T(8,128)(2,1)}, u32[]{:S(2)}, u32[]{:S(2)}) collective-permute-start(bf16[2,256,1280]{2,1,0:T(8,128)(2,1)} %pad_maximum_fusion.2), channel_id=1, source_target_pairs={{0,1},{1,0},{2,3},{3,2},{4,5},{5,4},{6,7},{7,6},{8,9},{9,8},{10,11... | collective-permute-start | bytes 3932168 | tf_op jit(solution)/shard_map/ppermute | solution.py:330
  114.5 16.9 %collective-permute-start.2 = (bf16[64,768]{1,0:T(8,128)(2,1)}, bf16[64,768]{1,0:T(8,128)(2,1)S(1)}, u32[]{:S(2)}, u32[]{:S(2)}) collective-permute-start(bf16[64,768]{1,0:T(8,128)(2,1)} %get-tuple-element.95), channel_id=1, source_target_pairs={{192,0},{256,64},{320,128},{384,192},{448,256},{0,320},{64,384},{1... | collective-permute-start | bytes 294920 | tf_op jit(solution)/shard_map/ppermute | solution.py:284
  119.5 16.0 %collective-permute-start.3 = (bf16[64,768]{1,0:T(8,128)(2,1)}, bf16[64,768]{1,0:T(8,128)(2,1)S(1)}, u32[]{:S(2)}, u32[]{:S(2)}) collective-permute-start(bf16[64,768]{1,0:T(8,128)(2,1)} %get-tuple-element.94), channel_id=1, source_target_pairs={{256,0},{320,64},{384,128},{448,192},{0,256},{64,320},{128,384},{1... | collective-permute-start | bytes 294920 | tf_op jit(solution)/shard_map/ppermute | solution.py:284
  125.0 14.7 %collective-permute-start.4 = (bf16[64,768]{1,0:T(8,128)(2,1)}, bf16[64,768]{1,0:T(8,128)(2,1)S(1)}, u32[]{:S(2)}, u32[]{:S(2)}) collective-permute-start(bf16[64,768]{1,0:T(8,128)(2,1)} %get-tuple-element.93), channel_id=1, source_target_pairs={{320,0},{384,64},{448,128},{0,192},{64,256},{128,320},{192,384},{2... | collective-permute-start | bytes 294920 | tf_op jit(solution)/shard_map/ppermute | solution.py:284
  128.5 15.2 %collective-permute-start.5 = (bf16[64,768]{1,0:T(8,128)(2,1)}, bf16[64,768]{1,0:T(8,128)(2,1)S(1)}, u32[]{:S(2)}, u32[]{:S(2)}) collective-permute-start(bf16[64,768]{1,0:T(8,128)(2,1)} %get-tuple-element.92), channel_id=1, source_target_pairs={{384,0},{448,64},{0,128},{64,192},{128,256},{192,320},{256,384},{3... | collective-permute-start | bytes 294920 | tf_op jit(solution)/shard_map/ppermute | solution.py:284
  131.4 19.4 %collective-permute-start.6 = (bf16[64,768]{1,0:T(8,128)(2,1)}, bf16[64,768]{1,0:T(8,128)(2,1)S(1)}, u32[]{:S(2)}, u32[]{:S(2)}) collective-permute-start(bf16[64,768]{1,0:T(8,128)(2,1)} %get-tuple-element.91), channel_id=1, source_target_pairs={{448,0},{0,64},{64,128},{128,192},{192,256},{256,320},{320,384},{3... | collective-permute-start | bytes 294920 | tf_op jit(solution)/shard_map/ppermute | solution.py:284
  150.8 10.7 %copy-start.3 = (bf16[8,64,768]{2,1,0:T(8,128)(2,1)}, bf16[8,64,768]{2,1,0:T(8,128)(2,1)S(1)}, u32[]{:S(2)}) copy-start(bf16[8,64,768]{2,1,0:T(8,128)(2,1)S(1)} %bitcast_dynamic-update-slice_fusion.7) | copy-start | bytes 2359300
  159.8 12.6 %copy-start.2 = (bf16[32,8,8,640]{3,2,1,0:T(8,128)(2,1)}, bf16[32,8,8,640]{3,2,1,0:T(8,128)(2,1)S(1)}, u32[]{:S(2)}) copy-start(bf16[32,8,8,640]{3,2,1,0:T(8,128)(2,1)S(1)} %all-to-all-done.1.u_ref) | copy-start | bytes 7864324
  161.5 21.7 %all-to-all-start = ((bf16[32,8,640]{2,1,0:T(8,128)(2,1)}), bf16[32,8,640]{2,1,0:T(8,128)(2,1)S(1)}, u32[]{:S(2)}, u32[]{:S(2)}) async-start(bf16[32,8,640]{2,1,0:T(8,128)(2,1)} %bitcast.152), calls=%async_computation | async-start | bytes 655360 | tf_op jit(solution)/shard_map/all_to_all | solution.py:338
  210.9 10.3 %copy-start.4 = (bf16[8,64,768]{2,1,0:T(8,128)(2,1)S(1)}, bf16[8,64,768]{2,1,0:T(8,128)(2,1)}, u32[]{:S(2)}) copy-start(bf16[8,64,768]{2,1,0:T(8,128)(2,1)} %copy-done.3) | copy-start | bytes 2359300
  214.8 17.1 %all-to-all-start.3 = ((bf16[32,8,640]{2,1,0:T(8,128)(2,1)}), bf16[32,8,640]{2,1,0:T(8,128)(2,1)S(1)}, u32[]{:S(2)}, u32[]{:S(2)}) async-start(bf16[32,8,640]{2,1,0:T(8,128)(2,1)} %bitcast.46), calls=%async_computation.3 | async-start | bytes 655360 | tf_op jit(solution)/shard_map/all_to_all | solution.py:338
  364.1 15.0 %all-to-all-start.11 = ((bf16[32,8,640]{2,1,0:T(8,128)(2,1)}), bf16[32,8,640]{2,1,0:T(8,128)(2,1)S(1)}, u32[]{:S(2)}, u32[]{:S(2)}) async-start(bf16[32,8,640]{2,1,0:T(8,128)(2,1)} %bitcast.59), calls=%async_computation.11 | async-start | bytes 655360 | tf_op jit(solution)/shard_map/all_to_all | solution.py:338
  463.2 15.6 %all-to-all-start.17 = ((bf16[8,64,512]{2,1,0:T(8,128)(2,1)}), bf16[8,64,512]{2,1,0:T(8,128)(2,1)S(1)}, u32[]{:S(2)}, u32[]{:S(2)}) async-start(bf16[8,64,512]{2,1,0:T(8,128)(2,1)} %expert.15), calls=%async_computation.17 | async-start | bytes 1048576 | tf_op jit(solution)/shard_map/all_to_all | solution.py:358
  482.0 22.3 %collective-permute-start.15 = (bf16[512,1280]{1,0:T(8,128)(2,1)}, bf16[512,1280]{1,0:T(8,128)(2,1)S(1)}, u32[]{:S(2)}, u32[]{:S(2)}) collective-permute-start(bf16[512,1280]{1,0:T(8,128)(2,1)} %convolution_convert_fusion.1), channel_id=1, source_target_pairs={{0,1},{1,0},{2,3},{3,2},{4,5},{5,4},{6,7},{7,6},{8,9},{9,8},{10,11... | collective-permute-start | bytes 3932168 | tf_op jit(solution)/shard_map/ppermute | solution.py:368
  504.3 3.4 copy-start.1
Sparse Core Ops, SparseCore 0:
  76.7 76.0 all-gather.6
  155.0 85.8 all-gather.8
  243.0 73.3 all-gather.10

commit v5 on v4

--- a/solution.py
+++ b/solution.py
@@ -13,7 +13,7 @@
 F32 = jnp.float32
 BF16 = jnp.bfloat16
 LIMIT = 48 * 1024 * 1024
-SETS = ((7, 6), (5, 4, 3), (2, 1, 0))
+SETS = ((7, 6), (5, 4), (3, 2, 1, 0))
 
 
 def dot_t(a, b):
@@ -124,7 +124,7 @@
             else [pltpu.VMEM((mats, 2, chunks, rows_c, half), BF16), pltpu.SemaphoreType.DMA((mats, 2))]
         ),
         input_output_aliases={3: 0},
-        compiler_params=pltpu.CompilerParams(vmem_limit_bytes=LIMIT),
+        compiler_params=pltpu.CompilerParams(vmem_limit_bytes=LIMIT // 3 if last else LIMIT),
         cost_estimate=pl.CostEstimate(
             flops=6 * rows_n * hidden * 2 * half, bytes_accessed=mats * 4 * hidden * half, transcendentals=0
         ),
@@ -277,14 +277,6 @@
 
     z = lax.axis_index("pipe")
 
-    def to_planes(blocks):
-        got = blocks
-        for d in range(1, layers):
-            piece = lax.dynamic_index_in_dim(blocks, (z - d + layers) % layers, 0, keepdims=False)
-            piece = lax.ppermute(piece, "pipe", [((p + d) % layers, p) for p in range(layers)])
-            got = lax.dynamic_update_index_in_dim(got, piece, (z + d) % layers, 0)
-        return got
-
     place = placing_of(routes[0, 0, :, 0].reshape(MICRO, tok), experts, cap)
     x = saved[0, 0].reshape(MICRO, tok, feat)
     x_slot = jnp.einsum("mst,mtd->msd", place, x, preferred_element_type=F32)
@@ -295,11 +287,22 @@
     units = lax.all_to_all(send, "expert", split_axis=0, concat_axis=0, tiled=True)
 
     cut = jnp.stack([w_down[0, 0], w_gate[0, 0], w_up[0, 0]]).reshape(3, layers, hidden // layers, half)
-    cut = to_planes(jnp.transpose(cut, (1, 0, 2, 3)))
+    cut = jnp.transpose(cut, (1, 0, 2, 3))
+    pieces = [lax.dynamic_index_in_dim(cut, z, 0, keepdims=False)]
+    for d in range(1, layers):
+        piece = lax.dynamic_index_in_dim(cut, (z - d + layers) % layers, 0, keepdims=False)
+        pieces.append(lax.ppermute(piece, "pipe", [((p + d) % layers, p) for p in range(layers)]))
+
+    def of_layer(layer):
+        out = pieces[0]
+        for d in range(1, layers):
+            out = jnp.where((z + d) % layers == layer, pieces[d], out)
+        return out
+
     weights = {}
     for members in SETS:
         low = min(members)
-        mine = cut[low : low + len(members)]
+        mine = jnp.stack([of_layer(low + i) for i in range(len(members))])
         got = lax.all_gather(mine, ("pipe", "dp"), axis=0)
         got = got.reshape(layers, 2, len(members), 3, hidden // layers, half)
         for layer in members:
@@ -315,7 +318,7 @@
         axis=2,
     )
     pack = jnp.concatenate([x_slot.astype(BF16).reshape(MICRO, slots, lanes), extra], axis=2)
-    pack = to_planes(pack)
+    pack = lax.all_to_all(pack, "pipe", split_axis=0, concat_axis=0, tiled=True)
     x_all = pack[:, :, :lanes]
     place_all = pack[:, :, lanes : lanes + tok]
     grad = pack[:, :, lanes + tok : lanes + tok + thin].reshape(layers, tok, PARTS * thin)

time: 516 us -> 546 us (1.058)
  waiting for transfers between devices: 96.7 us -> 150 us
  local copies, waits for them, and re-layouts: 21.4 us -> 9.36 us
  starting transfers between devices: 112 us -> 103 us
  blocking collectives: 214 us -> 206 us
  other arithmetic: 10.6 us -> 17.6 us
    all_to_all x1, waiting for transfers between devices: 0.01 us -> 50.8 us  [shards(): lax.all_to_all(send, 'expert', split_axis=0, concat_axis=0, tiled=True)]
    all_to_all x0 -> x1, waiting for transfers between devices: none -> 30.6 us  [shards(): pack = lax.all_to_all(pack, 'pipe', split_axis=0, concat_axis=0, tiled=True)]
    ppermute x14 -> x7, waiting for transfers between devices: 56.7 us -> 30.9 us  [shards(): lax.ppermute(piece, 'pipe', [((p + d) % layers, p) for p in range(layers)])]
    ppermute x14 -> x7, starting transfers between devices: 55.3 us -> 32.4 us  [shards(): lax.ppermute(piece, 'pipe', [((p + d) % layers, p) for p in range(layers)])]
    all_to_all x1, blocking collectives: 26.9 us -> 15.8 us  [shards(): fac = lax.all_to_all(fac, 'pipe', split_axis=0, concat_axis=0, tiled=True)]
    another operation x0 -> x11, other arithmetic: none -> 7.49 us  [shards(): mine = jnp.stack([of_layer(low + i) for i in range(len(members))])]
    all_to_all x0 -> x1, starting transfers between devices: none -> 7.44 us  [shards(): pack = lax.all_to_all(pack, 'pipe', split_axis=0, concat_axis=0, tiled=True)]
  transfers between devices with their start and end apart: 24 -> 18, of which waited for: 12 -> 10; matrix products, arithmetic and copies ran while one was open for 6% -> 4% of each run, Pallas kernels for 5% -> 4%
where the time goes in v5:
time: 546 us; the launch traced here: 545 us
  blocking collectives  206 us (38%)
  waiting for transfers between devices  150 us (27%)
  starting transfers between devices  103 us (19%)
  Pallas kernels  38.4 us (7%)
  other arithmetic  17.6 us (3%)
  between operations  14.5 us (3%)
  local copies, waits for them, and re-layouts  9.36 us (2%)
  matrix products  6.33 us (1%)
    all_to_all x12, blocking collectives, exchange(): lax.all_to_all(block, 'expert', split_axis=0, concat_axis=0, tiled=True)  190 us
    all_to_all x1, waiting for transfers between devices, shards(): lax.all_to_all(send, 'expert', split_axis=0, concat_axis=0, tiled=True)  50.8 us
    ppermute x7, starting transfers between devices, shards(): lax.ppermute(piece, 'pipe', [((p + d) % layers, p) for p in range(layers)])  32.4 us
    ppermute x7, waiting for transfers between devices, shards(): lax.ppermute(piece, 'pipe', [((p + d) % layers, p) for p in range(layers)])  30.9 us
    all_to_all x1, waiting for transfers between devices, shards(): pack = lax.all_to_all(pack, 'pipe', split_axis=0, concat_axis=0, tiled=True)  30.6 us
    ppermute x1, starting transfers between devices, shards(): got = lax.ppermute(outer(other), 'dp', swap)  24.7 us
    all_to_all x3, waiting for transfers between devices, exchange(): lax.all_to_all(block, 'expert', split_axis=0, concat_axis=0, tiled=True)  22.6 us
    all_to_all x3, starting transfers between devices, exchange(): lax.all_to_all(block, 'expert', split_axis=0, concat_axis=0, tiled=True)  20.6 us
  transfers between devices with their start and end apart: 18, of which 10 were waited for; matrix products, arithmetic and copies ran while one was open for 4% of the time, Pallas kernels for 4%

profile of v5, /device:TPU:1, one launch (start us, length us, event | category | flops | bytes accessed | tf_op | source)
XLA Modules:
  0.0 544.7 jit_solution(17200378313359304968)
XLA Ops:
  7.3 1.7 pad_maximum_fusion.1
  10.1 4.8 collective-permute-start
  14.9 5.8 %collective-permute-start.1 = (bf16[3,32,1280]{2,1,0:T(8,128)(2,1)S(1)}, bf16[3,32,1280]{2,1,0:T(8,128)(2,1)S(1)}, u32[]{:S(2)}, u32[]{:S(2)}) collective-permute-start(bf16[3,32,1280]{2,1,0:T(8,128)(2,1)S(1)} %get-tuple-element.81), channel_id=1, source_target_pairs={{384,0},{448,64},{0,128},{64,192},{128,256},{192,320},{256,384},{3... | collective-permute-start | bytes 737288 | tf_op jit(solution)/shard_map/ppermute | solution.py:294
  20.8 7.0 %collective-permute-start.2 = (bf16[3,32,1280]{2,1,0:T(8,128)(2,1)}, bf16[3,32,1280]{2,1,0:T(8,128)(2,1)S(1)}, u32[]{:S(2)}, u32[]{:S(2)}) collective-permute-start(bf16[3,32,1280]{2,1,0:T(8,128)(2,1)} %get-tuple-element.80), channel_id=1, source_target_pairs={{320,0},{384,64},{448,128},{0,192},{64,256},{128,320},{192,384},{2... | collective-permute-start | bytes 737288 | tf_op jit(solution)/shard_map/ppermute | solution.py:294
  27.8 2.8 collective-permute-start.3
  30.6 6.4 %collective-permute-start.4 = (bf16[3,32,1280]{2,1,0:T(8,128)(2,1)}, bf16[3,32,1280]{2,1,0:T(8,128)(2,1)}, u32[]{:S(2)}, u32[]{:S(2)}) collective-permute-start(bf16[3,32,1280]{2,1,0:T(8,128)(2,1)} %get-tuple-element.78), channel_id=1, source_target_pairs={{192,0},{256,64},{320,128},{384,192},{448,256},{0,320},{64,384},{1... | collective-permute-start | bytes 737288 | tf_op jit(solution)/shard_map/ppermute | solution.py:294
  37.0 3.4 collective-permute-start.5
  40.4 2.2 collective-permute-start.6
  42.7 15.9 %collective-permute-done.2 = bf16[3,32,1280]{2,1,0:T(8,128)(2,1)S(1)} collective-permute-done((bf16[3,32,1280]{2,1,0:T(8,128)(2,1)}, bf16[3,32,1280]{2,1,0:T(8,128)(2,1)S(1)}, u32[]{:S(2)}, u32[]{:S(2)}) %collective-permute-start.2) | collective-permute-done | bytes 245792 | tf_op jit(solution)/shard_map/ppermute | solution.py:294
  58.6 13.2 %collective-permute-done.5 = bf16[3,32,1280]{2,1,0:T(8,128)(2,1)} collective-permute-done((bf16[3,32,1280]{2,1,0:T(8,128)(2,1)}, bf16[3,32,1280]{2,1,0:T(8,128)(2,1)}, u32[]{:S(2)}, u32[]{:S(2)}) %collective-permute-start.5) | collective-permute-done | bytes 245792 | tf_op jit(solution)/shard_map/ppermute | solution.py:294
  71.8 1.8 collective-permute-done.6
  80.3 1.1 pad_maximum_fusion.3
  84.7 1.1 maximum_maximum_fusion
  85.8 7.4 %all-to-all-start = ((bf16[8,64,768]{2,1,0:T(8,128)(2,1)}), bf16[8,64,768]{2,1,0:T(8,128)(2,1)S(1)}, u32[]{:S(2)}, u32[]{:S(2)}) async-start(bf16[8,64,768]{2,1,0:T(8,128)(2,1)} %maximum_maximum_fusion), calls=%async_computation | async-start | bytes 1572864 | tf_op jit(solution)/shard_map/all_to_all | solution.py:321
  93.7 30.6 %all-to-all-done = bf16[8,64,768]{2,1,0:T(8,128)(2,1)S(1)} async-done(((bf16[8,64,768]{2,1,0:T(8,128)(2,1)}), bf16[8,64,768]{2,1,0:T(8,128)(2,1)S(1)}, u32[]{:S(2)}, u32[]{:S(2)}) %all-to-all-start) | async-done | bytes 786464 | tf_op jit(solution)/shard_map/all_to_all | solution.py:321
  124.3 1.8 broadcast_in_dim.45
  126.1 10.0 %all-to-all-start.2 = ((bf16[32,8,8,640]{3,2,1,0:T(8,128)(2,1)}), bf16[32,8,8,640]{3,2,1,0:T(8,128)(2,1)S(1)}, u32[]{:S(2)}, u32[]{:S(2)}) async-start(bf16[32,8,8,640]{3,2,1,0:T(8,128)(2,1)} %bitcast.243), calls=%async_computation.2 | async-start | bytes 5242880 | tf_op jit(solution)/shard_map/all_to_all | solution.py:287
  136.2 2.3 pad_maximum_fusion.2
  138.5 3.9 collective-permute-start.7
  144.0 50.8 %all-to-all-done.2.u_ref = bf16[32,8,8,640]{3,2,1,0:T(8,128)(2,1)S(1)} async-done(((bf16[32,8,8,640]{3,2,1,0:T(8,128)(2,1)}), bf16[32,8,8,640]{3,2,1,0:T(8,128)(2,1)S(1)}, u32[]{:S(2)}, u32[]{:S(2)}) %all-to-all-start.2) | async-done | bytes 2621472 | tf_op jit(solution)/shard_map/all_to_all | solution.py:287
  195.6 7.1 %all-to-all-start.1 = ((bf16[32,8,640]{2,1,0:T(8,128)(2,1)}), bf16[32,8,640]{2,1,0:T(8,128)(2,1)S(1)}, u32[]{:S(2)}, u32[]{:S(2)}) async-start(bf16[32,8,640]{2,1,0:T(8,128)(2,1)} %bitcast.4), calls=%async_computation.1 | async-start | bytes 655360 | tf_op jit(solution)/shard_map/all_to_all | solution.py:341
  202.7 1.9 select_bitcast_fusion.1
  204.6 1.7 pad_maximum_fusion.w_ref
  206.3 5.4 factors.1
  211.7 1.9 all-to-all-done.1
  213.6 15.8 %all_to_all.95.fac_ref = bf16[8,64,512]{2,1,0:T(8,128)(2,1)S(1)} all-to-all(bf16[8,64,512]{2,1,0:T(8,128)(2,1)} %get-tuple-element.38), channel_id=1, replica_groups=mesh['pipe'=8,'expert'=32,'dp'=2] {'pipe'}, dimensions={0} | all-to-all | bytes 1048576 | tf_op jit(solution)/shard_map/all_to_all | solution.py:337
  230.2 3.8 expert.8
  234.0 9.4 %all-to-all-start.4 = ((bf16[32,8,640]{2,1,0:T(8,128)(2,1)}), bf16[32,8,640]{2,1,0:T(8,128)(2,1)S(1)}, u32[]{:S(2)}, u32[]{:S(2)}) async-start(bf16[32,8,640]{2,1,0:T(8,128)(2,1)} %bitcast.30), calls=%async_computation.4 | async-start | bytes 655360 | tf_op jit(solution)/shard_map/all_to_all | solution.py:341
  244.1 10.0 %all-to-all-done.4 = bf16[32,8,640]{2,1,0:T(8,128)(2,1)S(1)} async-done(((bf16[32,8,640]{2,1,0:T(8,128)(2,1)}), bf16[32,8,640]{2,1,0:T(8,128)(2,1)S(1)}, u32[]{:S(2)}, u32[]{:S(2)}) %all-to-all-start.4) | async-done | bytes 327712 | tf_op jit(solution)/shard_map/all_to_all | solution.py:341
  254.1 2.4 home.7
  256.5 14.5 %all_to_all.96 = bf16[32,8,640]{2,1,0:T(8,128)(2,1)S(1)} all-to-all(bf16[32,8,640]{2,1,0:T(8,128)(2,1)S(1)} %get-tuple-element.40), channel_id=1, replica_groups=mesh['pipe'=8,'expert'=32,'dp'=2] {'expert'}, dimensions={0} | all-to-all | bytes 655360 | tf_op jit(solution)/shard_map/all_to_all | solution.py:341
  271.0 2.4 expert.9
  273.4 4.1 all-to-all-start.6
  277.6 10.7 %all-to-all-done.6 = bf16[32,8,640]{2,1,0:T(8,128)(2,1)S(1)} async-done(((bf16[32,8,640]{2,1,0:T(8,128)(2,1)}), bf16[32,8,640]{2,1,0:T(8,128)(2,1)S(1)}, u32[]{:S(2)}, u32[]{:S(2)}) %all-to-all-start.6) | async-done | bytes 327712 | tf_op jit(solution)/shard_map/all_to_all | solution.py:341
  288.2 2.3 home.8
  290.5 14.5 %all_to_all.97 = bf16[32,8,640]{2,1,0:T(8,128)(2,1)S(1)} all-to-all(bf16[32,8,640]{2,1,0:T(8,128)(2,1)S(1)} %get-tuple-element.45), channel_id=1, replica_groups=mesh['pipe'=8,'expert'=32,'dp'=2] {'expert'}, dimensions={0} | all-to-all | bytes 655360 | tf_op jit(solution)/shard_map/all_to_all | solution.py:341
  305.1 2.1 expert.10
  307.2 14.7 %all_to_all.98 = bf16[32,8,640]{2,1,0:T(8,128)(2,1)S(1)} all-to-all(bf16[32,8,640]{2,1,0:T(8,128)(2,1)S(1)} %bitcast.230), channel_id=1, replica_groups=mesh['pipe'=8,'expert'=32,'dp'=2] {'expert'}, dimensions={0} | all-to-all | bytes 655360 | tf_op jit(solution)/shard_map/all_to_all | solution.py:341
  321.9 2.2 home.9
  324.1 14.7 %all_to_all.99 = bf16[32,8,640]{2,1,0:T(8,128)(2,1)S(1)} all-to-all(bf16[32,8,640]{2,1,0:T(8,128)(2,1)S(1)} %get-tuple-element.50), channel_id=1, replica_groups=mesh['pipe'=8,'expert'=32,'dp'=2] {'expert'}, dimensions={0} | all-to-all | bytes 655360 | tf_op jit(solution)/shard_map/all_to_all | solution.py:341
  338.8 2.1 expert.11
  340.9 15.3 %all_to_all.100 = bf16[32,8,640]{2,1,0:T(8,128)(2,1)S(1)} all-to-all(bf16[32,8,640]{2,1,0:T(8,128)(2,1)S(1)} %bitcast.231), channel_id=1, replica_groups=mesh['pipe'=8,'expert'=32,'dp'=2] {'expert'}, dimensions={0} | all-to-all | bytes 655360 | tf_op jit(solution)/shard_map/all_to_all | solution.py:341
  356.2 2.1 home.10
  358.4 17.1 %all_to_all.101 = bf16[32,8,640]{2,1,0:T(8,128)(2,1)S(1)} all-to-all(bf16[32,8,640]{2,1,0:T(8,128)(2,1)S(1)} %get-tuple-element.55), channel_id=1, replica_groups=mesh['pipe'=8,'expert'=32,'dp'=2] {'expert'}, dimensions={0} | all-to-all | bytes 655360 | tf_op jit(solution)/shard_map/all_to_all | solution.py:341
  375.5 2.1 expert.12
  377.6 16.4 %all_to_all.102 = bf16[32,8,640]{2,1,0:T(8,128)(2,1)S(1)} all-to-all(bf16[32,8,640]{2,1,0:T(8,128)(2,1)S(1)} %bitcast.232), channel_id=1, replica_groups=mesh['pipe'=8,'expert'=32,'dp'=2] {'expert'}, dimensions={0} | all-to-all | bytes 655360 | tf_op jit(solution)/shard_map/all_to_all | solution.py:341
  394.0 2.1 home.11
  396.1 16.4 %all_to_all.103 = bf16[32,8,640]{2,1,0:T(8,128)(2,1)S(1)} all-to-all(bf16[32,8,640]{2,1,0:T(8,128)(2,1)S(1)} %get-tuple-element.60), channel_id=1, replica_groups=mesh['pipe'=8,'expert'=32,'dp'=2] {'expert'}, dimensions={0} | all-to-all | bytes 655360 | tf_op jit(solution)/shard_map/all_to_all | solution.py:341
  412.5 2.1 expert.13
  414.6 16.0 %all_to_all.104 = bf16[32,8,640]{2,1,0:T(8,128)(2,1)S(1)} all-to-all(bf16[32,8,640]{2,1,0:T(8,128)(2,1)S(1)} %bitcast.233), channel_id=1, replica_groups=mesh['pipe'=8,'expert'=32,'dp'=2] {'expert'}, dimensions={0} | all-to-all | bytes 655360 | tf_op jit(solution)/shard_map/all_to_all | solution.py:341
  430.6 2.1 home.12
  432.7 16.8 %all_to_all.105 = bf16[32,8,640]{2,1,0:T(8,128)(2,1)S(1)} all-to-all(bf16[32,8,640]{2,1,0:T(8,128)(2,1)S(1)} %get-tuple-element.65), channel_id=1, replica_groups=mesh['pipe'=8,'expert'=32,'dp'=2] {'expert'}, dimensions={0} | all-to-all | bytes 655360 | tf_op jit(solution)/shard_map/all_to_all | solution.py:341
  449.5 2.1 expert.14
  451.6 16.8 %all_to_all.106 = bf16[32,8,640]{2,1,0:T(8,128)(2,1)S(1)} all-to-all(bf16[32,8,640]{2,1,0:T(8,128)(2,1)S(1)} %bitcast.234), channel_id=1, replica_groups=mesh['pipe'=8,'expert'=32,'dp'=2] {'expert'}, dimensions={0} | all-to-all | bytes 655360 | tf_op jit(solution)/shard_map/all_to_all | solution.py:341
  468.3 2.0 home.13
  470.3 16.6 %all_to_all.107 = bf16[32,8,640]{2,1,0:T(8,128)(2,1)S(1)} all-to-all(bf16[32,8,640]{2,1,0:T(8,128)(2,1)S(1)} %get-tuple-element.70), channel_id=1, replica_groups=mesh['pipe'=8,'expert'=32,'dp'=2] {'expert'}, dimensions={0} | all-to-all | bytes 655360 | tf_op jit(solution)/shard_map/all_to_all | solution.py:341
  487.0 1.1 expert.15
  488.1 3.5 all-to-all-start.18
  491.6 12.3 %all-to-all-done.18 = bf16[8,64,512]{2,1,0:T(8,128)(2,1)S(1)} async-done(((bf16[8,64,512]{2,1,0:T(8,128)(2,1)}), bf16[8,64,512]{2,1,0:T(8,128)(2,1)S(1)}, u32[]{:S(2)}, u32[]{:S(2)}) %all-to-all-start.18) | async-done | bytes 524320 | tf_op jit(solution)/shard_map/all_to_all | solution.py:361
  503.9 3.3 convolution_convert_fusion.1
  507.2 24.7 %collective-permute-start.8 = (bf16[512,1280]{1,0:T(8,128)(2,1)}, bf16[512,1280]{1,0:T(8,128)(2,1)S(1)}, u32[]{:S(2)}, u32[]{:S(2)}) collective-permute-start(bf16[512,1280]{1,0:T(8,128)(2,1)} %convolution_convert_fusion.1), channel_id=1, source_target_pairs={{0,1},{1,0},{2,3},{3,2},{4,5},{5,4},{6,7},{7,6},{8,9},{9,8},{10,11... | collective-permute-start | bytes 3932168 | tf_op jit(solution)/shard_map/ppermute | solution.py:371
  531.9 2.8 collective-permute-done.8
  534.8 2.3 add_convert_fusion
  537.0 1.1 slice_bitcast_fusion
  (80 shorter events, 15.2 us)
Async XLA Ops:
  7.2 76.4 %copy-start = (bf16[1,1,128,2560]{3,2,1,0:T(8,128)(2,1)S(1)}, bf16[1,1,128,2560]{3,2,1,0:T(8,128)(2,1)}, u32[]{:S(2)}) copy-start(bf16[1,1,128,2560]{3,2,1,0:T(8,128)(2,1)} %param.6) | copy-start | bytes 1966084
  7.2 222.2 %all-gather.7.cloned.1.call-start = ((), (), s32[]{:S(2)}) async-start(), calls=%async_computation.19 | async-start | bytes 8355840 | tf_op jit(solution)/shard_map/all_gather | solution.py:306
  10.1 26.9 %collective-permute-start = (bf16[3,32,1280]{2,1,0:T(8,128)(2,1)S(1)}, bf16[3,32,1280]{2,1,0:T(8,128)(2,1)S(1)}, u32[]{:S(2)}, u32[]{:S(2)}) collective-permute-start(bf16[3,32,1280]{2,1,0:T(8,128)(2,1)S(1)} %get-tuple-element.82), channel_id=1, source_target_pairs={{448,0},{0,64},{64,128},{128,192},{192,256},{256,320},{320,384},{3... | collective-permute-start | bytes 737288 | tf_op jit(solution)/shard_map/ppermute | solution.py:294
  14.9 25.5 %collective-permute-start.1 = (bf16[3,32,1280]{2,1,0:T(8,128)(2,1)S(1)}, bf16[3,32,1280]{2,1,0:T(8,128)(2,1)S(1)}, u32[]{:S(2)}, u32[]{:S(2)}) collective-permute-start(bf16[3,32,1280]{2,1,0:T(8,128)(2,1)S(1)} %get-tuple-element.81), channel_id=1, source_target_pairs={{384,0},{448,64},{0,128},{64,192},{128,256},{192,320},{256,384},{3... | collective-permute-start | bytes 737288 | tf_op jit(solution)/shard_map/ppermute | solution.py:294
  20.8 37.8 %collective-permute-start.2 = (bf16[3,32,1280]{2,1,0:T(8,128)(2,1)}, bf16[3,32,1280]{2,1,0:T(8,128)(2,1)S(1)}, u32[]{:S(2)}, u32[]{:S(2)}) collective-permute-start(bf16[3,32,1280]{2,1,0:T(8,128)(2,1)} %get-tuple-element.80), channel_id=1, source_target_pairs={{320,0},{384,64},{448,128},{0,192},{64,256},{128,320},{192,384},{2... | collective-permute-start | bytes 737288 | tf_op jit(solution)/shard_map/ppermute | solution.py:294
  27.8 30.8 %collective-permute-start.3 = (bf16[3,32,1280]{2,1,0:T(8,128)(2,1)}, bf16[3,32,1280]{2,1,0:T(8,128)(2,1)}, u32[]{:S(2)}, u32[]{:S(2)}) collective-permute-start(bf16[3,32,1280]{2,1,0:T(8,128)(2,1)} %get-tuple-element.79), channel_id=1, source_target_pairs={{256,0},{320,64},{384,128},{448,192},{0,256},{64,320},{128,384},{1... | collective-permute-start | bytes 737288 | tf_op jit(solution)/shard_map/ppermute | solution.py:294
  30.6 28.0 %collective-permute-start.4 = (bf16[3,32,1280]{2,1,0:T(8,128)(2,1)}, bf16[3,32,1280]{2,1,0:T(8,128)(2,1)}, u32[]{:S(2)}, u32[]{:S(2)}) collective-permute-start(bf16[3,32,1280]{2,1,0:T(8,128)(2,1)} %get-tuple-element.78), channel_id=1, source_target_pairs={{192,0},{256,64},{320,128},{384,192},{448,256},{0,320},{64,384},{1... | collective-permute-start | bytes 737288 | tf_op jit(solution)/shard_map/ppermute | solution.py:294
  37.0 34.8 %collective-permute-start.5 = (bf16[3,32,1280]{2,1,0:T(8,128)(2,1)}, bf16[3,32,1280]{2,1,0:T(8,128)(2,1)}, u32[]{:S(2)}, u32[]{:S(2)}) collective-permute-start(bf16[3,32,1280]{2,1,0:T(8,128)(2,1)} %get-tuple-element.77), channel_id=1, source_target_pairs={{128,0},{192,64},{256,128},{320,192},{384,256},{448,320},{0,384},{... | collective-permute-start | bytes 737288 | tf_op jit(solution)/shard_map/ppermute | solution.py:294
  40.4 33.2 %collective-permute-start.6 = (bf16[3,32,1280]{2,1,0:T(8,128)(2,1)}, bf16[3,32,1280]{2,1,0:T(8,128)(2,1)}, u32[]{:S(2)}, u32[]{:S(2)}) collective-permute-start(bf16[3,32,1280]{2,1,0:T(8,128)(2,1)} %get-tuple-element.76), channel_id=1, source_target_pairs={{64,0},{128,64},{192,128},{256,192},{320,256},{384,320},{448,384},... | collective-permute-start | bytes 737288 | tf_op jit(solution)/shard_map/ppermute | solution.py:294
  74.7 202.9 %all-gather.9.cloned.1.call-start = ((), (), s32[]{:S(2)}) async-start(), calls=%async_computation.20 | async-start | bytes 8355840 | tf_op jit(solution)/shard_map/all_gather | solution.py:306
  76.8 279.4 %all-gather.11.cloned.1.call-start = ((), (), s32[]{:S(2)}) async-start(), calls=%async_computation.21 | async-start | bytes 16711680 | tf_op jit(solution)/shard_map/all_gather | solution.py:306
  80.3 1.2 copy-start.6
  80.3 1.9 copy-start.7
  85.8 38.5 %all-to-all-start = ((bf16[8,64,768]{2,1,0:T(8,128)(2,1)}), bf16[8,64,768]{2,1,0:T(8,128)(2,1)S(1)}, u32[]{:S(2)}, u32[]{:S(2)}) async-start(bf16[8,64,768]{2,1,0:T(8,128)(2,1)} %maximum_maximum_fusion), calls=%async_computation | async-start | bytes 1572864 | tf_op jit(solution)/shard_map/all_to_all | solution.py:321
  124.3 1.8 copy-start.4
  126.1 10.1 %copy-start.3 = (bf16[1,1,256,1280]{3,2,1,0:T(8,128)(2,1)S(1)}, bf16[1,1,256,1280]{3,2,1,0:T(8,128)(2,1)}, u32[]{:S(2)}) copy-start(bf16[1,1,256,1280]{3,2,1,0:T(8,128)(2,1)} %param.10) | copy-start | bytes 1966084
  126.1 68.7 %all-to-all-start.2 = ((bf16[32,8,8,640]{3,2,1,0:T(8,128)(2,1)}), bf16[32,8,8,640]{3,2,1,0:T(8,128)(2,1)S(1)}, u32[]{:S(2)}, u32[]{:S(2)}) async-start(bf16[32,8,8,640]{3,2,1,0:T(8,128)(2,1)} %bitcast.243), calls=%async_computation.2 | async-start | bytes 5242880 | tf_op jit(solution)/shard_map/all_to_all | solution.py:287
  136.2 7.5 %slice-start = ((bf16[8,64,768]{2,1,0:T(8,128)(2,1)}), bf16[8,64,16]{2,1,0:T(8,128)(2,1)S(1)}, s32[]{:S(2)}) async-start(bf16[8,64,768]{2,1,0:T(8,128)(2,1)} %copy-done.4), calls=%async_computation.22 | async-start | bytes 262144 | tf_op jit(solution)/shard_map/slice | solution.py:323
  138.5 64.2 %collective-permute-start.7 = (bf16[2,256,1280]{2,1,0:T(8,128)(2,1)}, bf16[2,256,1280]{2,1,0:T(8,128)(2,1)}, u32[]{:S(2)}, u32[]{:S(2)}) collective-permute-start(bf16[2,256,1280]{2,1,0:T(8,128)(2,1)} %pad_maximum_fusion.2), channel_id=1, source_target_pairs={{0,1},{1,0},{2,3},{3,2},{4,5},{5,4},{6,7},{7,6},{8,9},{9,8},{10,11... | collective-permute-start | bytes 3932168 | tf_op jit(solution)/shard_map/ppermute | solution.py:333
  194.8 9.8 %copy-start.2 = (bf16[32,8,8,640]{3,2,1,0:T(8,128)(2,1)}, bf16[32,8,8,640]{3,2,1,0:T(8,128)(2,1)S(1)}, u32[]{:S(2)}) copy-start(bf16[32,8,8,640]{3,2,1,0:T(8,128)(2,1)S(1)} %all-to-all-done.2.u_ref) | copy-start | bytes 7864324
  195.6 18.0 %all-to-all-start.1 = ((bf16[32,8,640]{2,1,0:T(8,128)(2,1)}), bf16[32,8,640]{2,1,0:T(8,128)(2,1)S(1)}, u32[]{:S(2)}, u32[]{:S(2)}) async-start(bf16[32,8,640]{2,1,0:T(8,128)(2,1)} %bitcast.4), calls=%async_computation.1 | async-start | bytes 655360 | tf_op jit(solution)/shard_map/all_to_all | solution.py:341
  230.2 13.3 %copy-start.5 = (bf16[8,64,768]{2,1,0:T(8,128)(2,1)S(1)}, bf16[8,64,768]{2,1,0:T(8,128)(2,1)}, u32[]{:S(2)}) copy-start(bf16[8,64,768]{2,1,0:T(8,128)(2,1)} %copy-done.4) | copy-start | bytes 2359300
  234.0 20.1 %all-to-all-start.4 = ((bf16[32,8,640]{2,1,0:T(8,128)(2,1)}), bf16[32,8,640]{2,1,0:T(8,128)(2,1)S(1)}, u32[]{:S(2)}, u32[]{:S(2)}) async-start(bf16[32,8,640]{2,1,0:T(8,128)(2,1)} %bitcast.30), calls=%async_computation.4 | async-start | bytes 655360 | tf_op jit(solution)/shard_map/all_to_all | solution.py:341
  273.4 14.8 %all-to-all-start.6 = ((bf16[32,8,640]{2,1,0:T(8,128)(2,1)}), bf16[32,8,640]{2,1,0:T(8,128)(2,1)S(1)}, u32[]{:S(2)}, u32[]{:S(2)}) async-start(bf16[32,8,640]{2,1,0:T(8,128)(2,1)} %bitcast.33), calls=%async_computation.6 | async-start | bytes 655360 | tf_op jit(solution)/shard_map/all_to_all | solution.py:341
  488.1 15.8 %all-to-all-start.18 = ((bf16[8,64,512]{2,1,0:T(8,128)(2,1)}), bf16[8,64,512]{2,1,0:T(8,128)(2,1)S(1)}, u32[]{:S(2)}, u32[]{:S(2)}) async-start(bf16[8,64,512]{2,1,0:T(8,128)(2,1)} %expert.15), calls=%async_computation.18 | async-start | bytes 1048576 | tf_op jit(solution)/shard_map/all_to_all | solution.py:361
  507.2 27.6 %collective-permute-start.8 = (bf16[512,1280]{1,0:T(8,128)(2,1)}, bf16[512,1280]{1,0:T(8,128)(2,1)S(1)}, u32[]{:S(2)}, u32[]{:S(2)}) collective-permute-start(bf16[512,1280]{1,0:T(8,128)(2,1)} %convolution_convert_fusion.1), channel_id=1, source_target_pairs={{0,1},{1,0},{2,3},{3,2},{4,5},{5,4},{6,7},{7,6},{8,9},{9,8},{10,11... | collective-permute-start | bytes 3932168 | tf_op jit(solution)/shard_map/ppermute | solution.py:371
  534.8 3.4 copy-start.1
Sparse Core Ops, SparseCore 0:
  74.8 77.8 all-gather.6
  154.8 54.8 all-gather.8
  211.8 96.5 all-gather.10
